TPU v7x, 128 devices: a whole 4x4x4 slice. The times are simulated.
128 devices in a mesh: ka: 16 (over z, y), row: 8 (over x, core).
Axes of the slice: x: 4, y: 4, z: 4, core: 2. Of those that a mesh axis runs over, the one named last changes fastest.
Arguments:
- packet: float32 [32, 384, 128, 128], P('ka', None, 'row'), may hold values from -6 to 6
- previous: float32 [32, 384, 128, 128], P('ka', None, 'row'), may hold values from -6 to 6
- basis_sizes: int32 [32], P('ka'), may hold values from 96 to 384, as said below
- centrifugal: float32 [32, 384], P('ka'), may hold values from 0.1 to 2
- coriolis: float32 [32, 384], replicated, may hold values from -3 to 3
- inertia: float32 [128, 128], replicated, may hold values from 0.25 to 4
- damping: float32 [128], P('row'), may hold values from 0.6 to 1
- radial_kin: float32 [128, 128], replicated, may hold values from -0.5 to 0.5
- stretch_kin: float32 [128, 128], replicated, may hold values from -0.5 to 0.5
- legendre: float32 [32, 512, 384], P('ka'), may hold values from -0.3125 to 0.3125
- potential: float32 [512, 128, 128], P(None, 'row'), may hold values from -1 to 1
Outputs:
- advanced: float32 [32, 384, 128, 128], P('ka', None, 'row')
Inputs may be any that keep to these rules, and one draw needn't show every extreme that they name: `basis_sizes`: one helicity block has exactly 384 live basis functions and another exactly 96.
All inputs are finite; a program needn't handle non-finite values.
Results may differ from a plain program's by a relative error of at most 0.0003.
Values sent between devices are 32-bit elements; how exact they have to be, the bound alone decides.
No kernel may reach another device: no remote copies, remote signals or barrier semaphores. Data moves between devices by JAX's collectives and lax.ppermute only.
A program may use at most 192 MiB of HBM per device.

v0:
```python
import functools

import jax
import jax.numpy as jnp
from jax import lax
from jax.experimental import pallas as pl
from jax.experimental.pallas import tpu as pltpu
from jax.sharding import PartitionSpec as P

F32 = jnp.float32
BF16 = jnp.bfloat16
MIB = 1 << 20


def from_behind(x, axis, by):
    peers = lax.axis_size(axis)
    pairs = [(i, i + by) for i in range(peers) if 0 <= i + by < peers]
    return lax.ppermute(x, axis, pairs)


def exchange(x):
    return lax.all_to_all(x, "row", split_axis=0, concat_axis=0, tiled=True)


def halves(x):
    high = x.astype(BF16)
    return high, (x - high.astype(F32)).astype(BF16)


def halves_outside(x):
    high = lax.reduce_precision(x, 8, 7)
    return high.astype(BF16), (x - high).astype(BF16)


def local_kernel(
    sizes, centrifugal, x_ref, previous_ref, potential_ref, legendre_ref, stretch_ref,
    inertia_ref, factor_ref, out_ref, acc, ahead, back,
):
    block = pl.program_id(0)
    live = sizes[block]
    angles, basis = legendre_ref.shape[1:]
    radial = inertia_ref.shape[0]
    rows = basis * radial
    high, low = halves(legendre_ref[0])
    ahead[:, :basis] = high
    ahead[:, basis : 2 * basis] = high
    ahead[:, 2 * basis :] = low
    high, low = halves(legendre_ref[0].T)
    back[:, :angles] = high
    back[:, angles : 2 * angles] = high
    back[:, 2 * angles :] = low

    piece = rows // 8

    @pl.loop(0, 8)
    def _(i):
        at = pl.ds(pl.multiple_of(i * piece, piece), piece)
        high, low = halves(x_ref[0, at, :])
        both = jnp.dot(
            jnp.concatenate([high, low], 1), stretch_ref[...], preferred_element_type=F32
        )
        acc[at, :] = both[:, :128] + both[:, 128:]

    mask = lax.broadcasted_iota(jnp.int32, (basis, 256), 0) < live

    @pl.loop(0, radial // 2)
    def _(i):
        r = 2 * i
        here = [pl.ds(r + k, basis, stride=radial) for k in range(2)]
        there = [pl.ds(r + k, angles, stride=radial) for k in range(2)]
        m = jnp.concatenate([x_ref[0, at, :] for at in here], 1)
        m = jnp.where(mask, m, 0.0)
        high, low = halves(m)
        grid = jnp.dot(
            ahead[...], jnp.concatenate([high, low, high], 0), preferred_element_type=F32
        )
        grid = grid * jnp.concatenate([potential_ref[at, :] for at in there], 1)
        high, low = halves(grid)
        term = jnp.dot(
            back[...], jnp.concatenate([high, low, high], 0), preferred_element_type=F32
        )
        for k in range(2):
            acc[here[k], :] += term[:, 128 * k : 128 * (k + 1)]

    inertia = inertia_ref[...]
    factor = factor_ref[...]

    @pl.loop(0, basis // 8)
    def _(i):
        for k in range(8):
            j = i * 8 + k
            at = pl.ds(pl.multiple_of(j * radial, radial), radial)
            value = acc[at, :] + (centrifugal[block, j] * inertia) * x_ref[0, at, :]
            value = factor * (2.0 * value - factor * previous_ref[0, at, :])
            out_ref[0, at, :] = jnp.where(j < live, value, 0.0)


def local_terms(sizes, centrifugal, x, previous, potential, legendre, stretch, inertia, factor):
    blocks, angles, basis = legendre.shape
    rows = x.shape[1]
    whole = pl.BlockSpec((1, rows, 128), lambda k: (k, 0, 0))
    smem = pl.BlockSpec(memory_space=pltpu.SMEM)
    once = lambda shape: pl.BlockSpec(shape, lambda k: (0,) * len(shape))
    return pl.pallas_call(
        local_kernel,
        grid=(blocks,),
        in_specs=[
            smem, smem, whole, whole, once(potential.shape),
            pl.BlockSpec((1, angles, basis), lambda k: (k, 0, 0)),
            once(stretch.shape), once(inertia.shape), once(factor.shape),
        ],
        out_specs=whole,
        out_shape=jax.ShapeDtypeStruct(x.shape, F32),
        scratch_shapes=[
            pltpu.VMEM((rows, 128), F32),
            pltpu.VMEM((angles, 3 * basis), BF16),
            pltpu.VMEM((basis, 3 * angles), BF16),
        ],
        compiler_params=pltpu.CompilerParams(vmem_limit_bytes=52 * MIB),
        cost_estimate=pl.CostEstimate(
            flops=12_000_000_000, bytes_accessed=27_000_000, transcendentals=0
        ),
        name="local_terms",
    )(sizes, centrifugal, x, previous, potential, legendre, stretch, inertia, factor)


def radial_kernel(matrix_ref, x_ref, out_ref):
    peers, columns, rows, width = x_ref.shape
    for c in range(0, columns, 2):
        m = jnp.concatenate(
            [x_ref[:, c + k].reshape(peers * rows, width) for k in range(2)], 1
        )
        high, low = halves(m)
        both = jnp.dot(
            matrix_ref[...], jnp.concatenate([high, low], 0), preferred_element_type=F32
        )
        total = both[:128] + both[128:]
        for k in range(2):
            out_ref[:, c + k] = total[:, 128 * k : 128 * (k + 1)].reshape(peers, rows, width)


def radial_apply(matrix, received):
    peers, columns, rows, width = received.shape
    some = pl.BlockSpec((peers, 8, rows, width), lambda i: (0, i, 0, 0))
    return pl.pallas_call(
        radial_kernel,
        grid=(columns // 8,),
        in_specs=[pl.BlockSpec(matrix.shape, lambda i: (0, 0)), some],
        out_specs=some,
        out_shape=jax.ShapeDtypeStruct(received.shape, F32),
        cost_estimate=pl.CostEstimate(
            flops=columns * 20_000_000, bytes_accessed=2 * 4 * received.size, transcendentals=0
        ),
        name="radial_apply",
    )(matrix, received)


def middle_kernel(
    sizes, coriolis, out_in, x_ref, lower_ref, upper_ref, first_ref, inertia_ref, factor_ref, out_ref
):
    step = pl.program_id(0)
    radial = inertia_ref.shape[0]
    count = x_ref.shape[1] // radial
    inertia = inertia_ref[...]
    double = 2.0 * factor_ref[...]
    both = double * inertia
    below, above = sizes[0], sizes[1]

    @pl.loop(0, count // 4)
    def _(i):
        for k in range(4):
            local = i * 4 + k
            j = step * count + local
            at = pl.ds(pl.multiple_of(local * radial, radial), radial)
            here = jnp.where(j < below, x_ref[0, at, :], 0.0)
            there = jnp.where(j < above, x_ref[1, at, :], 0.0)
            low = coriolis[1, j] * there + coriolis[0, j] * lower_ref[at, :]
            high = coriolis[2, j] * upper_ref[at, :] + coriolis[1, j] * here
            out_ref[0, at, :] = out_in[0, at, :] + jnp.where(j < below, both * low, 0.0)
            out_ref[1, at, :] = out_in[1, at, :] + jnp.where(j < above, both * high, 0.0)

    @pl.when(step == 0)
    def _():
        @pl.loop(0, count // 4)
        def _(i):
            for k in range(4):
                j = i * 4 + k
                at = pl.ds(pl.multiple_of(j * radial, radial), radial)
                for b in range(2):
                    out_ref[b, at, :] += jnp.where(j < sizes[b], double * first_ref[b, at, :], 0.0)


def middle_terms(sizes, coriolis, out, x, lower, upper, first, inertia, factor):
    blocks, rows, width = x.shape
    parts = 4
    smem = pl.BlockSpec(memory_space=pltpu.SMEM)
    pair = pl.BlockSpec((blocks, rows // parts, width), lambda i: (0, i, 0))
    one = pl.BlockSpec((rows // parts, width), lambda i: (i, 0))
    small = pl.BlockSpec(inertia.shape, lambda i: (0, 0))
    return pl.pallas_call(
        middle_kernel,
        grid=(parts,),
        in_specs=[
            smem, smem, pair, pair, one, one,
            pl.BlockSpec(first.shape, lambda i: (0, 0, 0)), small, small,
        ],
        out_specs=pair,
        out_shape=jax.ShapeDtypeStruct(out.shape, F32),
        input_output_aliases={2: 0},
        compiler_params=pltpu.CompilerParams(vmem_limit_bytes=40 * MIB),
        cost_estimate=pl.CostEstimate(flops=30_000_000, bytes_accessed=27_000_000, transcendentals=0),
        name="middle_terms",
    )(sizes, coriolis, out, x, lower, upper, first, inertia, factor)


def add_second_kernel(sizes, out_in, back_ref, factor_ref, out_ref):
    radial = factor_ref.shape[0]
    basis = out_in.shape[0] // (2 * radial)
    first = basis // 4
    kept = back_ref.shape[0] // radial
    double = 2.0 * factor_ref[...]
    below, above = sizes[0], sizes[1]
    taken = below - first
    out_ref[...] = out_in[...]

    def add(target, source):
        at = pl.ds(pl.multiple_of(target * radial, radial), radial)
        of = pl.ds(pl.multiple_of(source * radial, radial), radial)
        out_ref[at, :] += double * back_ref[of, :]

    @pl.loop(0, taken)
    def _(i):
        add(first + i, i)

    @pl.loop(0, jnp.minimum(above - first, kept - taken))
    def _(i):
        add(basis + first + i, taken + i)


def add_second(sizes, out, back, factor):
    smem = pl.BlockSpec(memory_space=pltpu.SMEM)
    full = lambda a: pl.BlockSpec(a.shape, lambda: (0, 0))
    return pl.pallas_call(
        add_second_kernel,
        in_specs=[smem, full(out), full(back), full(factor)],
        out_specs=full(out),
        out_shape=jax.ShapeDtypeStruct(out.shape, F32),
        input_output_aliases={1: 0},
        compiler_params=pltpu.CompilerParams(vmem_limit_bytes=40 * MIB),
        cost_estimate=pl.CostEstimate(flops=3_000_000, bytes_accessed=15_000_000, transcendentals=0),
        name="add_second",
    )(sizes, out, back, factor)


def add_tail_kernel(sizes, skipped, out_in, back_ref, factor_ref, out_ref):
    radial = factor_ref.shape[0]
    double = 2.0 * factor_ref[...]
    out_ref[...] = out_in[...]

    @pl.loop(0, skipped[1])
    def _(i):
        at = pl.ds(pl.multiple_of((skipped[0] + i) * radial, radial), radial)
        of = pl.ds(pl.multiple_of(i * radial, radial), radial)
        out_ref[at, :] += double * back_ref[of, :]


def add_tail(sizes, skipped, out, back, factor):
    smem = pl.BlockSpec(memory_space=pltpu.SMEM)
    last = pl.BlockSpec(back.shape, lambda i: (out.shape[0] // back.shape[0] - 1, 0))
    full = lambda a: pl.BlockSpec(a.shape, lambda i: (0, 0))
    return pl.pallas_call(
        add_tail_kernel,
        grid=(1,),
        in_specs=[smem, smem, last, full(back), full(factor)],
        out_specs=last,
        out_shape=jax.ShapeDtypeStruct(out.shape, F32),
        input_output_aliases={2: 0},
        compiler_params=pltpu.CompilerParams(vmem_limit_bytes=30 * MIB),
        cost_estimate=pl.CostEstimate(flops=1_000_000, bytes_accessed=6_300_000, transcendentals=0),
        name="add_tail",
    )(sizes, skipped, out, back, factor)


def shards(
    packet, previous, basis_sizes, centrifugal, coriolis, inertia, damping,
    radial_kin, stretch_kin, legendre, potential,
):
    blocks, basis, radial, width = packet.shape
    peers = lax.axis_size("row")
    ka = lax.axis_index("ka")
    row = lax.axis_index("row")
    columns = blocks * basis
    first = basis // 4
    kept = 5 * columns // 12
    tail = columns - 2 * first - kept
    unit = tail // 4

    flat = packet.reshape(columns, radial, width)
    chunk_a = jnp.concatenate([flat[:first], flat[basis : basis + first]], 0)
    got_a = exchange(chunk_a)
    rest = jnp.concatenate([flat[first:basis], flat[basis + first :]], 0)
    rest = lax.dynamic_update_slice(rest, flat[basis + first :], (basis_sizes[0] - first, 0, 0))
    got_b = exchange(rest[:kept])

    live_mask = (lax.broadcasted_iota(jnp.int32, (blocks, basis), 1) < basis_sizes[:, None]).astype(F32)
    masked = packet * live_mask[:, :, None, None]
    upper = from_behind(masked[:1], "ka", -1).reshape(basis * radial, width)
    lower = from_behind(masked[1:], "ka", 1).reshape(basis * radial, width)

    inertia_local = lax.dynamic_slice_in_dim(inertia, row * radial, radial, 0)
    factor = jnp.broadcast_to(damping[:, None], (radial, width))
    t_high, t_low = halves_outside(radial_kin)
    t_high, t_low = [jnp.concatenate([t, t], 1) for t in (t_high, t_low)]
    matrix = jnp.concatenate([t_high, t_low], 0)
    s_high, s_low = halves_outside(stretch_kin.T)
    stretch = jnp.concatenate([jnp.concatenate([s_high, s_low], 1)] * 2, 0)
    start = jnp.maximum(ka * blocks - 1, 0)
    coupling = jnp.concatenate(
        [lax.dynamic_slice_in_dim(coriolis, start, 1, 0),
         lax.dynamic_slice_in_dim(coriolis, ka * blocks, blocks, 0)], 0
    )

    rows = basis * radial
    out = local_terms(
        basis_sizes, centrifugal, packet.reshape(blocks, rows, width),
        previous.reshape(blocks, rows, width),
        potential.reshape(potential.shape[0] * radial, width),
        legendre, stretch, inertia_local, factor,
    )

    def apply(got):
        shape = got.shape
        made = radial_apply(matrix, got.reshape(peers, shape[0] // peers, radial, width))
        return made.reshape(shape)

    back_a = exchange(apply(got_a))
    back_b = exchange(apply(got_b))
    live = basis_sizes[0] + basis_sizes[1]
    over = jnp.maximum(live - 2 * first - kept, 0)

    def take(n):
        def run(rest):
            if n == 0:
                return jnp.zeros((tail, radial, width), F32)
            done = exchange(apply(exchange(rest[kept : kept + n * unit])))
            return jnp.pad(done, ((0, tail - n * unit), (0, 0), (0, 0)))
        return run

    back_t = lax.switch((over + unit - 1) // unit, [take(n) for n in range(5)], rest)

    out = middle_terms(
        basis_sizes, coupling, out, packet.reshape(blocks, rows, width), lower, upper,
        back_a.reshape(blocks, first * radial, width), inertia_local, factor,
    )
    out = add_second(
        basis_sizes, out.reshape(columns * radial, width), back_b.reshape(kept * radial, width), factor
    )
    begin = kept + 2 * first - basis_sizes[0] - (basis - tail)
    out = add_tail(
        basis_sizes, jnp.stack([begin, over]).astype(jnp.int32), out,
        back_t.reshape(tail * radial, width), factor,
    )
    return out.reshape(packet.shape)


def solution(mesh):
    in_specs = (
        P("ka", None, "row", None),
        P("ka", None, "row", None),
        P("ka"),
        P("ka", None),
        P(),
        P(),
        P("row"),
        P(),
        P(),
        P("ka", None, None),
        P(None, "row", None),
    )
    out_specs = P("ka", None, "row", None)
    return jax.shard_map(shards, mesh=mesh, in_specs=in_specs, out_specs=out_specs, check_vma=False)
```

profile of v0, /device:TPU:50, one launch (start us, length us, event | category | flops | bytes accessed | tf_op | source)
XLA Modules:
  0.0 259.3 jit_solution(8199962334785037379)
XLA Ops:
  0.0 0.0 copy-start
  0.0 2.7 %fusion.3 = (f32[96,16,128]{2,1,0:T(8,128)}, f32[96,16,128]{2,1,0:T(8,128)}) fusion(f32[768,16,128]{2,1,0:T(8,128)} %bitcast.32), kind=kLoop, calls=%fused_computation.19 | loop fusion | bytes 3145728 | tf_op jit(solution)/shard_map/slice | solution.py:299
  2.7 0.0 copy-start.4
  2.7 0.0 copy-start.11
  2.7 4.1 %fusion.2 = (f32[288,16,128]{2,1,0:T(8,128)S(1)}, f32[288,16,128]{2,1,0:T(8,128)}) fusion(f32[768,16,128]{2,1,0:T(8,128)} %bitcast.33), kind=kLoop, calls=%fused_computation.18 | loop fusion | bytes 9437184 | tf_op jit(solution)/shard_map/slice | solution.py:301
  6.8 0.0 copy-done.4
  6.8 0.6 fusion.5
  8.8 0.0 copy-done.11
  10.2 0.0 copy-start.8
  10.2 2.8 %pad_maximum_fusion.1 = f32[192,16,128]{2,1,0:T(8,128)} fusion(f32[96,16,128]{2,1,0:T(8,128)} %get-tuple-element.39, f32[96,16,128]{2,1,0:T(8,128)} %get-tuple-element.38), kind=kLoop, calls=%fused_computation.2 | loop fusion | flops 393216 | bytes 3145728 | tf_op jit(solution)/shard_map/concatenate | solution.py:299
  13.0 0.0 copy-done.8
  13.0 2.5 pad_maximum_fusion
  15.5 3.2 %constant_dynamic-update-slice_fusion = f32[576,16,128]{2,1,0:T(8,128)} fusion(f32[576,16,128]{2,1,0:T(8,128)} %pad_maximum_fusion, s32[]{:T(128)S(6)} %select_n.17, f32[768,16,128]{2,1,0:T(8,128)} %bitcast.34), kind=kLoop, calls=%fused_computation.13 | loop fusion | bytes 4718596 | tf_op jit(solution)/shard_map/dynamic_update_slice | solution.py:302
  18.7 67.8 %conditional.1 = (f32[4096,128]{1,0:T(8,128)S(1)}) conditional(s32[]{:T(128)} %clamp.3, () %tuple.25, (f32[576,16,128]{2,1,0:T(8,128)}, bf16[256,256]{1,0:T(8,128)(2,1)S(1)}) %tuple.26, (f32[576,16,128]{2,1,0:T(8,128)}, bf16[256,256]{1,0:T(8,128)(2,1)S(1)}) %tuple.26, (f32[576,16,128]{2,1,0:T(8,128)}, ...), branch_computations={%region_0.1_spmd, %region_1.2_spmd, %region_2.3_spmd, %region_3.4_... | conditional | flops 640000000 | bytes 16777224 | solution.py:349
  18.7 1.7 slice.32
  20.4 30.8 %all_to_all.58 = f32[256,16,128]{2,1,0:T(8,128)} all-to-all(f32[256,16,128]{2,1,0:T(8,128)S(1)} %slice.32), channel_id=1, replica_groups=mesh['ka'=16,'row'=8] {'row'}, dimensions={0} | all-to-all | bytes 4194304 | tf_op jit(solution)/shard_map/cond/branch_4_fun/all_to_all | solution.py:22
  51.2 4.3 %radial_apply.9 = f32[8,32,16,128]{3,2,1,0:T(8,128)} custom-call(bf16[256,256]{1,0:T(8,128)(2,1)S(1)} %get-tuple-element.34.matrix_ref, f32[8,32,16,128]{3,2,1,0:T(8,128)} %bitcast.48), custom_call_target="tpu_custom_call" | custom-call | flops 640000000 | bytes 4194304 | tf_op jit(solution)/shard_map/cond/branch_4_fun/radial_apply/pallas_call | solution.py:145
  55.5 31.0 %all_to_all.59 = f32[256,16,128]{2,1,0:T(8,128)S(1)} all-to-all(f32[256,16,128]{2,1,0:T(8,128)} %bitcast.49), channel_id=1, replica_groups=mesh['ka'=16,'row'=8] {'row'}, dimensions={0} | all-to-all | bytes 4194304 | tf_op jit(solution)/shard_map/cond/branch_4_fun/all_to_all | solution.py:22
  86.5 0.0 copy-start.9
  86.5 5.6 %all-to-all-start.8 = ((f32[192,16,128]{2,1,0:T(8,128)}), f32[192,16,128]{2,1,0:T(8,128)}, u32[]{:S(2)}, u32[]{:S(2)}) async-start(f32[192,16,128]{2,1,0:T(8,128)} %pad_maximum_fusion.1), calls=%async_computation.8 | async-start | bytes 3145728 | tf_op jit(solution)/shard_map/all_to_all | solution.py:22
  92.2 3.4 %slice.57 = f32[320,16,128]{2,1,0:T(8,128)} slice(f32[576,16,128]{2,1,0:T(8,128)} %constant_dynamic-update-slice_fusion), slice={[0:320], [0:16], [0:128]} | slice | bytes 5242880 | tf_op jit(solution)/shard_map/slice | solution.py:303
  95.6 0.0 copy-done.9
  95.6 16.9 %all-to-all-done.8 = f32[192,16,128]{2,1,0:T(8,128)} async-done(((f32[192,16,128]{2,1,0:T(8,128)}), f32[192,16,128]{2,1,0:T(8,128)}, u32[]{:S(2)}, u32[]{:S(2)}) %all-to-all-start.8) | async-done | bytes 1572896 | tf_op jit(solution)/shard_map/all_to_all | solution.py:22
  112.4 5.0 %all-to-all-start.10 = ((f32[320,16,128]{2,1,0:T(8,128)}), f32[320,16,128]{2,1,0:T(8,128)S(1)}, u32[]{:S(2)}, u32[]{:S(2)}) async-start(f32[320,16,128]{2,1,0:T(8,128)} %slice.57), calls=%async_computation.10 | async-start | bytes 5242880 | tf_op jit(solution)/shard_map/all_to_all | solution.py:22
  117.4 0.1 compare_convert_fusion
  117.5 3.8 %radial_apply.10 = f32[8,24,16,128]{3,2,1,0:T(8,128)} custom-call(bf16[256,256]{1,0:T(8,128)(2,1)S(1)} %maximum_maximum_fusion.1.matrix_ref, f32[8,24,16,128]{3,2,1,0:T(8,128)} %bitcast.19.x_ref), custom_call_target="tpu_custom_call" | custom-call | flops 480000000 | bytes 3145728 | tf_op jit(solution)/shard_map/radial_apply/pallas_call | solution.py:145
  121.2 27.6 %all-to-all-done.10 = f32[320,16,128]{2,1,0:T(8,128)S(1)} async-done(((f32[320,16,128]{2,1,0:T(8,128)}), f32[320,16,128]{2,1,0:T(8,128)S(1)}, u32[]{:S(2)}, u32[]{:S(2)}) %all-to-all-start.10) | async-done | bytes 2621472 | tf_op jit(solution)/shard_map/all_to_all | solution.py:22
  148.8 0.0 copy-start.7
  148.8 1.5 copy-done.7
  150.3 4.9 %all-to-all-start.9 = ((f32[192,16,128]{2,1,0:T(8,128)}), f32[192,16,128]{2,1,0:T(8,128)S(1)}, u32[]{:S(2)}, u32[]{:S(2)}) async-start(f32[192,16,128]{2,1,0:T(8,128)} %bitcast.50), calls=%async_computation.9 | async-start | bytes 3145728 | tf_op jit(solution)/shard_map/all_to_all | solution.py:22
  155.2 3.3 %broadcast_multiply_fusion = f32[2,384,16,128]{3,2,1,0:T(8,128)S(1)} fusion(f32[2,384,16,128]{3,2,1,0:T(8,128)} %param.16, f32[2,384]{1,0:T(2,128)S(1)} %compare_convert_fusion), kind=kLoop, calls=%fused_computation.1 | loop fusion | flops 1572864 | bytes 12585984 | tf_op jit(solution)/shard_map/mul | solution.py:306
  158.6 3.0 %fusion.4 = (f32[1,384,16,128]{3,2,1,0:T(8,128)}, f32[1,384,16,128]{3,2,1,0:T(8,128)}) fusion(f32[2,384,16,128]{3,2,1,0:T(8,128)S(1)} %broadcast_multiply_fusion), kind=kLoop, calls=%fused_computation.20 | loop fusion | bytes 12582912 | tf_op jit(solution)/shard_map/slice | solution.py:307
  161.6 1.9 collective-permute-start
  163.5 3.9 %collective-permute-start.1 = (f32[1,384,16,128]{3,2,1,0:T(8,128)}, f32[1,384,16,128]{3,2,1,0:T(8,128)}, u32[]{:S(2)}, u32[]{:S(2)}) collective-permute-start(f32[1,384,16,128]{3,2,1,0:T(8,128)} %get-tuple-element.40), channel_id=1, source_target_pairs={{8,0},{16,8},{24,16},{32,24},{40,32},{48,40},{56,48},{64,56},{72,6... | collective-permute-start | bytes 9437192 | tf_op jit(solution)/shard_map/ppermute | solution.py:18
  167.5 5.3 %radial_apply.11 = f32[8,40,16,128]{3,2,1,0:T(8,128)} custom-call(bf16[256,256]{1,0:T(8,128)(2,1)S(1)} %maximum_maximum_fusion.1.matrix_ref, f32[8,40,16,128]{3,2,1,0:T(8,128)} %bitcast.43), custom_call_target="tpu_custom_call" | custom-call | flops 800000000 | bytes 5242880 | tf_op jit(solution)/shard_map/radial_apply/pallas_call | solution.py:145
  172.8 2.6 all-to-all-done.9
  175.4 0.0 copy-start.2
  175.4 1.2 copy-done.2
  176.6 0.0 copy-start.12
  176.6 0.0 copy-start.13
  176.6 5.1 %all-to-all-start.11 = ((f32[320,16,128]{2,1,0:T(8,128)}), f32[320,16,128]{2,1,0:T(8,128)S(1)}, u32[]{:S(2)}, u32[]{:S(2)}) async-start(f32[320,16,128]{2,1,0:T(8,128)} %bitcast.42), calls=%async_computation.11 | async-start | bytes 5242880 | tf_op jit(solution)/shard_map/all_to_all | solution.py:22
  182.4 0.0 copy-done.12
  182.4 0.1 copy.15
  182.5 0.1 pad_add_fusion.skipped
  182.6 0.7 constant_dynamic-slice_fusion.2
  183.3 0.7 constant_dynamic-slice_fusion.1
  184.0 0.0 copy-done
  184.1 0.0 copy-done.13
  184.1 0.0 slice-start
  184.1 0.1 broadcast_in_dim.2.factor_ref
  184.2 0.0 copy-done.6
  184.2 1.6 copy-done.5
  185.7 42.0 %local_terms.1.out_in = f32[2,6144,128]{2,1,0:T(8,128)} custom-call(s32[2]{0:T(128)S(1)} %copy-done.4, f32[2,384]{1,0:T(2,128)S(1)} %copy-done.6, f32[2,6144,128]{2,1,0:T(8,128)} %bitcast.35, f32[2,6144,128]{2,1,0:T(8,128)} %bitcast.57, f32[8192,128]{1,0:T(8,128)} %bitcast.58, f32[2,512,384]{2,1,0:T(8,128)S(1)} %copy-done.5, ...), custom_call_target="tpu_custom_call" | custom-call | flops 12000000000 | bytes 27000000 | tf_op jit(solution)/shard_map/local_terms/pallas_call | solution.py:104
  227.8 6.2 %collective-permute-done = f32[1,384,16,128]{3,2,1,0:T(8,128)} collective-permute-done((f32[1,384,16,128]{3,2,1,0:T(8,128)}, f32[1,384,16,128]{3,2,1,0:T(8,128)}, u32[]{:S(2)}, u32[]{:S(2)}) %collective-permute-start) | collective-permute-done | bytes 3145760 | tf_op jit(solution)/shard_map/ppermute | solution.py:18
  234.0 1.9 collective-permute-done.1
  235.9 0.0 slice-done
  235.9 0.0 slice-done.1
  235.9 1.4 copy-done.3
  237.3 9.1 %middle_terms.1 = f32[2,6144,128]{2,1,0:T(8,128)} custom-call(s32[2]{0:T(128)S(1)} %copy-done.4, f32[3,384]{1,0:T(4,128)S(1)} %pad_maximum_fusion.2.coriolis, f32[2,6144,128]{2,1,0:T(8,128)} %local_terms.1.out_in, f32[2,6144,128]{2,1,0:T(8,128)S(1)} %bitcast.38, f32[6144,128]{1,0:T(8,128)} %bitcast.16.lower_ref, ...), custom_call_target="tpu_custom_call", output_to_operand_aliasing={{}: (2, {})} | custom-call | flops 30000000 | bytes 27000000 | tf_op jit(solution)/shard_map/middle_terms/pallas_call | solution.py:200
  246.4 0.0 all-to-all-done.11
  246.4 7.9 %add_second.1.out_in = f32[12288,128]{1,0:T(8,128)} custom-call(s32[2]{0:T(128)S(1)} %copy-done.4, f32[12288,128]{1,0:T(8,128)} %bitcast.41, f32[5120,128]{1,0:T(8,128)S(1)} %bitcast.39, f32[16,128]{1,0:T(8,128)S(1)} %broadcast_in_dim.2.factor_ref), custom_call_target="tpu_custom_call", output_to_operand_aliasing={{}: (1, {})} | custom-call | flops 3000000 | bytes 15000000 | tf_op jit(solution)/shard_map/add_second/pallas_call | solution.py:243
  254.4 0.0 copy-done.10
  254.4 4.9 %add_tail.1 = f32[12288,128]{1,0:T(8,128)} custom-call(s32[2]{0:T(128)S(1)} %copy-done.4, s32[2]{0:T(128)S(1)} %pad_add_fusion.skipped, f32[12288,128]{1,0:T(8,128)} %add_second.1.out_in, f32[4096,128]{1,0:T(8,128)S(1)} %copy-done.10, f32[16,128]{1,0:T(8,128)S(1)} %broadcast_in_dim.2.factor_ref), custom_call_target="tpu_custom_call", output_to_operand_aliasing={{}: (2, {})} | custom-call | flops 1000000 | bytes 6300000 | tf_op jit(solution)/shard_map/add_tail/pallas_call | solution.py:271
  259.3 0.0 copy-done.1
  (13 shorter events, 0.1 us)
Async XLA Ops:
  0.0 184.0 %copy-start = (f32[128,128]{1,0:T(8,128)S(1)}, f32[128,128]{1,0:T(8,128)}, u32[]{:S(2)}) copy-start(f32[128,128]{1,0:T(8,128)} %param.21) | copy-start | bytes 196612
  2.7 4.1 %copy-start.4 = (s32[2]{0:T(128)S(1)}, s32[2]{0:T(128)}, u32[]{:S(2)}) copy-start(s32[2]{0:T(128)} %sizes.7) | copy-start | bytes 28
  2.7 6.1 %copy-start.11 = (f32[128,128]{1,0:T(8,128)S(1)}, f32[128,128]{1,0:T(8,128)}, u32[]{:S(2)}) copy-start(f32[128,128]{1,0:T(8,128)} %param.23) | copy-start | bytes 196612
  10.2 2.8 %copy-start.8 = (f32[288,16,128]{2,1,0:T(8,128)S(1)}, f32[288,16,128]{2,1,0:T(8,128)}, u32[]{:S(2)}) copy-start(f32[288,16,128]{2,1,0:T(8,128)} %get-tuple-element.37) | copy-start | bytes 7077892
  86.5 9.0 %copy-start.9 = (f32[4096,128]{1,0:T(8,128)}, f32[4096,128]{1,0:T(8,128)S(1)}, u32[]{:S(2)}) copy-start(f32[4096,128]{1,0:T(8,128)S(1)} %get-tuple-element.48.back_ref) | copy-start | bytes 6291460
  86.5 25.9 %all-to-all-start.8 = ((f32[192,16,128]{2,1,0:T(8,128)}), f32[192,16,128]{2,1,0:T(8,128)}, u32[]{:S(2)}, u32[]{:S(2)}) async-start(f32[192,16,128]{2,1,0:T(8,128)} %pad_maximum_fusion.1), calls=%async_computation.8 | async-start | bytes 3145728 | tf_op jit(solution)/shard_map/all_to_all | solution.py:22
  112.4 36.4 %all-to-all-start.10 = ((f32[320,16,128]{2,1,0:T(8,128)}), f32[320,16,128]{2,1,0:T(8,128)S(1)}, u32[]{:S(2)}, u32[]{:S(2)}) async-start(f32[320,16,128]{2,1,0:T(8,128)} %slice.57), calls=%async_computation.10 | async-start | bytes 5242880 | tf_op jit(solution)/shard_map/all_to_all | solution.py:22
  148.8 1.5 copy-start.7
  150.3 25.1 %all-to-all-start.9 = ((f32[192,16,128]{2,1,0:T(8,128)}), f32[192,16,128]{2,1,0:T(8,128)S(1)}, u32[]{:S(2)}, u32[]{:S(2)}) async-start(f32[192,16,128]{2,1,0:T(8,128)} %bitcast.50), calls=%async_computation.9 | async-start | bytes 3145728 | tf_op jit(solution)/shard_map/all_to_all | solution.py:22
  161.6 72.4 %collective-permute-start = (f32[1,384,16,128]{3,2,1,0:T(8,128)}, f32[1,384,16,128]{3,2,1,0:T(8,128)}, u32[]{:S(2)}, u32[]{:S(2)}) collective-permute-start(f32[1,384,16,128]{3,2,1,0:T(8,128)} %get-tuple-element.41), channel_id=1, source_target_pairs={{0,8},{8,16},{16,24},{24,32},{32,40},{40,48},{48,56},{56,64},{64,7... | collective-permute-start | bytes 9437192 | tf_op jit(solution)/shard_map/ppermute | solution.py:18
  163.5 72.4 %collective-permute-start.1 = (f32[1,384,16,128]{3,2,1,0:T(8,128)}, f32[1,384,16,128]{3,2,1,0:T(8,128)}, u32[]{:S(2)}, u32[]{:S(2)}) collective-permute-start(f32[1,384,16,128]{3,2,1,0:T(8,128)} %get-tuple-element.40), channel_id=1, source_target_pairs={{8,0},{16,8},{24,16},{32,24},{40,32},{48,40},{56,48},{64,56},{72,6... | collective-permute-start | bytes 9437192 | tf_op jit(solution)/shard_map/ppermute | solution.py:18
  175.4 1.2 copy-start.2
  176.6 5.8 %copy-start.12 = (f32[128,128]{1,0:T(8,128)S(1)}, f32[128,128]{1,0:T(8,128)}, u32[]{:S(2)}) copy-start(f32[128,128]{1,0:T(8,128)} %param.24) | copy-start | bytes 196612
  176.6 7.5 %copy-start.13 = (f32[16]{0:T(128)S(1)}, f32[16]{0:T(128)}, u32[]{:S(2)}) copy-start(f32[16]{0:T(128)} %param.22) | copy-start | bytes 196
  176.6 7.6 %copy-start.6 = (f32[2,384]{1,0:T(2,128)S(1)}, f32[2,384]{1,0:T(2,128)}, u32[]{:S(2)}) copy-start(f32[2,384]{1,0:T(2,128)} %centrifugal.1) | copy-start | bytes 9220
  176.6 69.9 %all-to-all-start.11 = ((f32[320,16,128]{2,1,0:T(8,128)}), f32[320,16,128]{2,1,0:T(8,128)S(1)}, u32[]{:S(2)}, u32[]{:S(2)}) async-start(f32[320,16,128]{2,1,0:T(8,128)} %bitcast.42), calls=%async_computation.11 | async-start | bytes 5242880 | tf_op jit(solution)/shard_map/all_to_all | solution.py:22
  184.1 51.8 %slice-start = ((s8[6291456]{0:T(1024)(128)(4,1)}), s8[4194304]{0:T(1024)(128)(4,1)S(1)}, s32[]{:S(2)}) async-start(s8[6291456]{0:T(1024)(128)(4,1)} %bitcast.36), calls=%async_computation.12 | async-start | bytes 8388608
  184.2 1.6 copy-start.5
  185.7 50.2 %slice-start.1 = ((s8[6291456]{0:T(1024)(128)(4,1)}), s8[2097152]{0:T(1024)(128)(4,1)S(1)}, s32[]{:S(2)}) async-start(s8[6291456]{0:T(1024)(128)(4,1)} %bitcast.36), calls=%async_computation.13 | async-start | bytes 4194304
  235.9 1.4 copy-start.3
  246.4 7.9 %copy-start.10 = (f32[4096,128]{1,0:T(8,128)S(1)}, f32[4096,128]{1,0:T(8,128)}, u32[]{:S(2)}) copy-start(f32[4096,128]{1,0:T(8,128)} %copy-done.9) | copy-start | bytes 6291460
  254.4 4.9 %copy-start.1 = (f32[128,128]{1,0:T(8,128)S(1)}, f32[128,128]{1,0:T(8,128)}, u32[]{:S(2)}) copy-start(f32[128,128]{1,0:T(8,128)} %param.21) | copy-start | bytes 196612
where the time goes:
time: 261 us; the launch traced here: 259 us
  Pallas kernels  77.4 us (30%)
  blocking collectives  61.8 us (24%)
  waiting for transfers between devices  55.1 us (21%)
  starting transfers between devices  26.5 us (10%)
  local copies, waits for them, and re-layouts  26.1 us (10%)
  other arithmetic  8.82 us (3%)
  between operations  3.56 us (1%)
    all_to_all x2, blocking collectives, exchange(): return lax.all_to_all(x, 'row', split_axis=0, concat_axis=0, tiled=True)  61.8 us
    all_to_all x4, waiting for transfers between devices, exchange(): return lax.all_to_all(x, 'row', split_axis=0, concat_axis=0, tiled=True)  47 us
    pallas_call x1, Pallas kernels, local_terms(): pl.pallas_call(local_kernel, grid=(blocks,), in_specs=[smem, smem, whole,...  42 us
    all_to_all x4, starting transfers between devices, exchange(): return lax.all_to_all(x, 'row', split_axis=0, concat_axis=0, tiled=True)  20.7 us
    pallas_call x3, Pallas kernels, radial_apply(): pl.pallas_call(radial_kernel, grid=(columns // 8,), in_specs=[pl.BlockSpe...  13.4 us
    pallas_call x1, Pallas kernels, middle_terms(): pl.pallas_call(middle_kernel, grid=(parts,), in_specs=[smem, smem, pair,...  9.11 us
    ppermute x2, waiting for transfers between devices, from_behind(): return lax.ppermute(x, axis, pairs)  8.13 us
    pallas_call x1, Pallas kernels, add_second(): pl.pallas_call(add_second_kernel, in_specs=[smem, full(out), full(back),...  7.93 us
  transfers between devices with their start and end apart: 6, of which 5 were waited for; matrix products, arithmetic and copies ran while one was open for 4% of the time, Pallas kernels for 23%

commit v1 on v0

v1 whole, which is shorter than its diff:
```python
import functools

import jax
import jax.numpy as jnp
from jax import lax
from jax.experimental import pallas as pl
from jax.experimental.pallas import tpu as pltpu
from jax.sharding import PartitionSpec as P

F32 = jnp.float32
BF16 = jnp.bfloat16
MIB = 1 << 20


def from_behind(x, axis, by):
    peers = lax.axis_size(axis)
    pairs = [(i, i + by) for i in range(peers) if 0 <= i + by < peers]
    return lax.ppermute(x, axis, pairs)


def exchange(x):
    return lax.all_to_all(x, "row", split_axis=0, concat_axis=0, tiled=True)


def halves(x):
    high = x.astype(BF16)
    return high, (x - high.astype(F32)).astype(BF16)


def halves_outside(x):
    high = lax.reduce_precision(x, 8, 7)
    return high.astype(BF16), (x - high).astype(BF16)


def local_kernel(
    block, sizes, centrifugal, x_ref, previous_ref, potential_ref, legendre_ref, stretch_ref,
    inertia_ref, factor_ref, out_ref, acc, ahead, back,
):
    live = sizes[block]
    angles, basis = legendre_ref.shape[1:]
    radial = inertia_ref.shape[0]
    rows = basis * radial
    high, low = halves(legendre_ref[0])
    ahead[:, :basis] = high
    ahead[:, basis : 2 * basis] = high
    ahead[:, 2 * basis :] = low
    high, low = halves(legendre_ref[0].T)
    back[:, :angles] = high
    back[:, angles : 2 * angles] = high
    back[:, 2 * angles :] = low

    piece = rows // 8

    @pl.loop(0, 8)
    def _(i):
        at = pl.ds(pl.multiple_of(i * piece, piece), piece)
        high, low = halves(x_ref[0, at, :])
        both = jnp.dot(
            jnp.concatenate([high, low], 1), stretch_ref[...], preferred_element_type=F32
        )
        acc[at, :] = both[:, :128] + both[:, 128:]

    mask = lax.broadcasted_iota(jnp.int32, (basis, 256), 0) < live

    @pl.loop(0, radial // 2)
    def _(i):
        r = 2 * i
        here = [pl.ds(r + k, basis, stride=radial) for k in range(2)]
        there = [pl.ds(r + k, angles, stride=radial) for k in range(2)]
        m = jnp.concatenate([x_ref[0, at, :] for at in here], 1)
        m = jnp.where(mask, m, 0.0)
        high, low = halves(m)
        grid = jnp.dot(
            ahead[...], jnp.concatenate([high, low, high], 0), preferred_element_type=F32
        )
        grid = grid * jnp.concatenate([potential_ref[at, :] for at in there], 1)
        high, low = halves(grid)
        term = jnp.dot(
            back[...], jnp.concatenate([high, low, high], 0), preferred_element_type=F32
        )
        for k in range(2):
            acc[here[k], :] += term[:, 128 * k : 128 * (k + 1)]

    inertia = inertia_ref[...]
    factor = factor_ref[...]

    @pl.loop(0, basis // 8)
    def _(i):
        for k in range(8):
            j = i * 8 + k
            at = pl.ds(pl.multiple_of(j * radial, radial), radial)
            value = acc[at, :] + (centrifugal[block, j] * inertia) * x_ref[0, at, :]
            value = factor * (2.0 * value - factor * previous_ref[0, at, :])
            out_ref[0, at, :] = jnp.where(j < live, value, 0.0)


def local_terms(block, sizes, centrifugal, x, previous, potential, legendre, stretch, inertia, factor):
    angles, basis = legendre.shape[1:]
    rows = x.shape[1]
    whole = pl.BlockSpec((1, rows, 128), lambda k: (block, 0, 0))
    smem = pl.BlockSpec(memory_space=pltpu.SMEM)
    once = lambda shape: pl.BlockSpec(shape, lambda k: (0,) * len(shape))
    return pl.pallas_call(
        functools.partial(local_kernel, block),
        grid=(1,),
        in_specs=[
            smem, smem, whole, whole, once(potential.shape),
            pl.BlockSpec((1, angles, basis), lambda k: (block, 0, 0)),
            once(stretch.shape), once(inertia.shape), once(factor.shape),
        ],
        out_specs=once((1, rows, 128)),
        out_shape=jax.ShapeDtypeStruct((1, rows, 128), F32),
        scratch_shapes=[
            pltpu.VMEM((rows, 128), F32),
            pltpu.VMEM((angles, 3 * basis), BF16),
            pltpu.VMEM((basis, 3 * angles), BF16),
        ],
        compiler_params=pltpu.CompilerParams(vmem_limit_bytes=40 * MIB),
        cost_estimate=pl.CostEstimate(
            flops=8_000_000_000, bytes_accessed=16_000_000, transcendentals=0
        ),
        name="local_terms",
    )(sizes, centrifugal, x, previous, potential, legendre, stretch, inertia, factor)


def pair_product(matrix, pair):
    m = jnp.concatenate(pair, 1)
    high, low = halves(m)
    both = jnp.dot(matrix, jnp.concatenate([high, low], 0), preferred_element_type=F32)
    half = both.shape[0] // 2
    total = both[:half] + both[half:]
    return total[:, :128], total[:, 128:]


def radial_kernel(matrix_ref, x_ref, out_ref):
    peers, columns, rows, width = x_ref.shape
    for c in range(0, columns, 2):
        pair = [x_ref[:, c + k].reshape(peers * rows, width) for k in range(2)]
        for k, total in enumerate(pair_product(matrix_ref[...], pair)):
            out_ref[:, c + k] = total.reshape(peers, rows, width)


def radial_apply(matrix, received):
    peers, columns, rows, width = received.shape
    some = pl.BlockSpec((peers, 8, rows, width), lambda i: (0, i, 0, 0))
    return pl.pallas_call(
        radial_kernel,
        grid=(columns // 8,),
        in_specs=[pl.BlockSpec(matrix.shape, lambda i: (0, 0)), some],
        out_specs=some,
        out_shape=jax.ShapeDtypeStruct(received.shape, F32),
        cost_estimate=pl.CostEstimate(
            flops=columns * 20_000_000, bytes_accessed=2 * 4 * received.size, transcendentals=0
        ),
        name="radial_apply",
    )(matrix, received)


def radial_apart_kernel(where_ref, matrix_ref, *refs):
    *ours, theirs, out_theirs, turned = refs
    chips = len(ours) // 2
    ours, outs = ours[:chips], ours[chips:]
    columns, rows, width = theirs.shape[1:]

    @pl.when(pl.program_id(0) == 0)
    def _():
        size = matrix_ref.shape[0]
        i = lax.broadcasted_iota(jnp.int32, (size, size), 0)
        j = lax.broadcasted_iota(jnp.int32, (size, size), 1)
        moved = jnp.where(j == (i ^ (where_ref[0] * rows)), 1.0, 0.0).astype(BF16)
        half = jnp.dot(moved, matrix_ref[...], preferred_element_type=F32).astype(BF16)
        turned[...] = jnp.dot(half, moved, preferred_element_type=F32).astype(BF16)

    for c in range(0, columns, 2):
        pair = []
        for k in range(2):
            pieces = []
            for d in range(chips):
                pieces += [ours[d][0, c + k], theirs[d, c + k]]
            pair.append(jnp.concatenate(pieces, 0))
        for k, total in enumerate(pair_product(turned[...], pair)):
            for d in range(chips):
                at = 2 * d * rows
                outs[d][c + k] = total[at : at + rows]
                out_theirs[d, c + k] = total[at + rows : at + 2 * rows]


def radial_apart(where, matrix, ours, theirs):
    chips = len(ours)
    columns, rows, width = theirs.shape[1:]
    mine = pl.BlockSpec((1, 8, rows, width), lambda i, where: (where[1], i, 0, 0))
    made = pl.BlockSpec((8, rows, width), lambda i, where: (i, 0, 0))
    all_chips = pl.BlockSpec((chips, 8, rows, width), lambda i, where: (0, i, 0, 0))

    def kernel(where_ref, matrix_ref, *refs):
        ins, theirs_ref = refs[:chips], refs[chips]
        outs, out_theirs, turned = refs[chips + 1 : 2 * chips + 1], refs[-2], refs[-1]
        radial_apart_kernel(where_ref, matrix_ref, *ins, *outs, theirs_ref, out_theirs, turned)

    return pl.pallas_call(
        kernel,
        grid_spec=pltpu.PrefetchScalarGridSpec(
            num_scalar_prefetch=1,
            grid=(columns // 8,),
            in_specs=[pl.BlockSpec(matrix.shape, lambda i, where: (0, 0))]
            + [mine] * chips + [all_chips],
            out_specs=[made] * chips + [all_chips],
            scratch_shapes=[pltpu.VMEM(matrix.shape, BF16)],
        ),
        out_shape=[jax.ShapeDtypeStruct(theirs.shape[1:], F32)] * chips
        + [jax.ShapeDtypeStruct(theirs.shape, F32)],
        cost_estimate=pl.CostEstimate(
            flops=columns * 20_000_000, bytes_accessed=16 * theirs.size, transcendentals=0
        ),
        name="radial_apart",
    )(where, matrix, *ours, theirs)


def middle_kernel(
    sizes, coriolis, below_ref, above_ref, x_ref, lower_ref, upper_ref, inertia_ref, factor_ref, out_ref
):
    step = pl.program_id(0)
    radial = inertia_ref.shape[0]
    count = x_ref.shape[1] // radial
    both = 2.0 * factor_ref[...] * inertia_ref[...]
    below, above = sizes[0], sizes[1]

    @pl.loop(0, count // 4)
    def _(i):
        for k in range(4):
            local = i * 4 + k
            j = step * count + local
            at = pl.ds(pl.multiple_of(local * radial, radial), radial)
            here = jnp.where(j < below, x_ref[0, at, :], 0.0)
            there = jnp.where(j < above, x_ref[1, at, :], 0.0)
            low = coriolis[1, j] * there + coriolis[0, j] * lower_ref[at, :]
            high = coriolis[2, j] * upper_ref[at, :] + coriolis[1, j] * here
            out_ref[0, at, :] = below_ref[0, at, :] + jnp.where(j < below, both * low, 0.0)
            out_ref[1, at, :] = above_ref[0, at, :] + jnp.where(j < above, both * high, 0.0)


def middle_terms(sizes, coriolis, below, above, x, lower, upper, inertia, factor):
    blocks, rows, width = x.shape
    parts = 8
    smem = pl.BlockSpec(memory_space=pltpu.SMEM)
    pair = pl.BlockSpec((blocks, rows // parts, width), lambda i: (0, i, 0))
    single = pl.BlockSpec((1, rows // parts, width), lambda i: (0, i, 0))
    one = pl.BlockSpec((rows // parts, width), lambda i: (i, 0))
    small = pl.BlockSpec(inertia.shape, lambda i: (0, 0))
    return pl.pallas_call(
        middle_kernel,
        grid=(parts,),
        in_specs=[smem, smem, single, single, pair, one, one, small, small],
        out_specs=pair,
        out_shape=jax.ShapeDtypeStruct(x.shape, F32),
        compiler_params=pltpu.CompilerParams(vmem_limit_bytes=20 * MIB),
        cost_estimate=pl.CostEstimate(flops=30_000_000, bytes_accessed=25_000_000, transcendentals=0),
        name="middle_terms",
    )(sizes, coriolis, below, above, x, lower, upper, inertia, factor)


def add_rows(target, source, double, columns, begin, live):
    radial = double.shape[0]

    @pl.loop(0, columns // 8)
    def _(i):
        for k in range(8):
            j = i * 8 + k
            at = pl.ds(pl.multiple_of(j * radial, radial), radial)
            target(at, jnp.where(begin + j < live, double * source[at, :], 0.0))


def add_apart_kernel(basis, lead, where, sizes, out_in, factor_ref, *refs):
    backs, out_ref = refs[:-1], refs[-1]
    step = pl.program_id(0)
    part = out_in.shape[0] // 2
    columns = part // factor_ref.shape[0]
    begin = (lead + (where[0] // 2 ^ step)) * 2 * columns
    live = jnp.where(begin < basis, sizes[0], sizes[1] + basis)
    for d, back_ref in enumerate(backs):
        @pl.when(step == d)
        def _():
            for core in range(2):
                source = back_ref.at[pl.ds(pl.multiple_of((where[1] ^ core) * part, part), part), :]

                def target(at, more):
                    to = pl.ds(core * part + at.start, at.size)
                    out_ref[to, :] = out_in[to, :] + more

                add_rows(target, source, 2.0 * factor_ref[...], columns, begin + core * columns, live)


def add_apart(basis, lead, where, sizes, out, backs, factor):
    rows, width = backs[0].shape
    window = pl.BlockSpec((rows, width), lambda i, where, sizes: (lead + (where[0] // 2 ^ i), 0))
    full = lambda a: pl.BlockSpec(a.shape, lambda i, where, sizes: (0, 0))
    return pl.pallas_call(
        functools.partial(add_apart_kernel, basis, lead),
        grid_spec=pltpu.PrefetchScalarGridSpec(
            num_scalar_prefetch=2,
            grid=(len(backs),),
            in_specs=[window, full(factor)] + [full(b) for b in backs],
            out_specs=window,
        ),
        out_shape=jax.ShapeDtypeStruct(out.shape, F32),
        input_output_aliases={2: 0},
        compiler_params=pltpu.CompilerParams(vmem_limit_bytes=20 * MIB),
        cost_estimate=pl.CostEstimate(
            flops=1_000_000, bytes_accessed=12 * rows * width * len(backs), transcendentals=0
        ),
        name="add_apart",
    )(where, sizes, out, factor, *backs)


def add_joined_kernel(basis, sizes, out_in, back_ref, factor_ref, out_ref):
    columns = out_in.shape[0] // factor_ref.shape[0]
    begin = pl.program_id(0) * columns
    live = jnp.where(begin < basis, sizes[0], sizes[1] + basis)

    def target(at, more):
        out_ref[at, :] = out_in[at, :] + more

    add_rows(target, back_ref, 2.0 * factor_ref[...], columns, begin, live)


def add_joined(basis, sizes, out, back, factor):
    rows, width = back.shape
    part = 128 * factor.shape[0]
    some = pl.BlockSpec((part, width), lambda i: (i, 0))
    return pl.pallas_call(
        functools.partial(add_joined_kernel, basis),
        grid=(rows // part,),
        in_specs=[
            pl.BlockSpec(memory_space=pltpu.SMEM), some, some,
            pl.BlockSpec(factor.shape, lambda i: (0, 0)),
        ],
        out_specs=some,
        out_shape=jax.ShapeDtypeStruct(out.shape, F32),
        input_output_aliases={1: 0},
        compiler_params=pltpu.CompilerParams(vmem_limit_bytes=20 * MIB),
        cost_estimate=pl.CostEstimate(
            flops=1_000_000, bytes_accessed=12 * rows * width, transcendentals=0
        ),
        name="add_joined",
    )(sizes, out, back, factor)


def swap(x, by):
    peers = lax.axis_size("row")
    return lax.ppermute(x, "row", [(i, i ^ by) for i in range(peers)])


def after(x, *first):
    return lax.optimization_barrier((x, *first))[0]


def shards(
    packet, previous, basis_sizes, centrifugal, coriolis, inertia, damping,
    radial_kin, stretch_kin, legendre, potential,
):
    blocks, basis, radial, width = packet.shape
    peers = lax.axis_size("row")
    ka = lax.axis_index("ka")
    row = lax.axis_index("row")
    columns = blocks * basis
    rows = basis * radial
    joined = 2 * columns // 3
    piece = (columns - joined) // peers
    chips = peers // 2
    x_chip, core = row // 2, row % 2

    flat = packet.reshape(columns, radial, width)
    sent_a = flat[:joined]
    got_a = exchange(sent_a)
    source = after(flat, sent_a)
    sent = [
        lax.dynamic_slice_in_dim(source, joined + (x_chip ^ d) * 2 * piece, 2 * piece, 0)
        for d in range(chips)
    ]
    ours = [sent[0]] + [swap(sent[d], 2 * d) for d in range(1, chips)]
    live_mask = (lax.broadcasted_iota(jnp.int32, (blocks, basis), 1) < basis_sizes[:, None]).astype(F32)
    source = after(packet, *sent)
    upper = source[:1] * live_mask[:1, :, None, None]
    lower = source[1:] * live_mask[1:, :, None, None]
    from_ahead = from_behind(upper, "ka", -1)
    from_below = from_behind(lower, "ka", 1)

    inertia_local = lax.dynamic_slice_in_dim(inertia, row * radial, radial, 0)
    factor = jnp.broadcast_to(damping[:, None], (radial, width))
    t_high, t_low = halves_outside(radial_kin)
    t_high, t_low = [jnp.concatenate([t, t], 1) for t in (t_high, t_low)]
    matrix = jnp.concatenate([t_high, t_low], 0)
    s_high, s_low = halves_outside(stretch_kin.T)
    stretch = jnp.concatenate([jnp.concatenate([s_high, s_low], 1)] * 2, 0)
    start = jnp.maximum(ka * blocks - 1, 0)
    coupling = jnp.concatenate(
        [lax.dynamic_slice_in_dim(coriolis, start, 1, 0),
         lax.dynamic_slice_in_dim(coriolis, ka * blocks, blocks, 0)], 0
    )

    x = packet.reshape(blocks, rows, width)
    before = previous.reshape(blocks, rows, width)
    grid = potential.reshape(potential.shape[0] * radial, width)

    def local(block, x):
        return local_terms(
            block, basis_sizes, centrifugal, x, before, grid, legendre, stretch, inertia_local, factor
        )

    below = local(0, after(x, upper, lower))
    above = local(1, after(x, below))
    made_a = radial_apply(after(matrix, above), got_a.reshape(peers, joined // peers, radial, width))
    back_a = exchange(made_a.reshape(joined, radial, width))
    ours = lax.optimization_barrier((made_a, *ours))[1:]
    ours = [o.reshape(2, piece, radial, width) for o in ours]
    passed = [lax.dynamic_index_in_dim(o, 1 - core, 0) for o in ours]
    theirs = swap(jnp.concatenate(passed, 0), 1)
    where = jnp.stack([row, core]).astype(jnp.int32)
    *made_b, passed = radial_apart(where, after(matrix, made_a, from_ahead, from_below), ours, theirs)
    passed = swap(passed, 1)
    joint = [jnp.concatenate([made_b[d], passed[d]], 0) for d in range(chips)]
    back_b = [joint[0]] + [swap(joint[d], 2 * d) for d in range(1, chips)]

    upper = from_ahead.reshape(rows, width)
    lower = from_below.reshape(rows, width)
    out = middle_terms(
        basis_sizes, coupling, below, above, after(x, *joint), lower, upper, inertia_local, factor
    )
    out = out.reshape(columns * radial, width)
    out = add_joined(basis, basis_sizes, out, back_a.reshape(joined * radial, width), factor)
    out = add_apart(
        basis, joined // (2 * piece), where, basis_sizes, out,
        [b.reshape(2 * piece * radial, width) for b in back_b], factor,
    )
    return out.reshape(packet.shape)


def solution(mesh):
    in_specs = (
        P("ka", None, "row", None),
        P("ka", None, "row", None),
        P("ka"),
        P("ka", None),
        P(),
        P(),
        P("row"),
        P(),
        P(),
        P("ka", None, None),
        P(None, "row", None),
    )
    out_specs = P("ka", None, "row", None)
    return jax.shard_map(shards, mesh=mesh, in_specs=in_specs, out_specs=out_specs, check_vma=False)
```

time: 261 us -> 170 us (0.65)
  the two profiles are of different devices: /device:TPU:50 before, /device:TPU:1 now
where the time goes in v1:
time: 170 us; the launch traced here: 169 us
  Pallas kernels  74.1 us (44%)
  waiting for transfers between devices  31.4 us (18%)
  starting transfers between devices  26.4 us (16%)
  local copies, waits for them, and re-layouts  24.8 us (15%)
  other arithmetic  12 us (7%)
    pallas_call x2, Pallas kernels, local_terms(): pl.pallas_call(functools.partial(local_kernel, block), grid=(1,), in_spec...  41.4 us
    ppermute x8, waiting for transfers between devices, swap(): return lax.ppermute(x, 'row', [(i, i ^ by) for i in range(peers)])  20.9 us
    unnamed x37, local copies, waits for them, and re-layouts  13.6 us
    all_to_all x2, starting transfers between devices, exchange(): return lax.all_to_all(x, 'row', split_axis=0, concat_axis=0, tiled=True)  11.9 us
    all_to_all x2, waiting for transfers between devices, exchange(): return lax.all_to_all(x, 'row', split_axis=0, concat_axis=0, tiled=True)  10.5 us
    pallas_call x1, Pallas kernels, middle_terms(): pl.pallas_call(middle_kernel, grid=(parts,), in_specs=[smem, smem, single...  8.43 us
    pallas_call x1, Pallas kernels, radial_apply(): pl.pallas_call(radial_kernel, grid=(columns // 8,), in_specs=[pl.BlockSpe...  7.57 us
    ppermute x8, starting transfers between devices, swap(): return lax.ppermute(x, 'row', [(i, i ^ by) for i in range(peers)])  7.56 us
  transfers between devices with their start and end apart: 12, of which 4 were waited for; matrix products, arithmetic and copies ran while one was open for 11% of the time, Pallas kernels for 41%

profile of v1, /device:TPU:1, one launch (start us, length us, event | category | flops | bytes accessed | tf_op | source)
XLA Modules:
  0.0 168.8 jit_solution(4680171779498105908)
XLA Ops:
  0.0 0.0 copy-start
  0.0 4.5 %slice.36 = f32[512,16,128]{2,1,0:T(8,128)} slice(f32[768,16,128]{2,1,0:T(8,128)} %bitcast.32), slice={[0:512], [0:16], [0:128]} | slice | bytes 8388608 | tf_op jit(solution)/shard_map/slice | solution.py:373
  4.5 5.9 %all-to-all-start = ((f32[512,16,128]{2,1,0:T(8,128)}), f32[512,16,128]{2,1,0:T(8,128)}, u32[]{:S(2)}, u32[]{:S(2)}) async-start(f32[512,16,128]{2,1,0:T(8,128)} %slice.36), calls=%async_computation | async-start | bytes 8388608 | tf_op jit(solution)/shard_map/all_to_all | solution.py:22
  10.4 2.9 %constant_dynamic-slice_fusion.5 = (f32[64,16,128]{2,1,0:T(8,128)}, f32[64,16,128]{2,1,0:T(8,128)}, f32[64,16,128]{2,1,0:T(8,128)}, f32[64,16,128]{2,1,0:T(8,128)}) fusion(f32[768,16,128]{2,1,0:T(8,128)} %bitcast.33, s32[]{:T(128)S(6)} %select_n.43, s32[]{:T(128)S(6)} %select_n.42, s32[]{:T(128)S(6)} %select_n.41, s32[]{:T(128)S(6)} %select_n.40), kind=kLoop, calls=%fused_computation.26 | loop fusion | bytes 4194320 | tf_op jit(solution)/shard_map/dynamic_slice | solution.py:377
  13.3 1.4 collective-permute-start.2
  14.7 2.4 %collective-permute-start.3 = (f32[64,16,128]{2,1,0:T(8,128)}, f32[64,16,128]{2,1,0:T(8,128)}, u32[]{:S(2)}, u32[]{:S(2)}) collective-permute-start(f32[64,16,128]{2,1,0:T(8,128)} %get-tuple-element.42), channel_id=1, source_target_pairs={{0,4},{1,5},{2,6},{3,7},{4,0},{5,1},{6,2},{7,3},{8,12},{9,13},{10,... | collective-permute-start | bytes 1572872 | tf_op jit(solution)/shard_map/ppermute | solution.py:350
  17.1 0.0 collective-permute-start.4
  17.2 0.0 copy-done.8
  17.2 0.1 compare_convert_fusion
  17.3 0.0 copy-start.17
  17.3 0.0 copy-start.12
  17.3 5.2 %slice_multiply_fusion = (f32[1,384,16,128]{3,2,1,0:T(8,128)}, f32[1,384,16,128]{3,2,1,0:T(8,128)}) fusion(f32[2,384,16,128]{3,2,1,0:T(8,128)} %param.11, f32[384]{0:T(512)S(1)} %get-tuple-element.37, f32[384]{0:T(512)S(1)} %get-tuple-element.38), kind=kLoop, calls=%fused_computation | loop fusion | flops 1572864 | bytes 12585984 | tf_op jit(solution)/shard_map/mul | solution.py:384
  22.5 1.3 collective-permute-start
  23.8 5.6 %collective-permute-start.1 = (f32[1,384,16,128]{3,2,1,0:T(8,128)}, f32[1,384,16,128]{3,2,1,0:T(8,128)}, u32[]{:S(2)}, u32[]{:S(2)}) collective-permute-start(f32[1,384,16,128]{3,2,1,0:T(8,128)} %get-tuple-element.39), channel_id=1, source_target_pairs={{0,8},{8,16},{16,24},{24,32},{32,40},{40,48},{48,56},{56,64},{64,7... | collective-permute-start | bytes 9437192 | tf_op jit(solution)/shard_map/ppermute | solution.py:18
  29.5 0.1 copy.14
  29.5 0.0 copy-done
  29.6 0.1 broadcast_in_dim.2.factor_ref
  29.7 2.2 %copy-done.10 = f32[512,16,128]{2,1,0:T(8,128)S(1)} copy-done((f32[512,16,128]{2,1,0:T(8,128)S(1)}, f32[512,16,128]{2,1,0:T(8,128)}, u32[]{:S(2)}) %copy-start.10) | copy-done | bytes 4194328
  31.9 1.4 copy-done.11
  33.3 20.7 %local_terms.2.below_ref = f32[1,6144,128]{2,1,0:T(8,128)S(1)} custom-call(s32[2]{0:T(128)S(1)} %copy-done.8, f32[2,384]{1,0:T(2,128)S(1)} %copy-done.12, f32[2,6144,128]{2,1,0:T(8,128)} %bitcast.34, f32[2,6144,128]{2,1,0:T(8,128)} %bitcast.45, f32[8192,128]{1,0:T(8,128)S(1)} %bitcast.39, f32[2,512,384]{2,1,0:T(8,128)S(1)} %copy-done.11, ...), custom_call_target="tpu_custom_call" | custom-call | flops 8000000000 | bytes 16000000 | tf_op jit(solution)/shard_map/local_terms/pallas_call | solution.py:103
  54.0 1.7 copy-done.3
  55.7 20.8 %local_terms.3.above_ref = f32[1,6144,128]{2,1,0:T(8,128)S(1)} custom-call(s32[2]{0:T(128)S(1)} %copy-done.8, f32[2,384]{1,0:T(2,128)S(1)} %copy-done.12, f32[2,6144,128]{2,1,0:T(8,128)} %bitcast.35, f32[2,6144,128]{2,1,0:T(8,128)} %bitcast.46, f32[8192,128]{1,0:T(8,128)S(1)} %bitcast.40, f32[2,512,384]{2,1,0:T(8,128)S(1)} %copy-done.11, ...), custom_call_target="tpu_custom_call" | custom-call | flops 8000000000 | bytes 16000000 | tf_op jit(solution)/shard_map/local_terms/pallas_call | solution.py:103
  76.5 1.6 copy-done.5
  78.1 0.0 copy-done.16
  78.1 0.7 maximum_maximum_fusion.1.matrix_ref
  78.8 0.0 all-to-all-done
  78.8 7.6 %radial_apply.1 = f32[8,64,16,128]{3,2,1,0:T(8,128)} custom-call(bf16[256,256]{1,0:T(8,128)(2,1)} %maximum_maximum_fusion.1.matrix_ref, f32[8,64,16,128]{3,2,1,0:T(8,128)} %bitcast.7.x_ref), custom_call_target="tpu_custom_call" | custom-call | flops 1280000000 | bytes 8388608 | tf_op jit(solution)/shard_map/radial_apply/pallas_call | solution.py:146
  86.3 0.0 collective-permute-done.2
  86.3 0.0 collective-permute-done.3
  86.3 0.0 collective-permute-done.4
  86.4 6.0 %all-to-all-start.1 = ((f32[512,16,128]{2,1,0:T(8,128)}), f32[512,16,128]{2,1,0:T(8,128)}, u32[]{:S(2)}, u32[]{:S(2)}) async-start(f32[512,16,128]{2,1,0:T(8,128)} %bitcast.42), calls=%async_computation.1 | async-start | bytes 8388608 | tf_op jit(solution)/shard_map/all_to_all | solution.py:22
  92.4 1.1 constant_dynamic-slice_fusion.2
  93.5 1.1 constant_dynamic-slice_fusion
  94.5 0.1 pad_maximum_fusion
  94.6 0.2 collective-permute-start.5
  94.8 0.6 pad_add_fusion.where_ref.where
  95.5 0.0 collective-permute-done
  95.5 0.0 collective-permute-done.1
  95.5 2.0 %collective-permute-done.5.refs_4_ = f32[4,32,16,128]{3,2,1,0:T(8,128)} collective-permute-done((f32[4,32,16,128]{3,2,1,0:T(8,128)S(1)}, f32[4,32,16,128]{3,2,1,0:T(8,128)}, u32[]{:S(2)}, u32[]{:S(2)}) %collective-permute-start.5) | collective-permute-done | bytes 1048608 | tf_op jit(solution)/shard_map/ppermute | solution.py:350
  97.5 5.4 %radial_apart.1 = (f32[32,16,128]{2,1,0:T(8,128)}, f32[32,16,128]{2,1,0:T(8,128)}, f32[32,16,128]{2,1,0:T(8,128)}, f32[32,16,128]{2,1,0:T(8,128)}, f32[4,32,16,128]{3,2,1,0:T(8,128)}) custom-call(s32[2]{0:T(128)} %pad_add_fusion.where_ref.where, bf16[256,256]{1,0:T(8,128)(2,1)} %maximum_maximum_fusion.1.matrix_ref, f32[2,32,16,128]{3,2,1,0:T(8,128)} %bitcast.44, ...), custom_call_target="tpu_custom_call" | custom-call | flops 640000000 | bytes 4194304 | tf_op jit(solution)/shard_map/radial_apart/pallas_call | solution.py:200
  102.9 0.2 collective-permute-start.6
  103.1 2.7 %collective-permute-done.6 = f32[4,32,16,128]{3,2,1,0:T(8,128)S(1)} collective-permute-done((f32[4,32,16,128]{3,2,1,0:T(8,128)}, f32[4,32,16,128]{3,2,1,0:T(8,128)S(1)}, u32[]{:S(2)}, u32[]{:S(2)}) %collective-permute-start.6) | collective-permute-done | bytes 1048608 | tf_op jit(solution)/shard_map/ppermute | solution.py:350
  105.9 0.1 slice_bitcast_fusion
  105.9 1.8 %pad_maximum_fusion.4 = f32[64,16,128]{2,1,0:T(8,128)} fusion(f32[32,16,128]{2,1,0:T(8,128)S(1)} %get-tuple-element.45, f32[32,16,128]{2,1,0:T(8,128)} %get-tuple-element.35), kind=kLoop, calls=%fused_computation.6 | loop fusion | flops 131072 | bytes 1048576 | tf_op jit(solution)/shard_map/concatenate | solution.py:421
  107.8 2.6 %collective-permute-start.9 = (f32[64,16,128]{2,1,0:T(8,128)}, f32[64,16,128]{2,1,0:T(8,128)}, u32[]{:S(2)}, u32[]{:S(2)}) collective-permute-start(f32[64,16,128]{2,1,0:T(8,128)} %pad_maximum_fusion.4), channel_id=1, source_target_pairs={{0,6},{1,7},{2,4},{3,5},{4,2},{5,3},{6,0},{7,1},{8,14},{9,15},{10,... | collective-permute-start | bytes 1572872 | tf_op jit(solution)/shard_map/ppermute | solution.py:350
  110.4 0.8 pad_maximum_fusion.3
  111.2 0.6 collective-permute-start.8
  111.8 0.8 pad_maximum_fusion.2
  112.6 0.1 collective-permute-start.7
  112.7 0.7 constant_dynamic-slice_fusion.10
  113.4 0.7 constant_dynamic-slice_fusion.9
  114.1 1.8 %pad_maximum_fusion.1 = f32[64,16,128]{2,1,0:T(8,128)} fusion(f32[32,16,128]{2,1,0:T(8,128)S(1)} %get-tuple-element.48, f32[32,16,128]{2,1,0:T(8,128)} %get-tuple-element.31), kind=kLoop, calls=%fused_computation.3 | loop fusion | flops 131072 | bytes 1048576 | tf_op jit(solution)/shard_map/concatenate | solution.py:421
  115.9 2.8 %copy-done.2 = f32[2,384,16,128]{3,2,1,0:T(8,128)S(1)} copy-done((f32[2,384,16,128]{3,2,1,0:T(8,128)S(1)}, f32[2,384,16,128]{3,2,1,0:T(8,128)}, u32[]{:S(2)}) %copy-start.2) | copy-done | bytes 6291480
  118.7 1.9 %copy-done.4 = f32[1,6144,128]{2,1,0:T(8,128)S(1)} copy-done((f32[1,6144,128]{2,1,0:T(8,128)S(1)}, f32[1,6144,128]{2,1,0:T(8,128)}, u32[]{:S(2)}) %copy-start.4) | copy-done | bytes 3145752
  120.6 1.9 %copy-done.6 = f32[1,6144,128]{2,1,0:T(8,128)S(1)} copy-done((f32[1,6144,128]{2,1,0:T(8,128)S(1)}, f32[1,6144,128]{2,1,0:T(8,128)}, u32[]{:S(2)}) %copy-start.6) | copy-done | bytes 3145752
  122.5 8.4 %middle_terms.1 = f32[2,6144,128]{2,1,0:T(8,128)} custom-call(s32[2]{0:T(128)S(1)} %copy-done.8, f32[3,384]{1,0:T(4,128)S(1)} %pad_maximum_fusion.5.coriolis, f32[1,6144,128]{2,1,0:T(8,128)S(1)} %copy-done.4, f32[1,6144,128]{2,1,0:T(8,128)S(1)} %copy-done.6, f32[2,6144,128]{2,1,0:T(8,128)S(1)} %bitcast.36, f32[6144,128]{1,0:T(8,128)} %bitcast.16.lower_ref, ...), custom_call_target="tpu_custom_call" | custom-call | flops 30000000 | bytes 25000000 | tf_op jit(solution)/shard_map/middle_terms/pallas_call | solution.py:250
  130.9 10.5 %all-to-all-done.1 = f32[512,16,128]{2,1,0:T(8,128)} async-done(((f32[512,16,128]{2,1,0:T(8,128)}), f32[512,16,128]{2,1,0:T(8,128)}, u32[]{:S(2)}, u32[]{:S(2)}) %all-to-all-start.1) | async-done | bytes 4194336 | tf_op jit(solution)/shard_map/all_to_all | solution.py:22
  141.4 6.2 %add_joined.1.out_in = f32[12288,128]{1,0:T(8,128)} custom-call(s32[2]{0:T(128)S(1)} %copy-done.8, f32[12288,128]{1,0:T(8,128)} %bitcast.41, f32[8192,128]{1,0:T(8,128)} %bitcast.20.back_ref, f32[16,128]{1,0:T(8,128)S(1)} %broadcast_in_dim.2.factor_ref), custom_call_target="tpu_custom_call", output_to_operand_aliasing={{}: (1, {})} | custom-call | flops 1000000 | bytes 12582912 | tf_op jit(solution)/shard_map/add_joined/pallas_call | solution.py:330
  147.5 16.1 %collective-permute-done.9 = f32[64,16,128]{2,1,0:T(8,128)} collective-permute-done((f32[64,16,128]{2,1,0:T(8,128)}, f32[64,16,128]{2,1,0:T(8,128)}, u32[]{:S(2)}, u32[]{:S(2)}) %collective-permute-start.9) | collective-permute-done | bytes 524320 | tf_op jit(solution)/shard_map/ppermute | solution.py:350
  163.7 0.0 collective-permute-done.8
  163.7 0.0 collective-permute-done.7
  163.7 0.0 copy-done.7
  163.7 0.0 copy-start.1
  163.7 5.1 %add_apart.1 = f32[12288,128]{1,0:T(8,128)} custom-call(s32[2]{0:T(128)S(1)} %copy-done.9, s32[2]{0:T(128)S(1)} %copy-done.8, f32[12288,128]{1,0:T(8,128)} %add_joined.1.out_in, f32[16,128]{1,0:T(8,128)S(1)} %broadcast_in_dim.2.factor_ref, f32[1024,128]{1,0:T(8,128)S(1)} %bitcast.38, f32[1024,128]{1,0:T(8,128)} %bitcast.22.refs_1_, ...), custom_call_target="tpu_custom_call", output_to_operand_aliasing={{}: (2, {})} | custom-call | flops 1000000 | bytes 6291456 | tf_op jit(solution)/shard_map/add_apart/pallas_call | solution.py:297
  (27 shorter events, 0.1 us)
Async XLA Ops:
  0.0 29.6 %copy-start = (f32[128,128]{1,0:T(8,128)S(1)}, f32[128,128]{1,0:T(8,128)}, u32[]{:S(2)}) copy-start(f32[128,128]{1,0:T(8,128)} %param.16) | copy-start | bytes 196612
  4.5 74.3 %all-to-all-start = ((f32[512,16,128]{2,1,0:T(8,128)}), f32[512,16,128]{2,1,0:T(8,128)}, u32[]{:S(2)}, u32[]{:S(2)}) async-start(f32[512,16,128]{2,1,0:T(8,128)} %slice.36), calls=%async_computation | async-start | bytes 8388608 | tf_op jit(solution)/shard_map/all_to_all | solution.py:22
  10.4 6.8 %copy-start.8 = (s32[2]{0:T(128)S(1)}, s32[2]{0:T(128)}, u32[]{:S(2)}) copy-start(s32[2]{0:T(128)} %sizes.9) | copy-start | bytes 28
  13.3 73.0 %collective-permute-start.2 = (f32[64,16,128]{2,1,0:T(8,128)}, f32[64,16,128]{2,1,0:T(8,128)}, u32[]{:S(2)}, u32[]{:S(2)}) collective-permute-start(f32[64,16,128]{2,1,0:T(8,128)} %get-tuple-element.43), channel_id=1, source_target_pairs={{0,2},{1,3},{2,0},{3,1},{4,6},{5,7},{6,4},{7,5},{8,10},{9,11},{10,... | collective-permute-start | bytes 1572872 | tf_op jit(solution)/shard_map/ppermute | solution.py:350
  14.7 71.6 %collective-permute-start.3 = (f32[64,16,128]{2,1,0:T(8,128)}, f32[64,16,128]{2,1,0:T(8,128)}, u32[]{:S(2)}, u32[]{:S(2)}) collective-permute-start(f32[64,16,128]{2,1,0:T(8,128)} %get-tuple-element.42), channel_id=1, source_target_pairs={{0,4},{1,5},{2,6},{3,7},{4,0},{5,1},{6,2},{7,3},{8,12},{9,13},{10,... | collective-permute-start | bytes 1572872 | tf_op jit(solution)/shard_map/ppermute | solution.py:350
  17.1 69.2 %collective-permute-start.4 = (f32[64,16,128]{2,1,0:T(8,128)}, f32[64,16,128]{2,1,0:T(8,128)}, u32[]{:S(2)}, u32[]{:S(2)}) collective-permute-start(f32[64,16,128]{2,1,0:T(8,128)} %get-tuple-element.41), channel_id=1, source_target_pairs={{0,6},{1,7},{2,4},{3,5},{4,2},{5,3},{6,0},{7,1},{8,14},{9,15},{10,... | collective-permute-start | bytes 1572872 | tf_op jit(solution)/shard_map/ppermute | solution.py:350
  17.3 12.2 %copy-start.15 = (f32[128,128]{1,0:T(8,128)S(1)}, f32[128,128]{1,0:T(8,128)}, u32[]{:S(2)}) copy-start(f32[128,128]{1,0:T(8,128)} %param.19) | copy-start | bytes 196612
  17.3 12.3 %copy-start.17 = (f32[16]{0:T(128)S(1)}, f32[16]{0:T(128)}, u32[]{:S(2)}) copy-start(f32[16]{0:T(128)} %param.17) | copy-start | bytes 196
  17.3 12.4 %copy-start.12 = (f32[2,384]{1,0:T(2,128)S(1)}, f32[2,384]{1,0:T(2,128)}, u32[]{:S(2)}) copy-start(f32[2,384]{1,0:T(2,128)} %centrifugal.3) | copy-start | bytes 9220
  22.5 72.9 %collective-permute-start = (f32[1,384,16,128]{3,2,1,0:T(8,128)}, f32[1,384,16,128]{3,2,1,0:T(8,128)S(1)}, u32[]{:S(2)}, u32[]{:S(2)}) collective-permute-start(f32[1,384,16,128]{3,2,1,0:T(8,128)} %get-tuple-element.40), channel_id=1, source_target_pairs={{8,0},{16,8},{24,16},{32,24},{40,32},{48,40},{56,48},{64,56},{72,6... | collective-permute-start | bytes 9437192 | tf_op jit(solution)/shard_map/ppermute | solution.py:18
  23.8 71.6 %collective-permute-start.1 = (f32[1,384,16,128]{3,2,1,0:T(8,128)}, f32[1,384,16,128]{3,2,1,0:T(8,128)}, u32[]{:S(2)}, u32[]{:S(2)}) collective-permute-start(f32[1,384,16,128]{3,2,1,0:T(8,128)} %get-tuple-element.39), channel_id=1, source_target_pairs={{0,8},{8,16},{16,24},{24,32},{32,40},{40,48},{48,56},{56,64},{64,7... | collective-permute-start | bytes 9437192 | tf_op jit(solution)/shard_map/ppermute | solution.py:18
  29.7 2.2 %copy-start.10 = (f32[512,16,128]{2,1,0:T(8,128)S(1)}, f32[512,16,128]{2,1,0:T(8,128)}, u32[]{:S(2)}) copy-start(f32[512,16,128]{2,1,0:T(8,128)} %param.21) | copy-start | bytes 12582916
  31.9 1.4 copy-start.11
  54.0 1.7 copy-start.3
  55.7 22.4 %copy-start.16 = (f32[128,128]{1,0:T(8,128)S(1)}, f32[128,128]{1,0:T(8,128)}, u32[]{:S(2)}) copy-start(f32[128,128]{1,0:T(8,128)} %param.18) | copy-start | bytes 196612
  76.4 1.6 copy-start.5
  86.4 55.0 %all-to-all-start.1 = ((f32[512,16,128]{2,1,0:T(8,128)}), f32[512,16,128]{2,1,0:T(8,128)}, u32[]{:S(2)}, u32[]{:S(2)}) async-start(f32[512,16,128]{2,1,0:T(8,128)} %bitcast.42), calls=%async_computation.1 | async-start | bytes 8388608 | tf_op jit(solution)/shard_map/all_to_all | solution.py:22
  94.6 2.9 %collective-permute-start.5 = (f32[4,32,16,128]{3,2,1,0:T(8,128)S(1)}, f32[4,32,16,128]{3,2,1,0:T(8,128)}, u32[]{:S(2)}, u32[]{:S(2)}) collective-permute-start(f32[4,32,16,128]{3,2,1,0:T(8,128)S(1)} %pad_maximum_fusion), channel_id=1, source_target_pairs={{0,1},{1,0},{2,3},{3,2},{4,5},{5,4},{6,7},{7,6},{8,9},{9,8},{10,11... | collective-permute-start | bytes 3145736 | tf_op jit(solution)/shard_map/ppermute | solution.py:350
  102.9 7.5 %copy-start.14 = (f32[32,16,128]{2,1,0:T(8,128)S(1)}, f32[32,16,128]{2,1,0:T(8,128)}, u32[]{:S(2)}) copy-start(f32[32,16,128]{2,1,0:T(8,128)} %get-tuple-element.34) | copy-start | bytes 786436
  102.9 8.9 %copy-start.13 = (f32[32,16,128]{2,1,0:T(8,128)S(1)}, f32[32,16,128]{2,1,0:T(8,128)}, u32[]{:S(2)}) copy-start(f32[32,16,128]{2,1,0:T(8,128)} %get-tuple-element.33) | copy-start | bytes 786436
  102.9 3.0 %collective-permute-start.6 = (f32[4,32,16,128]{3,2,1,0:T(8,128)}, f32[4,32,16,128]{3,2,1,0:T(8,128)S(1)}, u32[]{:S(2)}, u32[]{:S(2)}) collective-permute-start(f32[4,32,16,128]{3,2,1,0:T(8,128)} %get-tuple-element.32), channel_id=1, source_target_pairs={{0,1},{1,0},{2,3},{3,2},{4,5},{5,4},{6,7},{7,6},{8,9},{9,8},{10,11... | collective-permute-start | bytes 3145736 | tf_op jit(solution)/shard_map/ppermute | solution.py:350
  107.8 55.9 %collective-permute-start.9 = (f32[64,16,128]{2,1,0:T(8,128)}, f32[64,16,128]{2,1,0:T(8,128)}, u32[]{:S(2)}, u32[]{:S(2)}) collective-permute-start(f32[64,16,128]{2,1,0:T(8,128)} %pad_maximum_fusion.4), channel_id=1, source_target_pairs={{0,6},{1,7},{2,4},{3,5},{4,2},{5,3},{6,0},{7,1},{8,14},{9,15},{10,... | collective-permute-start | bytes 1572872 | tf_op jit(solution)/shard_map/ppermute | solution.py:350
  111.2 52.5 %collective-permute-start.8 = (f32[64,16,128]{2,1,0:T(8,128)}, f32[64,16,128]{2,1,0:T(8,128)}, u32[]{:S(2)}, u32[]{:S(2)}) collective-permute-start(f32[64,16,128]{2,1,0:T(8,128)} %pad_maximum_fusion.3), channel_id=1, source_target_pairs={{0,4},{1,5},{2,6},{3,7},{4,0},{5,1},{6,2},{7,3},{8,12},{9,13},{10,... | collective-permute-start | bytes 1572872 | tf_op jit(solution)/shard_map/ppermute | solution.py:350
  112.6 51.1 %collective-permute-start.7 = (f32[64,16,128]{2,1,0:T(8,128)}, f32[64,16,128]{2,1,0:T(8,128)}, u32[]{:S(2)}, u32[]{:S(2)}) collective-permute-start(f32[64,16,128]{2,1,0:T(8,128)} %pad_maximum_fusion.2), channel_id=1, source_target_pairs={{0,2},{1,3},{2,0},{3,1},{4,6},{5,7},{6,4},{7,5},{8,10},{9,11},{10,... | collective-permute-start | bytes 1572872 | tf_op jit(solution)/shard_map/ppermute | solution.py:350
  115.9 2.8 %copy-start.2 = (f32[2,384,16,128]{3,2,1,0:T(8,128)S(1)}, f32[2,384,16,128]{3,2,1,0:T(8,128)}, u32[]{:S(2)}) copy-start(f32[2,384,16,128]{3,2,1,0:T(8,128)} %param.11) | copy-start | bytes 18874372
  118.7 1.9 %copy-start.4 = (f32[1,6144,128]{2,1,0:T(8,128)S(1)}, f32[1,6144,128]{2,1,0:T(8,128)}, u32[]{:S(2)}) copy-start(f32[1,6144,128]{2,1,0:T(8,128)} %copy-done.3) | copy-start | bytes 9437188
  120.6 1.9 %copy-start.6 = (f32[1,6144,128]{2,1,0:T(8,128)S(1)}, f32[1,6144,128]{2,1,0:T(8,128)}, u32[]{:S(2)}) copy-start(f32[1,6144,128]{2,1,0:T(8,128)} %copy-done.5) | copy-start | bytes 9437188
  141.4 22.3 %copy-start.7 = (f32[64,16,128]{2,1,0:T(8,128)S(1)}, f32[64,16,128]{2,1,0:T(8,128)}, u32[]{:S(2)}) copy-start(f32[64,16,128]{2,1,0:T(8,128)} %pad_maximum_fusion.1) | copy-start | bytes 1572868
  141.4 22.3 %copy-start.9 = (s32[2]{0:T(128)S(1)}, s32[2]{0:T(128)}, u32[]{:S(2)}) copy-start(s32[2]{0:T(128)} %pad_add_fusion.where_ref.where) | copy-start | bytes 28
  163.7 5.1 %copy-start.1 = (f32[128,128]{1,0:T(8,128)S(1)}, f32[128,128]{1,0:T(8,128)}, u32[]{:S(2)}) copy-start(f32[128,128]{1,0:T(8,128)} %param.16) | copy-start | bytes 196612

commit v2 on v1

--- a/solution.py
+++ b/solution.py
@@ -10,6 +10,7 @@
 F32 = jnp.float32
 BF16 = jnp.bfloat16
 MIB = 1 << 20
+BRIEF = pl.CostEstimate(flops=1_000_000, bytes_accessed=100_000, transcendentals=0)
 
 
 def from_behind(x, axis, by):
@@ -30,6 +31,42 @@
 def halves_outside(x):
     high = lax.reduce_precision(x, 8, 7)
     return high.astype(BF16), (x - high).astype(BF16)
+
+
+def leading_kernel(x_ref, out_ref, held, come, go):
+    parts, size = held.shape[:2]
+    into = [
+        pltpu.make_async_copy(x_ref.at[pl.ds(i * size, size)], held.at[i], come.at[i])
+        for i in range(parts)
+    ]
+    onward = [
+        pltpu.make_async_copy(held.at[i], out_ref.at[pl.ds(i * size, size)], go.at[i])
+        for i in range(parts)
+    ]
+    for copy in into:
+        copy.start()
+    for i in range(parts):
+        into[i].wait()
+        onward[i].start()
+    for copy in onward:
+        copy.wait()
+
+
+def leading(x, count):
+    parts = 8
+    return pl.pallas_call(
+        leading_kernel,
+        in_specs=[pl.BlockSpec(memory_space=pl.ANY)],
+        out_specs=pl.BlockSpec(memory_space=pl.ANY),
+        out_shape=jax.ShapeDtypeStruct((count, *x.shape[1:]), F32),
+        scratch_shapes=[
+            pltpu.VMEM((parts, count // parts, *x.shape[1:]), F32),
+            pltpu.SemaphoreType.DMA((parts,)),
+            pltpu.SemaphoreType.DMA((parts,)),
+        ],
+        cost_estimate=BRIEF,
+        name="leading",
+    )(x)
 
 
 def local_kernel(
@@ -116,9 +153,7 @@
             pltpu.VMEM((basis, 3 * angles), BF16),
         ],
         compiler_params=pltpu.CompilerParams(vmem_limit_bytes=40 * MIB),
-        cost_estimate=pl.CostEstimate(
-            flops=8_000_000_000, bytes_accessed=16_000_000, transcendentals=0
-        ),
+        cost_estimate=BRIEF,
         name="local_terms",
     )(sizes, centrifugal, x, previous, potential, legendre, stretch, inertia, factor)
 
@@ -149,9 +184,7 @@
         in_specs=[pl.BlockSpec(matrix.shape, lambda i: (0, 0)), some],
         out_specs=some,
         out_shape=jax.ShapeDtypeStruct(received.shape, F32),
-        cost_estimate=pl.CostEstimate(
-            flops=columns * 20_000_000, bytes_accessed=2 * 4 * received.size, transcendentals=0
-        ),
+        cost_estimate=BRIEF,
         name="radial_apply",
     )(matrix, received)
 
@@ -209,54 +242,69 @@
         ),
         out_shape=[jax.ShapeDtypeStruct(theirs.shape[1:], F32)] * chips
         + [jax.ShapeDtypeStruct(theirs.shape, F32)],
-        cost_estimate=pl.CostEstimate(
-            flops=columns * 20_000_000, bytes_accessed=16 * theirs.size, transcendentals=0
-        ),
+        cost_estimate=BRIEF,
         name="radial_apart",
     )(where, matrix, *ours, theirs)
 
 
 def middle_kernel(
-    sizes, coriolis, below_ref, above_ref, x_ref, lower_ref, upper_ref, inertia_ref, factor_ref, out_ref
+    sizes, coriolis, below_ref, above_ref, x_ref, lower_ref, upper_ref, first_ref, second_ref,
+    inertia_ref, factor_ref, out_ref
 ):
     step = pl.program_id(0)
     radial = inertia_ref.shape[0]
     count = x_ref.shape[1] // radial
-    both = 2.0 * factor_ref[...] * inertia_ref[...]
+    double = 2.0 * factor_ref[...]
+    inertia = inertia_ref[...]
     below, above = sizes[0], sizes[1]
 
-    @pl.loop(0, count // 4)
-    def _(i):
-        for k in range(4):
-            local = i * 4 + k
-            j = step * count + local
-            at = pl.ds(pl.multiple_of(local * radial, radial), radial)
-            here = jnp.where(j < below, x_ref[0, at, :], 0.0)
-            there = jnp.where(j < above, x_ref[1, at, :], 0.0)
-            low = coriolis[1, j] * there + coriolis[0, j] * lower_ref[at, :]
-            high = coriolis[2, j] * upper_ref[at, :] + coriolis[1, j] * here
-            out_ref[0, at, :] = below_ref[0, at, :] + jnp.where(j < below, both * low, 0.0)
-            out_ref[1, at, :] = above_ref[0, at, :] + jnp.where(j < above, both * high, 0.0)
-
-
-def middle_terms(sizes, coriolis, below, above, x, lower, upper, inertia, factor):
+    def part(more):
+        @pl.loop(0, count // 4)
+        def _(i):
+            for k in range(4):
+                local = i * 4 + k
+                j = step * count + local
+                at = pl.ds(pl.multiple_of(local * radial, radial), radial)
+                here = jnp.where(j < below, x_ref[0, at, :], 0.0)
+                there = jnp.where(j < above, x_ref[1, at, :], 0.0)
+                low = coriolis[1, j] * there + coriolis[0, j] * lower_ref[at, :]
+                high = coriolis[2, j] * upper_ref[at, :] + coriolis[1, j] * here
+                low = double * (inertia * low + first_ref[at, :])
+                high = inertia * high
+                if more:
+                    high = high + second_ref[at, :]
+                high = double * high
+                out_ref[0, at, :] = below_ref[0, at, :] + jnp.where(j < below, low, 0.0)
+                out_ref[1, at, :] = above_ref[0, at, :] + jnp.where(j < above, high, 0.0)
+
+    pl.when(step < SECOND_PARTS)(lambda: part(True))
+    pl.when(step >= SECOND_PARTS)(lambda: part(False))
+
+
+MIDDLE_PARTS = 12
+SECOND_PARTS = 4
+
+
+def middle_terms(sizes, coriolis, below, above, x, lower, upper, back, inertia, factor):
     blocks, rows, width = x.shape
-    parts = 8
+    size = rows // MIDDLE_PARTS
+    assert back.shape[0] == rows + size * SECOND_PARTS
     smem = pl.BlockSpec(memory_space=pltpu.SMEM)
-    pair = pl.BlockSpec((blocks, rows // parts, width), lambda i: (0, i, 0))
-    single = pl.BlockSpec((1, rows // parts, width), lambda i: (0, i, 0))
-    one = pl.BlockSpec((rows // parts, width), lambda i: (i, 0))
+    pair = pl.BlockSpec((blocks, size, width), lambda i: (0, i, 0))
+    single = pl.BlockSpec((1, size, width), lambda i: (0, i, 0))
+    one = pl.BlockSpec((size, width), lambda i: (i, 0))
+    second = pl.BlockSpec((size, width), lambda i: (MIDDLE_PARTS + jnp.minimum(i, SECOND_PARTS - 1), 0))
     small = pl.BlockSpec(inertia.shape, lambda i: (0, 0))
     return pl.pallas_call(
         middle_kernel,
-        grid=(parts,),
-        in_specs=[smem, smem, single, single, pair, one, one, small, small],
+        grid=(MIDDLE_PARTS,),
+        in_specs=[smem, smem, single, single, pair, one, one, one, second, small, small],
         out_specs=pair,
         out_shape=jax.ShapeDtypeStruct(x.shape, F32),
         compiler_params=pltpu.CompilerParams(vmem_limit_bytes=20 * MIB),
-        cost_estimate=pl.CostEstimate(flops=30_000_000, bytes_accessed=25_000_000, transcendentals=0),
+        cost_estimate=BRIEF,
         name="middle_terms",
-    )(sizes, coriolis, below, above, x, lower, upper, inertia, factor)
+    )(sizes, coriolis, below, above, x, lower, upper, back, back, inertia, factor)
 
 
 def add_rows(target, source, double, columns, begin, live):
@@ -305,44 +353,9 @@
         out_shape=jax.ShapeDtypeStruct(out.shape, F32),
         input_output_aliases={2: 0},
         compiler_params=pltpu.CompilerParams(vmem_limit_bytes=20 * MIB),
-        cost_estimate=pl.CostEstimate(
-            flops=1_000_000, bytes_accessed=12 * rows * width * len(backs), transcendentals=0
-        ),
+        cost_estimate=BRIEF,
         name="add_apart",
     )(where, sizes, out, factor, *backs)
-
-
-def add_joined_kernel(basis, sizes, out_in, back_ref, factor_ref, out_ref):
-    columns = out_in.shape[0] // factor_ref.shape[0]
-    begin = pl.program_id(0) * columns
-    live = jnp.where(begin < basis, sizes[0], sizes[1] + basis)
-
-    def target(at, more):
-        out_ref[at, :] = out_in[at, :] + more
-
-    add_rows(target, back_ref, 2.0 * factor_ref[...], columns, begin, live)
-
-
-def add_joined(basis, sizes, out, back, factor):
-    rows, width = back.shape
-    part = 128 * factor.shape[0]
-    some = pl.BlockSpec((part, width), lambda i: (i, 0))
-    return pl.pallas_call(
-        functools.partial(add_joined_kernel, basis),
-        grid=(rows // part,),
-        in_specs=[
-            pl.BlockSpec(memory_space=pltpu.SMEM), some, some,
-            pl.BlockSpec(factor.shape, lambda i: (0, 0)),
-        ],
-        out_specs=some,
-        out_shape=jax.ShapeDtypeStruct(out.shape, F32),
-        input_output_aliases={1: 0},
-        compiler_params=pltpu.CompilerParams(vmem_limit_bytes=20 * MIB),
-        cost_estimate=pl.CostEstimate(
-            flops=1_000_000, bytes_accessed=12 * rows * width, transcendentals=0
-        ),
-        name="add_joined",
-    )(sizes, out, back, factor)
 
 
 def swap(x, by):
@@ -370,7 +383,7 @@
     x_chip, core = row // 2, row % 2
 
     flat = packet.reshape(columns, radial, width)
-    sent_a = flat[:joined]
+    sent_a = leading(flat, joined)
     got_a = exchange(sent_a)
     source = after(flat, sent_a)
     sent = [
@@ -408,15 +421,15 @@
         )
 
     below = local(0, after(x, upper, lower))
-    above = local(1, after(x, below))
-    made_a = radial_apply(after(matrix, above), got_a.reshape(peers, joined // peers, radial, width))
+    made_a = radial_apply(after(matrix, below), got_a.reshape(peers, joined // peers, radial, width))
     back_a = exchange(made_a.reshape(joined, radial, width))
     ours = lax.optimization_barrier((made_a, *ours))[1:]
+    above = local(1, after(x, *ours))
     ours = [o.reshape(2, piece, radial, width) for o in ours]
     passed = [lax.dynamic_index_in_dim(o, 1 - core, 0) for o in ours]
     theirs = swap(jnp.concatenate(passed, 0), 1)
     where = jnp.stack([row, core]).astype(jnp.int32)
-    *made_b, passed = radial_apart(where, after(matrix, made_a, from_ahead, from_below), ours, theirs)
+    *made_b, passed = radial_apart(where, after(matrix, above, from_ahead, from_below), ours, theirs)
     passed = swap(passed, 1)
     joint = [jnp.concatenate([made_b[d], passed[d]], 0) for d in range(chips)]
     back_b = [joint[0]] + [swap(joint[d], 2 * d) for d in range(1, chips)]
@@ -424,10 +437,10 @@
     upper = from_ahead.reshape(rows, width)
     lower = from_below.reshape(rows, width)
     out = middle_terms(
-        basis_sizes, coupling, below, above, after(x, *joint), lower, upper, inertia_local, factor
+        basis_sizes, coupling, below, above, x, lower, upper,
+        back_a.reshape(joined * radial, width), inertia_local, factor,
     )
     out = out.reshape(columns * radial, width)
-    out = add_joined(basis, basis_sizes, out, back_a.reshape(joined * radial, width), factor)
     out = add_apart(
         basis, joined // (2 * piece), where, basis_sizes, out,
         [b.reshape(2 * piece * radial, width) for b in back_b], factor,

time: 170 us -> 155 us (0.912)
  waiting for transfers between devices: 31.4 us -> 22.1 us
  local copies, waits for them, and re-layouts: 24.8 us -> 18.2 us
    all_to_all x2, waiting for transfers between devices: 10.5 us -> 5.28 us  [exchange(): return lax.all_to_all(x, 'row', split_axis=0, concat_axis=0, tiled=True)]
    slice x1 -> x0, local copies, waits for them, and re-layouts: 4.5 us -> none  [shards(): sent_a = flat[:joined]]
    ppermute x8, waiting for transfers between devices: 20.9 us -> 16.8 us  [swap(): return lax.ppermute(x, 'row', [(i, i ^ by) for i in range(peers)])]
    unnamed x37, local copies, waits for them, and re-layouts: 13.6 us -> 11.6 us
  transfers between devices with their start and end apart: 12 -> 12, of which waited for: 4 -> 4; matrix products, arithmetic and copies ran while one was open for 11% -> 12% of each run, Pallas kernels for 41% -> 43%
where the time goes in v2:
time: 155 us; the launch traced here: 154 us
  Pallas kernels  74.8 us (48%)
  starting transfers between devices  26.6 us (17%)
  waiting for transfers between devices  22.1 us (14%)
  local copies, waits for them, and re-layouts  18.2 us (12%)
  other arithmetic  11.9 us (8%)
    pallas_call x2, Pallas kernels, local_terms(): pl.pallas_call(functools.partial(local_kernel, block), grid=(1,), in_spec...  41.5 us
    ppermute x8, waiting for transfers between devices, swap(): return lax.ppermute(x, 'row', [(i, i ^ by) for i in range(peers)])  16.8 us
    pallas_call x1, Pallas kernels, middle_terms(): pl.pallas_call(middle_kernel, grid=(MIDDLE_PARTS,), in_specs=[smem, smem,...  11.7 us
    all_to_all x2, starting transfers between devices, exchange(): return lax.all_to_all(x, 'row', split_axis=0, concat_axis=0, tiled=True)  11.6 us
    unnamed x37, local copies, waits for them, and re-layouts  11.6 us
    ppermute x8, starting transfers between devices, swap(): return lax.ppermute(x, 'row', [(i, i ^ by) for i in range(peers)])  8.79 us
    pallas_call x1, Pallas kernels, radial_apply(): pl.pallas_call(radial_kernel, grid=(columns // 8,), in_specs=[pl.BlockSpe...  7.54 us
    ppermute x2, starting transfers between devices, from_behind(): return lax.ppermute(x, axis, pairs)  6.22 us
  transfers between devices with their start and end apart: 12, of which 4 were waited for; matrix products, arithmetic and copies ran while one was open for 12% of the time, Pallas kernels for 43%

profile of v2, /device:TPU:1, one launch (start us, length us, event | category | flops | bytes accessed | tf_op | source)
XLA Modules:
  0.0 153.9 jit_solution(14300128449868876318)
XLA Ops:
  0.0 0.0 copy-start
  0.0 3.6 %leading.1 = f32[512,16,128]{2,1,0:T(8,128)} custom-call(f32[768,16,128]{2,1,0:T(8,128)} %bitcast.32), custom_call_target="tpu_custom_call" | custom-call | flops 1000000 | bytes 100000 | tf_op jit(solution)/shard_map/leading/pallas_call | solution.py:57
  3.6 5.8 %all-to-all-start = ((f32[512,16,128]{2,1,0:T(8,128)}), f32[512,16,128]{2,1,0:T(8,128)}, u32[]{:S(2)}, u32[]{:S(2)}) async-start(f32[512,16,128]{2,1,0:T(8,128)} %leading.1), calls=%async_computation | async-start | bytes 8388608 | tf_op jit(solution)/shard_map/all_to_all | solution.py:23
  9.5 2.9 %constant_dynamic-slice_fusion.5 = (f32[64,16,128]{2,1,0:T(8,128)}, f32[64,16,128]{2,1,0:T(8,128)}, f32[64,16,128]{2,1,0:T(8,128)}, f32[64,16,128]{2,1,0:T(8,128)}) fusion(f32[768,16,128]{2,1,0:T(8,128)} %bitcast.33, s32[]{:T(128)S(6)} %select_n.43, s32[]{:T(128)S(6)} %select_n.42, s32[]{:T(128)S(6)} %select_n.41, s32[]{:T(128)S(6)} %select_n.40), kind=kLoop, calls=%fused_computation.26 | loop fusion | bytes 4194320 | tf_op jit(solution)/shard_map/dynamic_slice | solution.py:390
  12.4 0.0 copy-done.10
  12.4 0.1 compare_convert_fusion
  12.5 0.0 copy-start.17
  12.5 0.0 copy-start.11
  12.5 5.2 %slice_multiply_fusion = (f32[1,384,16,128]{3,2,1,0:T(8,128)}, f32[1,384,16,128]{3,2,1,0:T(8,128)}) fusion(f32[2,384,16,128]{3,2,1,0:T(8,128)} %param.11, f32[384]{0:T(512)S(1)} %get-tuple-element.35, f32[384]{0:T(512)S(1)} %get-tuple-element.36), kind=kLoop, calls=%fused_computation | loop fusion | flops 1572864 | bytes 12585984 | tf_op jit(solution)/shard_map/mul | solution.py:397
  17.7 4.9 %collective-permute-start.3 = (f32[1,384,16,128]{3,2,1,0:T(8,128)}, f32[1,384,16,128]{3,2,1,0:T(8,128)}, u32[]{:S(2)}, u32[]{:S(2)}) collective-permute-start(f32[1,384,16,128]{3,2,1,0:T(8,128)} %get-tuple-element.37), channel_id=1, source_target_pairs={{0,8},{8,16},{16,24},{24,32},{32,40},{40,48},{48,56},{56,64},{64,7... | collective-permute-start | bytes 9437192 | tf_op jit(solution)/shard_map/ppermute | solution.py:19
  22.6 1.3 collective-permute-start.4
  23.9 1.5 collective-permute-start
  25.4 2.4 %collective-permute-start.1 = (f32[64,16,128]{2,1,0:T(8,128)}, f32[64,16,128]{2,1,0:T(8,128)}, u32[]{:S(2)}, u32[]{:S(2)}) collective-permute-start(f32[64,16,128]{2,1,0:T(8,128)} %get-tuple-element.40), channel_id=1, source_target_pairs={{0,4},{1,5},{2,6},{3,7},{4,0},{5,1},{6,2},{7,3},{8,12},{9,13},{10,... | collective-permute-start | bytes 1572872 | tf_op jit(solution)/shard_map/ppermute | solution.py:363
  27.8 0.1 collective-permute-start.2
  27.9 0.0 copy-done.15
  27.9 0.1 copy.13
  28.0 0.0 copy-done
  28.1 0.1 broadcast_in_dim.2.factor_ref
  28.1 0.0 copy-done.11
  28.1 2.2 %copy-done.3 = f32[512,16,128]{2,1,0:T(8,128)S(1)} copy-done((f32[512,16,128]{2,1,0:T(8,128)S(1)}, f32[512,16,128]{2,1,0:T(8,128)}, u32[]{:S(2)}) %copy-start.3) | copy-done | bytes 4194328
  30.3 1.4 copy-done.7
  31.7 20.7 %local_terms.2.below_ref = f32[1,6144,128]{2,1,0:T(8,128)S(1)} custom-call(s32[2]{0:T(128)S(1)} %copy-done.10, f32[2,384]{1,0:T(2,128)S(1)} %copy-done.11, f32[2,6144,128]{2,1,0:T(8,128)} %bitcast.34, f32[2,6144,128]{2,1,0:T(8,128)} %bitcast.41, f32[8192,128]{1,0:T(8,128)S(1)} %bitcast.37, f32[2,512,384]{2,1,0:T(8,128)S(1)} %copy-done.7, ...), custom_call_target="tpu_custom_call" | custom-call | flops 1000000 | bytes 100000 | tf_op jit(solution)/shard_map/local_terms/pallas_call | solution.py:140
  52.5 0.7 maximum_maximum_fusion.1.matrix_ref
  53.2 5.3 %all-to-all-done = f32[512,16,128]{2,1,0:T(8,128)} async-done(((f32[512,16,128]{2,1,0:T(8,128)}), f32[512,16,128]{2,1,0:T(8,128)}, u32[]{:S(2)}, u32[]{:S(2)}) %all-to-all-start) | async-done | bytes 4194336 | tf_op jit(solution)/shard_map/all_to_all | solution.py:23
  58.4 7.5 %radial_apply.1 = f32[8,64,16,128]{3,2,1,0:T(8,128)} custom-call(bf16[256,256]{1,0:T(8,128)(2,1)} %maximum_maximum_fusion.1.matrix_ref, f32[8,64,16,128]{3,2,1,0:T(8,128)} %bitcast.7.x_ref), custom_call_target="tpu_custom_call" | custom-call | flops 1000000 | bytes 100000 | tf_op jit(solution)/shard_map/radial_apply/pallas_call | solution.py:181
  66.0 5.8 %all-to-all-start.1 = ((f32[512,16,128]{2,1,0:T(8,128)}), f32[512,16,128]{2,1,0:T(8,128)}, u32[]{:S(2)}, u32[]{:S(2)}) async-start(f32[512,16,128]{2,1,0:T(8,128)} %bitcast.43), calls=%async_computation.1 | async-start | bytes 8388608 | tf_op jit(solution)/shard_map/all_to_all | solution.py:23
  71.7 0.0 collective-permute-done
  71.7 9.2 %collective-permute-done.1 = f32[64,16,128]{2,1,0:T(8,128)} collective-permute-done((f32[64,16,128]{2,1,0:T(8,128)}, f32[64,16,128]{2,1,0:T(8,128)}, u32[]{:S(2)}, u32[]{:S(2)}) %collective-permute-start.1) | collective-permute-done | bytes 524320 | tf_op jit(solution)/shard_map/ppermute | solution.py:363
  81.0 0.0 collective-permute-done.2
  81.0 1.1 constant_dynamic-slice_fusion.2
  82.0 1.1 constant_dynamic-slice_fusion
  83.1 0.1 pad_maximum_fusion
  83.2 1.5 collective-permute-start.5
  84.7 0.6 pad_add_fusion.where_ref.where
  85.3 1.4 copy-done.8
  86.7 20.8 %local_terms.3.above_ref = f32[1,6144,128]{2,1,0:T(8,128)S(1)} custom-call(s32[2]{0:T(128)S(1)} %copy-done.10, f32[2,384]{1,0:T(2,128)S(1)} %copy-done.11, f32[2,6144,128]{2,1,0:T(8,128)} %bitcast.35, f32[2,6144,128]{2,1,0:T(8,128)} %bitcast.42, f32[8192,128]{1,0:T(8,128)S(1)} %bitcast.38, f32[2,512,384]{2,1,0:T(8,128)S(1)} %copy-done.8, ...), custom_call_target="tpu_custom_call" | custom-call | flops 1000000 | bytes 100000 | tf_op jit(solution)/shard_map/local_terms/pallas_call | solution.py:140
  107.4 1.8 %copy-done.5 = f32[1,6144,128]{2,1,0:T(8,128)} copy-done((f32[1,6144,128]{2,1,0:T(8,128)}, f32[1,6144,128]{2,1,0:T(8,128)S(1)}, u32[]{:S(2)}) %copy-start.5) | copy-done | bytes 3145752
  109.2 0.0 collective-permute-done.3
  109.2 0.0 collective-permute-done.4
  109.2 0.0 collective-permute-done.5.refs_4_
  109.2 5.4 %radial_apart.1 = (f32[32,16,128]{2,1,0:T(8,128)}, f32[32,16,128]{2,1,0:T(8,128)}, f32[32,16,128]{2,1,0:T(8,128)}, f32[32,16,128]{2,1,0:T(8,128)}, f32[4,32,16,128]{3,2,1,0:T(8,128)}) custom-call(s32[2]{0:T(128)} %pad_add_fusion.where_ref.where, bf16[256,256]{1,0:T(8,128)(2,1)} %maximum_maximum_fusion.1.matrix_ref, f32[2,32,16,128]{3,2,1,0:T(8,128)} %bitcast.45, ...), custom_call_target="tpu_custom_call" | custom-call | flops 1000000 | bytes 100000 | tf_op jit(solution)/shard_map/radial_apart/pallas_call | solution.py:233
  114.6 0.1 collective-permute-start.6
  114.7 2.9 %collective-permute-done.6 = f32[4,32,16,128]{3,2,1,0:T(8,128)S(1)} collective-permute-done((f32[4,32,16,128]{3,2,1,0:T(8,128)}, f32[4,32,16,128]{3,2,1,0:T(8,128)S(1)}, u32[]{:S(2)}, u32[]{:S(2)}) %collective-permute-start.6) | collective-permute-done | bytes 1048608 | tf_op jit(solution)/shard_map/ppermute | solution.py:363
  117.6 0.1 slice_bitcast_fusion
  117.7 1.8 %pad_maximum_fusion.4 = f32[64,16,128]{2,1,0:T(8,128)} fusion(f32[32,16,128]{2,1,0:T(8,128)S(1)} %get-tuple-element.43, f32[32,16,128]{2,1,0:T(8,128)} %get-tuple-element.34), kind=kLoop, calls=%fused_computation.6 | loop fusion | flops 131072 | bytes 1048576 | tf_op jit(solution)/shard_map/concatenate | solution.py:434
  119.5 0.9 collective-permute-start.9
  120.4 0.0 copy-done.14
  120.4 0.8 pad_maximum_fusion.3
  121.2 1.2 collective-permute-start.8
  122.4 0.8 pad_maximum_fusion.2
  123.3 1.2 collective-permute-start.7
  124.4 0.7 constant_dynamic-slice_fusion.10
  125.1 0.7 constant_dynamic-slice_fusion.9
  125.9 1.8 %pad_maximum_fusion.1 = f32[64,16,128]{2,1,0:T(8,128)} fusion(f32[32,16,128]{2,1,0:T(8,128)S(1)} %get-tuple-element.46, f32[32,16,128]{2,1,0:T(8,128)} %get-tuple-element.30), kind=kLoop, calls=%fused_computation.3 | loop fusion | flops 131072 | bytes 1048576 | tf_op jit(solution)/shard_map/concatenate | solution.py:434
  127.6 0.0 all-to-all-done.1
  127.6 2.8 %copy-done.2 = f32[2,384,16,128]{3,2,1,0:T(8,128)S(1)} copy-done((f32[2,384,16,128]{3,2,1,0:T(8,128)S(1)}, f32[2,384,16,128]{3,2,1,0:T(8,128)}, u32[]{:S(2)}) %copy-start.2) | copy-done | bytes 6291480
  130.4 1.9 %copy-done.6 = f32[1,6144,128]{2,1,0:T(8,128)S(1)} copy-done((f32[1,6144,128]{2,1,0:T(8,128)S(1)}, f32[1,6144,128]{2,1,0:T(8,128)}, u32[]{:S(2)}) %copy-start.6) | copy-done | bytes 3145752
  132.3 11.7 %middle_terms.1 = f32[2,6144,128]{2,1,0:T(8,128)} custom-call(s32[2]{0:T(128)S(1)} %copy-done.10, f32[3,384]{1,0:T(4,128)S(1)} %pad_maximum_fusion.5.coriolis, f32[1,6144,128]{2,1,0:T(8,128)S(1)} %local_terms.2.below_ref, f32[1,6144,128]{2,1,0:T(8,128)S(1)} %copy-done.6, f32[2,6144,128]{2,1,0:T(8,128)S(1)} %bitcast.36, f32[6144,128]{1,0:T(8,128)} %bitcast.8.lower_ref, ...), custom_call_target="tpu_custom_call" | custom-call | flops 1000000 | bytes 100000 | tf_op jit(solution)/shard_map/middle_terms/pallas_call | solution.py:298
  144.1 4.7 %collective-permute-done.9 = f32[64,16,128]{2,1,0:T(8,128)} collective-permute-done((f32[64,16,128]{2,1,0:T(8,128)}, f32[64,16,128]{2,1,0:T(8,128)}, u32[]{:S(2)}, u32[]{:S(2)}) %collective-permute-start.9) | collective-permute-done | bytes 524320 | tf_op jit(solution)/shard_map/ppermute | solution.py:363
  148.8 0.0 collective-permute-done.8
  148.8 0.0 collective-permute-done.7
  148.8 0.0 copy-done.12
  148.8 0.0 copy-start.1
  148.8 5.1 %add_apart.1 = f32[12288,128]{1,0:T(8,128)} custom-call(s32[2]{0:T(128)S(1)} %copy-done.12, s32[2]{0:T(128)S(1)} %copy-done.10, f32[12288,128]{1,0:T(8,128)} %bitcast.40, f32[16,128]{1,0:T(8,128)S(1)} %broadcast_in_dim.2.factor_ref, f32[1024,128]{1,0:T(8,128)S(1)} %bitcast.39, f32[1024,128]{1,0:T(8,128)} %bitcast.20.refs_1_, ...), custom_call_target="tpu_custom_call", output_to_operand_aliasing={{}: (2, {})} | custom-call | flops 1000000 | bytes 100000 | tf_op jit(solution)/shard_map/add_apart/pallas_call | solution.py:345
  (26 shorter events, 0.1 us)
Async XLA Ops:
  0.0 28.0 %copy-start = (f32[128,128]{1,0:T(8,128)S(1)}, f32[128,128]{1,0:T(8,128)}, u32[]{:S(2)}) copy-start(f32[128,128]{1,0:T(8,128)} %param.16) | copy-start | bytes 196612
  3.6 54.8 %all-to-all-start = ((f32[512,16,128]{2,1,0:T(8,128)}), f32[512,16,128]{2,1,0:T(8,128)}, u32[]{:S(2)}, u32[]{:S(2)}) async-start(f32[512,16,128]{2,1,0:T(8,128)} %leading.1), calls=%async_computation | async-start | bytes 8388608 | tf_op jit(solution)/shard_map/all_to_all | solution.py:23
  9.5 2.9 %copy-start.10 = (s32[2]{0:T(128)S(1)}, s32[2]{0:T(128)}, u32[]{:S(2)}) copy-start(s32[2]{0:T(128)} %sizes.7) | copy-start | bytes 28
  12.5 15.4 %copy-start.15 = (f32[128,128]{1,0:T(8,128)S(1)}, f32[128,128]{1,0:T(8,128)}, u32[]{:S(2)}) copy-start(f32[128,128]{1,0:T(8,128)} %param.19) | copy-start | bytes 196612
  12.5 15.6 %copy-start.17 = (f32[16]{0:T(128)S(1)}, f32[16]{0:T(128)}, u32[]{:S(2)}) copy-start(f32[16]{0:T(128)} %param.17) | copy-start | bytes 196
  12.5 15.7 %copy-start.11 = (f32[2,384]{1,0:T(2,128)S(1)}, f32[2,384]{1,0:T(2,128)}, u32[]{:S(2)}) copy-start(f32[2,384]{1,0:T(2,128)} %centrifugal.3) | copy-start | bytes 9220
  17.7 91.5 %collective-permute-start.3 = (f32[1,384,16,128]{3,2,1,0:T(8,128)}, f32[1,384,16,128]{3,2,1,0:T(8,128)}, u32[]{:S(2)}, u32[]{:S(2)}) collective-permute-start(f32[1,384,16,128]{3,2,1,0:T(8,128)} %get-tuple-element.37), channel_id=1, source_target_pairs={{0,8},{8,16},{16,24},{24,32},{32,40},{40,48},{48,56},{56,64},{64,7... | collective-permute-start | bytes 9437192 | tf_op jit(solution)/shard_map/ppermute | solution.py:19
  22.6 86.6 %collective-permute-start.4 = (f32[1,384,16,128]{3,2,1,0:T(8,128)}, f32[1,384,16,128]{3,2,1,0:T(8,128)}, u32[]{:S(2)}, u32[]{:S(2)}) collective-permute-start(f32[1,384,16,128]{3,2,1,0:T(8,128)} %get-tuple-element.38), channel_id=1, source_target_pairs={{8,0},{16,8},{24,16},{32,24},{40,32},{48,40},{56,48},{64,56},{72,6... | collective-permute-start | bytes 9437192 | tf_op jit(solution)/shard_map/ppermute | solution.py:19
  23.9 47.8 %collective-permute-start = (f32[64,16,128]{2,1,0:T(8,128)}, f32[64,16,128]{2,1,0:T(8,128)}, u32[]{:S(2)}, u32[]{:S(2)}) collective-permute-start(f32[64,16,128]{2,1,0:T(8,128)} %get-tuple-element.41), channel_id=1, source_target_pairs={{0,2},{1,3},{2,0},{3,1},{4,6},{5,7},{6,4},{7,5},{8,10},{9,11},{10,... | collective-permute-start | bytes 1572872 | tf_op jit(solution)/shard_map/ppermute | solution.py:363
  25.4 55.5 %collective-permute-start.1 = (f32[64,16,128]{2,1,0:T(8,128)}, f32[64,16,128]{2,1,0:T(8,128)}, u32[]{:S(2)}, u32[]{:S(2)}) collective-permute-start(f32[64,16,128]{2,1,0:T(8,128)} %get-tuple-element.40), channel_id=1, source_target_pairs={{0,4},{1,5},{2,6},{3,7},{4,0},{5,1},{6,2},{7,3},{8,12},{9,13},{10,... | collective-permute-start | bytes 1572872 | tf_op jit(solution)/shard_map/ppermute | solution.py:363
  27.8 53.1 %collective-permute-start.2 = (f32[64,16,128]{2,1,0:T(8,128)}, f32[64,16,128]{2,1,0:T(8,128)}, u32[]{:S(2)}, u32[]{:S(2)}) collective-permute-start(f32[64,16,128]{2,1,0:T(8,128)} %get-tuple-element.39), channel_id=1, source_target_pairs={{0,6},{1,7},{2,4},{3,5},{4,2},{5,3},{6,0},{7,1},{8,14},{9,15},{10,... | collective-permute-start | bytes 1572872 | tf_op jit(solution)/shard_map/ppermute | solution.py:363
  28.1 2.2 %copy-start.3 = (f32[512,16,128]{2,1,0:T(8,128)S(1)}, f32[512,16,128]{2,1,0:T(8,128)}, u32[]{:S(2)}) copy-start(f32[512,16,128]{2,1,0:T(8,128)} %param.21) | copy-start | bytes 12582916
  30.3 1.4 copy-start.7
  31.7 20.7 %copy-start.16 = (f32[128,128]{1,0:T(8,128)S(1)}, f32[128,128]{1,0:T(8,128)}, u32[]{:S(2)}) copy-start(f32[128,128]{1,0:T(8,128)} %param.18) | copy-start | bytes 196612
  66.0 61.7 %all-to-all-start.1 = ((f32[512,16,128]{2,1,0:T(8,128)}), f32[512,16,128]{2,1,0:T(8,128)}, u32[]{:S(2)}, u32[]{:S(2)}) async-start(f32[512,16,128]{2,1,0:T(8,128)} %bitcast.43), calls=%async_computation.1 | async-start | bytes 8388608 | tf_op jit(solution)/shard_map/all_to_all | solution.py:23
  71.7 13.5 %copy-start.4 = (f32[512,16,128]{2,1,0:T(8,128)S(1)}, f32[512,16,128]{2,1,0:T(8,128)}, u32[]{:S(2)}) copy-start(f32[512,16,128]{2,1,0:T(8,128)} %param.21) | copy-start | bytes 12582916
  83.2 26.0 %collective-permute-start.5 = (f32[4,32,16,128]{3,2,1,0:T(8,128)S(1)}, f32[4,32,16,128]{3,2,1,0:T(8,128)}, u32[]{:S(2)}, u32[]{:S(2)}) collective-permute-start(f32[4,32,16,128]{3,2,1,0:T(8,128)S(1)} %pad_maximum_fusion), channel_id=1, source_target_pairs={{0,1},{1,0},{2,3},{3,2},{4,5},{5,4},{6,7},{7,6},{8,9},{9,8},{10,11... | collective-permute-start | bytes 3145736 | tf_op jit(solution)/shard_map/ppermute | solution.py:363
  85.3 1.4 copy-start.8
  107.4 1.8 %copy-start.5 = (f32[1,6144,128]{2,1,0:T(8,128)}, f32[1,6144,128]{2,1,0:T(8,128)S(1)}, u32[]{:S(2)}) copy-start(f32[1,6144,128]{2,1,0:T(8,128)S(1)} %local_terms.3.above_ref) | copy-start | bytes 9437188
  114.6 5.7 %copy-start.14 = (f32[32,16,128]{2,1,0:T(8,128)S(1)}, f32[32,16,128]{2,1,0:T(8,128)}, u32[]{:S(2)}) copy-start(f32[32,16,128]{2,1,0:T(8,128)} %get-tuple-element.33) | copy-start | bytes 786436
  114.6 7.8 %copy-start.13 = (f32[32,16,128]{2,1,0:T(8,128)S(1)}, f32[32,16,128]{2,1,0:T(8,128)}, u32[]{:S(2)}) copy-start(f32[32,16,128]{2,1,0:T(8,128)} %get-tuple-element.32) | copy-start | bytes 786436
  114.6 3.0 %collective-permute-start.6 = (f32[4,32,16,128]{3,2,1,0:T(8,128)}, f32[4,32,16,128]{3,2,1,0:T(8,128)S(1)}, u32[]{:S(2)}, u32[]{:S(2)}) collective-permute-start(f32[4,32,16,128]{3,2,1,0:T(8,128)} %get-tuple-element.31), channel_id=1, source_target_pairs={{0,1},{1,0},{2,3},{3,2},{4,5},{5,4},{6,7},{7,6},{8,9},{9,8},{10,11... | collective-permute-start | bytes 3145736 | tf_op jit(solution)/shard_map/ppermute | solution.py:363
  119.5 29.3 %collective-permute-start.9 = (f32[64,16,128]{2,1,0:T(8,128)}, f32[64,16,128]{2,1,0:T(8,128)}, u32[]{:S(2)}, u32[]{:S(2)}) collective-permute-start(f32[64,16,128]{2,1,0:T(8,128)} %pad_maximum_fusion.4), channel_id=1, source_target_pairs={{0,6},{1,7},{2,4},{3,5},{4,2},{5,3},{6,0},{7,1},{8,14},{9,15},{10,... | collective-permute-start | bytes 1572872 | tf_op jit(solution)/shard_map/ppermute | solution.py:363
  121.2 27.6 %collective-permute-start.8 = (f32[64,16,128]{2,1,0:T(8,128)}, f32[64,16,128]{2,1,0:T(8,128)}, u32[]{:S(2)}, u32[]{:S(2)}) collective-permute-start(f32[64,16,128]{2,1,0:T(8,128)} %pad_maximum_fusion.3), channel_id=1, source_target_pairs={{0,4},{1,5},{2,6},{3,7},{4,0},{5,1},{6,2},{7,3},{8,12},{9,13},{10,... | collective-permute-start | bytes 1572872 | tf_op jit(solution)/shard_map/ppermute | solution.py:363
  123.3 25.5 %collective-permute-start.7 = (f32[64,16,128]{2,1,0:T(8,128)}, f32[64,16,128]{2,1,0:T(8,128)}, u32[]{:S(2)}, u32[]{:S(2)}) collective-permute-start(f32[64,16,128]{2,1,0:T(8,128)} %pad_maximum_fusion.2), channel_id=1, source_target_pairs={{0,2},{1,3},{2,0},{3,1},{4,6},{5,7},{6,4},{7,5},{8,10},{9,11},{10,... | collective-permute-start | bytes 1572872 | tf_op jit(solution)/shard_map/ppermute | solution.py:363
  127.6 2.8 %copy-start.2 = (f32[2,384,16,128]{3,2,1,0:T(8,128)S(1)}, f32[2,384,16,128]{3,2,1,0:T(8,128)}, u32[]{:S(2)}) copy-start(f32[2,384,16,128]{3,2,1,0:T(8,128)} %param.11) | copy-start | bytes 18874372
  130.4 1.9 %copy-start.6 = (f32[1,6144,128]{2,1,0:T(8,128)S(1)}, f32[1,6144,128]{2,1,0:T(8,128)}, u32[]{:S(2)}) copy-start(f32[1,6144,128]{2,1,0:T(8,128)} %copy-done.5) | copy-start | bytes 9437188
  132.3 16.5 %copy-start.9 = (f32[64,16,128]{2,1,0:T(8,128)S(1)}, f32[64,16,128]{2,1,0:T(8,128)}, u32[]{:S(2)}) copy-start(f32[64,16,128]{2,1,0:T(8,128)} %pad_maximum_fusion.1) | copy-start | bytes 1572868
  132.3 16.5 %copy-start.12 = (s32[2]{0:T(128)S(1)}, s32[2]{0:T(128)}, u32[]{:S(2)}) copy-start(s32[2]{0:T(128)} %pad_add_fusion.where_ref.where) | copy-start | bytes 28
  148.8 5.1 %copy-start.1 = (f32[128,128]{1,0:T(8,128)S(1)}, f32[128,128]{1,0:T(8,128)}, u32[]{:S(2)}) copy-start(f32[128,128]{1,0:T(8,128)} %param.16) | copy-start | bytes 196612

commit v3 on v2

--- a/solution.py
+++ b/solution.py
@@ -10,7 +10,7 @@
 F32 = jnp.float32
 BF16 = jnp.bfloat16
 MIB = 1 << 20
-BRIEF = pl.CostEstimate(flops=1_000_000, bytes_accessed=100_000, transcendentals=0)
+BRIEF = pl.CostEstimate(flops=1, bytes_accessed=1, transcendentals=0)
 
 
 def from_behind(x, axis, by):
@@ -53,7 +53,7 @@
 
 
 def leading(x, count):
-    parts = 8
+    parts = 4
     return pl.pallas_call(
         leading_kernel,
         in_specs=[pl.BlockSpec(memory_space=pl.ANY)],
@@ -152,7 +152,7 @@
             pltpu.VMEM((angles, 3 * basis), BF16),
             pltpu.VMEM((basis, 3 * angles), BF16),
         ],
-        compiler_params=pltpu.CompilerParams(vmem_limit_bytes=40 * MIB),
+        compiler_params=pltpu.CompilerParams(vmem_limit_bytes=60 * MIB),
         cost_estimate=BRIEF,
         name="local_terms",
     )(sizes, centrifugal, x, previous, potential, legendre, stretch, inertia, factor)
@@ -177,13 +177,14 @@
 
 def radial_apply(matrix, received):
     peers, columns, rows, width = received.shape
-    some = pl.BlockSpec((peers, 8, rows, width), lambda i: (0, i, 0, 0))
+    some = pl.BlockSpec((peers, 16, rows, width), lambda i: (0, i, 0, 0))
     return pl.pallas_call(
         radial_kernel,
-        grid=(columns // 8,),
+        grid=(columns // 16,),
         in_specs=[pl.BlockSpec(matrix.shape, lambda i: (0, 0)), some],
         out_specs=some,
         out_shape=jax.ShapeDtypeStruct(received.shape, F32),
+        compiler_params=pltpu.CompilerParams(vmem_limit_bytes=60 * MIB),
         cost_estimate=BRIEF,
         name="radial_apply",
     )(matrix, received)
@@ -248,8 +249,8 @@
 
 
 def middle_kernel(
-    sizes, coriolis, below_ref, above_ref, x_ref, lower_ref, upper_ref, first_ref, second_ref,
-    inertia_ref, factor_ref, out_ref
+    sizes, coriolis, where, below_ref, above_ref, x_ref, lower_ref, upper_ref, first_ref, second_ref,
+    own_ref, inertia_ref, factor_ref, out_ref
 ):
     step = pl.program_id(0)
     radial = inertia_ref.shape[0]
@@ -279,16 +280,32 @@
 
     pl.when(step < SECOND_PARTS)(lambda: part(True))
     pl.when(step >= SECOND_PARTS)(lambda: part(False))
+    own = SECOND_PARTS + where[0] // 2 * 2
+
+    @pl.when((step == own) | (step == own + 1))
+    def _():
+        start = ((step - own) ^ where[1]) * count
+
+        @pl.loop(0, count // 4)
+        def _(i):
+            for k in range(4):
+                local = i * 4 + k
+                at = pl.ds(pl.multiple_of(local * radial, radial), radial)
+                of = pl.ds(pl.multiple_of((start + local) * radial, radial), radial)
+                more = jnp.where(step * count + local < above, double * own_ref[of, :], 0.0)
+                out_ref[1, at, :] += more
 
 
 MIDDLE_PARTS = 12
 SECOND_PARTS = 4
 
 
-def middle_terms(sizes, coriolis, below, above, x, lower, upper, back, inertia, factor):
+def middle_terms(
+    sizes, coriolis, where, below, above, x, lower, upper, back, own, inertia, factor
+):
     blocks, rows, width = x.shape
     size = rows // MIDDLE_PARTS
-    assert back.shape[0] == rows + size * SECOND_PARTS
+    assert back.shape[0] == rows + size * SECOND_PARTS and own.shape[0] == 2 * size
     smem = pl.BlockSpec(memory_space=pltpu.SMEM)
     pair = pl.BlockSpec((blocks, size, width), lambda i: (0, i, 0))
     single = pl.BlockSpec((1, size, width), lambda i: (0, i, 0))
@@ -298,61 +315,71 @@
     return pl.pallas_call(
         middle_kernel,
         grid=(MIDDLE_PARTS,),
-        in_specs=[smem, smem, single, single, pair, one, one, one, second, small, small],
+        in_specs=[
+            smem, smem, smem, single, single, pair, one, one, one, second,
+            pl.BlockSpec(own.shape, lambda i: (0, 0)), small, small,
+        ],
         out_specs=pair,
         out_shape=jax.ShapeDtypeStruct(x.shape, F32),
-        compiler_params=pltpu.CompilerParams(vmem_limit_bytes=20 * MIB),
+        compiler_params=pltpu.CompilerParams(vmem_limit_bytes=60 * MIB),
         cost_estimate=BRIEF,
         name="middle_terms",
-    )(sizes, coriolis, below, above, x, lower, upper, back, back, inertia, factor)
-
-
-def add_rows(target, source, double, columns, begin, live):
-    radial = double.shape[0]
-
-    @pl.loop(0, columns // 8)
-    def _(i):
-        for k in range(8):
-            j = i * 8 + k
-            at = pl.ds(pl.multiple_of(j * radial, radial), radial)
-            target(at, jnp.where(begin + j < live, double * source[at, :], 0.0))
+    )(sizes, coriolis, where, below, above, x, lower, upper, back, back, own, inertia, factor)
 
 
 def add_apart_kernel(basis, lead, where, sizes, out_in, factor_ref, *refs):
-    backs, out_ref = refs[:-1], refs[-1]
-    step = pl.program_id(0)
-    part = out_in.shape[0] // 2
-    columns = part // factor_ref.shape[0]
-    begin = (lead + (where[0] // 2 ^ step)) * 2 * columns
-    live = jnp.where(begin < basis, sizes[0], sizes[1] + basis)
-    for d, back_ref in enumerate(backs):
-        @pl.when(step == d)
-        def _():
-            for core in range(2):
-                source = back_ref.at[pl.ds(pl.multiple_of((where[1] ^ core) * part, part), part), :]
-
-                def target(at, more):
-                    to = pl.ds(core * part + at.start, at.size)
-                    out_ref[to, :] = out_in[to, :] + more
-
-                add_rows(target, source, 2.0 * factor_ref[...], columns, begin + core * columns, live)
+    backs, (out_ref, held, sems, end_sems) = refs[:-4], refs[-4:]
+    radial = factor_ref.shape[0]
+    rows = held.shape[1]
+    columns = rows // radial
+    half = columns // 2
+    double = 2.0 * factor_ref[...]
+    places = [lead + (where[0] // 2 ^ (i + 1)) for i in range(len(backs))]
+    windows = [out_ref.at[pl.ds(pl.multiple_of(p * rows, rows), rows), :] for p in places]
+    reads = [
+        pltpu.make_async_copy(w, held.at[i], sems.at[i]) for i, w in enumerate(windows)
+    ]
+    writes = [
+        pltpu.make_async_copy(held.at[i], w, end_sems.at[i]) for i, w in enumerate(windows)
+    ]
+    for read in reads:
+        read.start()
+    for i in range(len(backs)):
+        reads[i].wait()
+        begin = places[i] * columns
+        live = jnp.where(begin < basis, sizes[0], sizes[1] + basis) - begin
+        for core in range(2):
+            shift = (where[1] ^ core) - core
+
+            @pl.loop(0, half // 8)
+            def _(c):
+                for k in range(8):
+                    j = core * half + c * 8 + k
+                    at = pl.ds(pl.multiple_of(j * radial, radial), radial)
+                    of = pl.ds(pl.multiple_of((j + shift * half) * radial, radial), radial)
+                    held[i, at, :] += jnp.where(j < live, double * backs[i][of, :], 0.0)
+        writes[i].start()
+    for write in writes:
+        write.wait()
 
 
 def add_apart(basis, lead, where, sizes, out, backs, factor):
     rows, width = backs[0].shape
-    window = pl.BlockSpec((rows, width), lambda i, where, sizes: (lead + (where[0] // 2 ^ i), 0))
-    full = lambda a: pl.BlockSpec(a.shape, lambda i, where, sizes: (0, 0))
+    count = len(backs)
+    smem = pl.BlockSpec(memory_space=pltpu.SMEM)
+    whole = pl.BlockSpec(memory_space=pl.ANY)
     return pl.pallas_call(
         functools.partial(add_apart_kernel, basis, lead),
-        grid_spec=pltpu.PrefetchScalarGridSpec(
-            num_scalar_prefetch=2,
-            grid=(len(backs),),
-            in_specs=[window, full(factor)] + [full(b) for b in backs],
-            out_specs=window,
-        ),
+        in_specs=[smem, smem, whole] + [pl.BlockSpec(memory_space=pltpu.VMEM)] * (1 + count),
+        out_specs=whole,
         out_shape=jax.ShapeDtypeStruct(out.shape, F32),
         input_output_aliases={2: 0},
-        compiler_params=pltpu.CompilerParams(vmem_limit_bytes=20 * MIB),
+        scratch_shapes=[
+            pltpu.VMEM((count, rows, width), F32),
+            pltpu.SemaphoreType.DMA((count,)),
+            pltpu.SemaphoreType.DMA((count,)),
+        ],
+        compiler_params=pltpu.CompilerParams(vmem_limit_bytes=16 * MIB),
         cost_estimate=BRIEF,
         name="add_apart",
     )(where, sizes, out, factor, *backs)
@@ -383,13 +410,13 @@
     x_chip, core = row // 2, row % 2
 
     flat = packet.reshape(columns, radial, width)
+    def part(x, d):
+        return lax.dynamic_slice_in_dim(x, joined + (x_chip ^ d) * 2 * piece, 2 * piece, 0)
+
     sent_a = leading(flat, joined)
     got_a = exchange(sent_a)
     source = after(flat, sent_a)
-    sent = [
-        lax.dynamic_slice_in_dim(source, joined + (x_chip ^ d) * 2 * piece, 2 * piece, 0)
-        for d in range(chips)
-    ]
+    sent = [part(source, d) for d in range(chips)]
     ours = [sent[0]] + [swap(sent[d], 2 * d) for d in range(1, chips)]
     live_mask = (lax.broadcasted_iota(jnp.int32, (blocks, basis), 1) < basis_sizes[:, None]).astype(F32)
     source = after(packet, *sent)
@@ -423,8 +450,8 @@
     below = local(0, after(x, upper, lower))
     made_a = radial_apply(after(matrix, below), got_a.reshape(peers, joined // peers, radial, width))
     back_a = exchange(made_a.reshape(joined, radial, width))
-    ours = lax.optimization_barrier((made_a, *ours))[1:]
-    above = local(1, after(x, *ours))
+    above = local(1, after(x, made_a))
+    ours = lax.optimization_barrier((above, *ours))[1:]
     ours = [o.reshape(2, piece, radial, width) for o in ours]
     passed = [lax.dynamic_index_in_dim(o, 1 - core, 0) for o in ours]
     theirs = swap(jnp.concatenate(passed, 0), 1)
@@ -437,13 +464,14 @@
     upper = from_ahead.reshape(rows, width)
     lower = from_below.reshape(rows, width)
     out = middle_terms(
-        basis_sizes, coupling, below, above, x, lower, upper,
-        back_a.reshape(joined * radial, width), inertia_local, factor,
+        basis_sizes, coupling, where, below, above, x, lower, upper,
+        back_a.reshape(joined * radial, width), joint[0].reshape(2 * piece * radial, width),
+        inertia_local, factor,
     )
     out = out.reshape(columns * radial, width)
+    back_b = [b.reshape(2 * piece * radial, width) for b in back_b]
     out = add_apart(
-        basis, joined // (2 * piece), where, basis_sizes, out,
-        [b.reshape(2 * piece * radial, width) for b in back_b], factor,
+        basis, joined // (2 * piece), where, basis_sizes, out, back_b[1:], factor
     )
     return out.reshape(packet.shape)
 

time: 155 us -> 153 us (0.987)
  local copies, waits for them, and re-layouts: 18.2 us -> 6.51 us
  starting transfers between devices: 26.6 us -> 33.7 us
  Pallas kernels: 74.8 us -> 79.8 us
  waiting for transfers between devices: 22.1 us -> 20.5 us
    unnamed x37 -> x33, local copies, waits for them, and re-layouts: 11.6 us -> 1.11 us
    all_to_all x2, starting transfers between devices: 11.6 us -> 19.7 us  [exchange(): return lax.all_to_all(x, 'row', split_axis=0, concat_axis=0, tiled=True)]
    pallas_call x2, Pallas kernels: 41.5 us -> 47.8 us  [local_terms(): pl.pallas_call(functools.partial(local_kernel, block), grid=(1,), in_spec...]
    ppermute x8, waiting for transfers between devices: 16.8 us -> 12.1 us  [swap(): return lax.ppermute(x, 'row', [(i, i ^ by) for i in range(peers)])]
    pallas_call x2, Pallas kernels: 12.6 us -> 8.45 us  [the longest x1 5.55 us: radial_apply(): pl.pallas_call(radial_kernel, grid=(columns // 16,), in_specs=[pl.BlockSp...]
    all_to_all x2, waiting for transfers between devices: 5.28 us -> 8.44 us  [exchange(): return lax.all_to_all(x, 'row', split_axis=0, concat_axis=0, tiled=True)]
    pallas_call x1, Pallas kernels: 11.7 us -> 14.9 us  [middle_terms(): pl.pallas_call(middle_kernel, grid=(MIDDLE_PARTS,), in_specs=[smem, smem,...]
    concatenate x4, other arithmetic: 5.24 us -> 2.83 us  [shards(): joint = [jnp.concatenate([made_b[d], passed[d]], 0) for d in range(chips)]]
  transfers between devices with their start and end apart: 12 -> 12, of which waited for: 4 -> 5; matrix products, arithmetic and copies ran while one was open for 12% -> 11% of each run, Pallas kernels for 43% -> 48%
where the time goes in v3:
time: 153 us; the launch traced here: 152 us
  Pallas kernels  79.8 us (52%)
  starting transfers between devices  33.7 us (22%)
  waiting for transfers between devices  20.5 us (13%)
  other arithmetic  11 us (7%)
  local copies, waits for them, and re-layouts  6.51 us (4%)
    pallas_call x2, Pallas kernels, local_terms(): pl.pallas_call(functools.partial(local_kernel, block), grid=(1,), in_spec...  47.8 us
    all_to_all x2, starting transfers between devices, exchange(): return lax.all_to_all(x, 'row', split_axis=0, concat_axis=0, tiled=True)  19.7 us
    pallas_call x1, Pallas kernels, middle_terms(): pl.pallas_call(middle_kernel, grid=(MIDDLE_PARTS,), in_specs=[smem, smem,...  14.9 us
    ppermute x8, waiting for transfers between devices, swap(): return lax.ppermute(x, 'row', [(i, i ^ by) for i in range(peers)])  12.1 us
    all_to_all x2, waiting for transfers between devices, exchange(): return lax.all_to_all(x, 'row', split_axis=0, concat_axis=0, tiled=True)  8.44 us
    ppermute x8, starting transfers between devices, swap(): return lax.ppermute(x, 'row', [(i, i ^ by) for i in range(peers)])  7.78 us
    ppermute x2, starting transfers between devices, from_behind(): return lax.ppermute(x, axis, pairs)  6.23 us
    pallas_call x1, Pallas kernels, radial_apply(): pl.pallas_call(radial_kernel, grid=(columns // 16,), in_specs=[pl.BlockSp...  5.55 us
  transfers between devices with their start and end apart: 12, of which 5 were waited for; matrix products, arithmetic and copies ran while one was open for 11% of the time, Pallas kernels for 48%

profile of v3, /device:TPU:1, one launch (start us, length us, event | category | flops | bytes accessed | tf_op | source)
XLA Modules:
  0.0 151.9 jit_solution(17390636418767204348)
XLA Ops:
  0.0 0.0 copy-start
  0.0 3.3 %leading.1 = f32[512,16,128]{2,1,0:T(8,128)} custom-call(f32[768,16,128]{2,1,0:T(8,128)} %bitcast.35), custom_call_target="tpu_custom_call" | custom-call | flops 1 | bytes 1 | tf_op jit(solution)/shard_map/leading/pallas_call | solution.py:57
  3.3 5.9 %all-to-all-start = ((f32[512,16,128]{2,1,0:T(8,128)}), f32[512,16,128]{2,1,0:T(8,128)}, u32[]{:S(2)}, u32[]{:S(2)}) async-start(f32[512,16,128]{2,1,0:T(8,128)} %leading.1), calls=%async_computation | async-start | bytes 8388608 | tf_op jit(solution)/shard_map/all_to_all | solution.py:23
  9.2 2.5 %constant_dynamic-slice_fusion.5 = (f32[64,16,128]{2,1,0:T(8,128)}, f32[64,16,128]{2,1,0:T(8,128)S(1)}, f32[64,16,128]{2,1,0:T(8,128)S(1)}, f32[64,16,128]{2,1,0:T(8,128)S(1)}) fusion(f32[768,16,128]{2,1,0:T(8,128)} %bitcast.36, s32[]{:T(128)S(6)} %select_n.43, s32[]{:T(128)S(6)} %select_n.42, s32[]{:T(128)S(6)} %select_n.41, s32[]{:T(128)S(6)} %select_n.40), kind=kLoop, calls=%fused_computation.26 | loop fusion | bytes 4194320 | tf_op jit(solution)/shard_map/dynamic_slice | solution.py:414
  11.7 0.0 copy-done.3
  11.7 0.1 compare_convert_fusion
  11.8 0.0 copy-start.15
  11.8 5.3 %slice_multiply_fusion = (f32[1,384,16,128]{3,2,1,0:T(8,128)}, f32[1,384,16,128]{3,2,1,0:T(8,128)}) fusion(f32[2,384,16,128]{3,2,1,0:T(8,128)} %param.11, f32[384]{0:T(512)S(1)} %get-tuple-element.35, f32[384]{0:T(512)S(1)} %get-tuple-element.36), kind=kLoop, calls=%fused_computation | loop fusion | flops 1572864 | bytes 12585984 | tf_op jit(solution)/shard_map/mul | solution.py:424
  17.2 5.0 %collective-permute-start = (f32[1,384,16,128]{3,2,1,0:T(8,128)}, f32[1,384,16,128]{3,2,1,0:T(8,128)}, u32[]{:S(2)}, u32[]{:S(2)}) collective-permute-start(f32[1,384,16,128]{3,2,1,0:T(8,128)} %get-tuple-element.37), channel_id=1, source_target_pairs={{0,8},{8,16},{16,24},{24,32},{32,40},{40,48},{48,56},{56,64},{64,7... | collective-permute-start | bytes 9437192 | tf_op jit(solution)/shard_map/ppermute | solution.py:19
  22.1 1.3 collective-permute-start.1
  23.4 2.7 %collective-permute-start.4 = (f32[64,16,128]{2,1,0:T(8,128)}, f32[64,16,128]{2,1,0:T(8,128)S(1)}, u32[]{:S(2)}, u32[]{:S(2)}) collective-permute-start(f32[64,16,128]{2,1,0:T(8,128)} %get-tuple-element.39), channel_id=1, source_target_pairs={{0,6},{1,7},{2,4},{3,5},{4,2},{5,3},{6,0},{7,1},{8,14},{9,15},{10,... | collective-permute-start | bytes 1572872 | tf_op jit(solution)/shard_map/ppermute | solution.py:390
  26.1 0.5 collective-permute-start.3
  26.7 0.1 collective-permute-start.2
  26.8 0.0 copy-done.13
  26.8 0.1 copy.13
  26.9 0.0 copy-done
  26.9 0.6 constant_dynamic-slice_fusion.4.inertia_ref
  27.5 0.7 maximum_maximum_fusion.stretch_ref
  28.2 0.0 copy-done.15
  28.2 0.7 broadcast_in_dim.2.factor_ref
  28.9 23.9 %local_terms.2.below_ref = f32[1,6144,128]{2,1,0:T(8,128)} custom-call(s32[2]{0:T(128)} %sizes.7, f32[2,384]{1,0:T(2,128)} %centrifugal.3, f32[2,6144,128]{2,1,0:T(8,128)} %bitcast.37, f32[2,6144,128]{2,1,0:T(8,128)} %bitcast.41, f32[8192,128]{1,0:T(8,128)} %bitcast.44, f32[2,512,384]{2,1,0:T(8,128)} %legendre_ref.3, ...), custom_call_target="tpu_custom_call" | custom-call | flops 1 | bytes 1 | tf_op jit(solution)/shard_map/local_terms/pallas_call | solution.py:140
  52.8 0.0 copy-done.14
  52.8 0.7 maximum_maximum_fusion.1.matrix_ref
  53.5 4.7 %all-to-all-done = f32[512,16,128]{2,1,0:T(8,128)} async-done(((f32[512,16,128]{2,1,0:T(8,128)}), f32[512,16,128]{2,1,0:T(8,128)}, u32[]{:S(2)}, u32[]{:S(2)}) %all-to-all-start) | async-done | bytes 4194336 | tf_op jit(solution)/shard_map/all_to_all | solution.py:23
  58.2 5.5 %radial_apply.1 = f32[8,64,16,128]{3,2,1,0:T(8,128)} custom-call(bf16[256,256]{1,0:T(8,128)(2,1)} %maximum_maximum_fusion.1.matrix_ref, f32[8,64,16,128]{3,2,1,0:T(8,128)} %bitcast.7.x_ref), custom_call_target="tpu_custom_call" | custom-call | flops 1 | bytes 1 | tf_op jit(solution)/shard_map/radial_apply/pallas_call | solution.py:181
  63.7 13.9 %all-to-all-start.1 = ((f32[512,16,128]{2,1,0:T(8,128)}), f32[512,16,128]{2,1,0:T(8,128)}, u32[]{:S(2)}, u32[]{:S(2)}) async-start(f32[512,16,128]{2,1,0:T(8,128)} %bitcast.43), calls=%async_computation.1 | async-start | bytes 8388608 | tf_op jit(solution)/shard_map/all_to_all | solution.py:23
  77.6 23.8 %local_terms.3.above_ref = f32[1,6144,128]{2,1,0:T(8,128)} custom-call(s32[2]{0:T(128)} %sizes.7, f32[2,384]{1,0:T(2,128)} %centrifugal.3, f32[2,6144,128]{2,1,0:T(8,128)} %bitcast.38, f32[2,6144,128]{2,1,0:T(8,128)} %bitcast.42, f32[8192,128]{1,0:T(8,128)} %bitcast.45, f32[2,512,384]{2,1,0:T(8,128)} %legendre_ref.3, ...), custom_call_target="tpu_custom_call" | custom-call | flops 1 | bytes 1 | tf_op jit(solution)/shard_map/local_terms/pallas_call | solution.py:140
  101.4 0.0 collective-permute-done.4
  101.4 0.0 collective-permute-done.3
  101.4 0.0 copy-start.8
  101.4 0.0 collective-permute-done.2
  101.5 0.0 copy-start.9
  101.5 0.0 copy-done.6
  101.6 0.1 pad_maximum_fusion
  101.7 0.1 collective-permute-start.5
  101.8 0.8 pad_add_fusion.where_ref.where
  102.6 0.0 collective-permute-done
  102.6 0.0 collective-permute-done.1
  102.6 1.8 %collective-permute-done.5.refs_4_ = f32[4,32,16,128]{3,2,1,0:T(8,128)S(1)} collective-permute-done((f32[4,32,16,128]{3,2,1,0:T(8,128)S(1)}, f32[4,32,16,128]{3,2,1,0:T(8,128)S(1)}, u32[]{:S(2)}, u32[]{:S(2)}) %collective-permute-start.5) | collective-permute-done | bytes 1048608 | tf_op jit(solution)/shard_map/ppermute | solution.py:390
  104.4 0.0 copy-done.7
  104.4 0.0 copy-done.8
  104.4 0.0 copy-done.9
  104.4 0.0 copy-start.10
  104.4 1.0 copy-done.10
  105.4 5.4 %radial_apart.1 = (f32[32,16,128]{2,1,0:T(8,128)}, f32[32,16,128]{2,1,0:T(8,128)}, f32[32,16,128]{2,1,0:T(8,128)}, f32[32,16,128]{2,1,0:T(8,128)}, f32[4,32,16,128]{3,2,1,0:T(8,128)}) custom-call(s32[2]{0:T(128)} %pad_add_fusion.where_ref.where, bf16[256,256]{1,0:T(8,128)(2,1)} %maximum_maximum_fusion.1.matrix_ref, f32[2,32,16,128]{3,2,1,0:T(8,128)} %bitcast.47, ...), custom_call_target="tpu_custom_call" | custom-call | flops 1 | bytes 1 | tf_op jit(solution)/shard_map/radial_apart/pallas_call | solution.py:234
  110.8 0.0 copy-start.11
  110.8 0.2 collective-permute-start.6
  111.0 2.7 %collective-permute-done.6 = f32[4,32,16,128]{3,2,1,0:T(8,128)S(1)} collective-permute-done((f32[4,32,16,128]{3,2,1,0:T(8,128)}, f32[4,32,16,128]{3,2,1,0:T(8,128)S(1)}, u32[]{:S(2)}, u32[]{:S(2)}) %collective-permute-start.6) | collective-permute-done | bytes 1048608 | tf_op jit(solution)/shard_map/ppermute | solution.py:390
  113.7 0.1 slice_bitcast_fusion
  113.8 1.0 pad_maximum_fusion.2
  114.8 1.5 collective-permute-start.7
  116.3 2.5 %collective-permute-start.8 = (f32[64,16,128]{2,1,0:T(8,128)S(1)}, f32[64,16,128]{2,1,0:T(8,128)S(1)}, u32[]{:S(2)}, u32[]{:S(2)}) collective-permute-start(f32[64,16,128]{2,1,0:T(8,128)S(1)} %pad_maximum_fusion.3), channel_id=1, source_target_pairs={{0,4},{1,5},{2,6},{3,7},{4,0},{5,1},{6,2},{7,3},{8,12},{9,13},{10,... | collective-permute-start | bytes 1572872 | tf_op jit(solution)/shard_map/ppermute | solution.py:390
  118.8 0.2 collective-permute-start.9
  119.0 0.7 constant_dynamic-slice_fusion.10
  119.7 0.7 constant_dynamic-slice_fusion.9
  120.4 0.6 pad_maximum_fusion.5.coriolis
  121.0 1.8 %pad_maximum_fusion.1 = f32[64,16,128]{2,1,0:T(8,128)} fusion(f32[32,16,128]{2,1,0:T(8,128)S(1)} %get-tuple-element.46, f32[32,16,128]{2,1,0:T(8,128)} %get-tuple-element.30), kind=kLoop, calls=%fused_computation.3 | loop fusion | flops 131072 | bytes 1048576 | tf_op jit(solution)/shard_map/concatenate | solution.py:461
  122.8 3.8 %all-to-all-done.1 = f32[512,16,128]{2,1,0:T(8,128)} async-done(((f32[512,16,128]{2,1,0:T(8,128)}), f32[512,16,128]{2,1,0:T(8,128)}, u32[]{:S(2)}, u32[]{:S(2)}) %all-to-all-start.1) | async-done | bytes 4194336 | tf_op jit(solution)/shard_map/all_to_all | solution.py:23
  126.5 14.9 %middle_terms.1 = f32[2,6144,128]{2,1,0:T(8,128)} custom-call(s32[2]{0:T(128)} %sizes.7, f32[3,384]{1,0:T(4,128)} %pad_maximum_fusion.5.coriolis, s32[2]{0:T(128)} %pad_add_fusion.where_ref.where, f32[1,6144,128]{2,1,0:T(8,128)} %local_terms.2.below_ref, f32[1,6144,128]{2,1,0:T(8,128)} %local_terms.3.above_ref, f32[2,6144,128]{2,1,0:T(8,128)} %bitcast.39, ...), custom_call_target="tpu_custom_call" | custom-call | flops 1 | bytes 1 | tf_op jit(solution)/shard_map/middle_terms/pallas_call | solution.py:315
  141.4 0.0 collective-permute-done.7
  141.4 7.5 %collective-permute-done.8 = f32[64,16,128]{2,1,0:T(8,128)S(1)} collective-permute-done((f32[64,16,128]{2,1,0:T(8,128)S(1)}, f32[64,16,128]{2,1,0:T(8,128)S(1)}, u32[]{:S(2)}, u32[]{:S(2)}) %collective-permute-start.8) | collective-permute-done | bytes 524320 | tf_op jit(solution)/shard_map/ppermute | solution.py:390
  148.9 0.0 collective-permute-done.9
  148.9 0.0 copy-start.1
  148.9 2.9 %add_apart.1 = f32[12288,128]{1,0:T(8,128)} custom-call(s32[2]{0:T(128)S(1)} %copy-done.5, s32[2]{0:T(128)S(1)} %copy-done.4, f32[12288,128]{1,0:T(8,128)} %bitcast.40, f32[16,128]{1,0:T(8,128)S(1)} %copy-done.2, f32[1024,128]{1,0:T(8,128)S(1)} %bitcast.32, f32[1024,128]{1,0:T(8,128)S(1)} %bitcast.33, ...), custom_call_target="tpu_custom_call", output_to_operand_aliasing={{}: (2, {})} | custom-call | flops 1 | bytes 1 | tf_op jit(solution)/shard_map/add_apart/pallas_call | solution.py:371
  (22 shorter events, 0.2 us)
Async XLA Ops:
  0.0 26.9 %copy-start = (f32[128,128]{1,0:T(8,128)S(1)}, f32[128,128]{1,0:T(8,128)}, u32[]{:S(2)}) copy-start(f32[128,128]{1,0:T(8,128)} %param.16) | copy-start | bytes 196612
  3.3 54.8 %all-to-all-start = ((f32[512,16,128]{2,1,0:T(8,128)}), f32[512,16,128]{2,1,0:T(8,128)}, u32[]{:S(2)}, u32[]{:S(2)}) async-start(f32[512,16,128]{2,1,0:T(8,128)} %leading.1), calls=%async_computation | async-start | bytes 8388608 | tf_op jit(solution)/shard_map/all_to_all | solution.py:23
  9.2 2.5 %copy-start.3 = (s32[2]{0:T(128)S(1)}, s32[2]{0:T(128)}, u32[]{:S(2)}) copy-start(s32[2]{0:T(128)} %sizes.7) | copy-start | bytes 28
  11.7 89.7 %copy-start.6 = (f32[64,16,128]{2,1,0:T(8,128)}, f32[64,16,128]{2,1,0:T(8,128)S(1)}, u32[]{:S(2)}) copy-start(f32[64,16,128]{2,1,0:T(8,128)S(1)} %get-tuple-element.26) | copy-start | bytes 1572868
  11.8 15.0 %copy-start.13 = (f32[128,128]{1,0:T(8,128)S(1)}, f32[128,128]{1,0:T(8,128)}, u32[]{:S(2)}) copy-start(f32[128,128]{1,0:T(8,128)} %param.19) | copy-start | bytes 196612
  11.8 16.4 %copy-start.15 = (f32[16]{0:T(128)S(1)}, f32[16]{0:T(128)}, u32[]{:S(2)}) copy-start(f32[16]{0:T(128)} %param.17) | copy-start | bytes 196
  17.2 85.4 %collective-permute-start = (f32[1,384,16,128]{3,2,1,0:T(8,128)}, f32[1,384,16,128]{3,2,1,0:T(8,128)}, u32[]{:S(2)}, u32[]{:S(2)}) collective-permute-start(f32[1,384,16,128]{3,2,1,0:T(8,128)} %get-tuple-element.37), channel_id=1, source_target_pairs={{0,8},{8,16},{16,24},{24,32},{32,40},{40,48},{48,56},{56,64},{64,7... | collective-permute-start | bytes 9437192 | tf_op jit(solution)/shard_map/ppermute | solution.py:19
  22.1 80.4 %collective-permute-start.1 = (f32[1,384,16,128]{3,2,1,0:T(8,128)}, f32[1,384,16,128]{3,2,1,0:T(8,128)}, u32[]{:S(2)}, u32[]{:S(2)}) collective-permute-start(f32[1,384,16,128]{3,2,1,0:T(8,128)} %get-tuple-element.38), channel_id=1, source_target_pairs={{8,0},{16,8},{24,16},{32,24},{40,32},{48,40},{56,48},{64,56},{72,6... | collective-permute-start | bytes 9437192 | tf_op jit(solution)/shard_map/ppermute | solution.py:19
  23.4 78.0 %collective-permute-start.4 = (f32[64,16,128]{2,1,0:T(8,128)}, f32[64,16,128]{2,1,0:T(8,128)S(1)}, u32[]{:S(2)}, u32[]{:S(2)}) collective-permute-start(f32[64,16,128]{2,1,0:T(8,128)} %get-tuple-element.39), channel_id=1, source_target_pairs={{0,6},{1,7},{2,4},{3,5},{4,2},{5,3},{6,0},{7,1},{8,14},{9,15},{10,... | collective-permute-start | bytes 1572872 | tf_op jit(solution)/shard_map/ppermute | solution.py:390
  26.1 75.3 %collective-permute-start.3 = (f32[64,16,128]{2,1,0:T(8,128)S(1)}, f32[64,16,128]{2,1,0:T(8,128)S(1)}, u32[]{:S(2)}, u32[]{:S(2)}) collective-permute-start(f32[64,16,128]{2,1,0:T(8,128)S(1)} %get-tuple-element.40), channel_id=1, source_target_pairs={{0,4},{1,5},{2,6},{3,7},{4,0},{5,1},{6,2},{7,3},{8,12},{9,13},{10,... | collective-permute-start | bytes 1572872 | tf_op jit(solution)/shard_map/ppermute | solution.py:390
  26.7 74.8 %collective-permute-start.2 = (f32[64,16,128]{2,1,0:T(8,128)S(1)}, f32[64,16,128]{2,1,0:T(8,128)S(1)}, u32[]{:S(2)}, u32[]{:S(2)}) collective-permute-start(f32[64,16,128]{2,1,0:T(8,128)S(1)} %get-tuple-element.41), channel_id=1, source_target_pairs={{0,2},{1,3},{2,0},{3,1},{4,6},{5,7},{6,4},{7,5},{8,10},{9,11},{10,... | collective-permute-start | bytes 1572872 | tf_op jit(solution)/shard_map/ppermute | solution.py:390
  28.9 23.9 %copy-start.14 = (f32[128,128]{1,0:T(8,128)S(1)}, f32[128,128]{1,0:T(8,128)}, u32[]{:S(2)}) copy-start(f32[128,128]{1,0:T(8,128)} %param.18) | copy-start | bytes 196612
  63.7 62.8 %all-to-all-start.1 = ((f32[512,16,128]{2,1,0:T(8,128)}), f32[512,16,128]{2,1,0:T(8,128)}, u32[]{:S(2)}, u32[]{:S(2)}) async-start(f32[512,16,128]{2,1,0:T(8,128)} %bitcast.43), calls=%async_computation.1 | async-start | bytes 8388608 | tf_op jit(solution)/shard_map/all_to_all | solution.py:23
  101.4 3.0 %copy-start.7 = (f32[64,16,128]{2,1,0:T(8,128)}, f32[64,16,128]{2,1,0:T(8,128)S(1)}, u32[]{:S(2)}) copy-start(f32[64,16,128]{2,1,0:T(8,128)S(1)} %collective-permute-done.4) | copy-start | bytes 1572868
  101.4 3.0 %copy-start.8 = (f32[64,16,128]{2,1,0:T(8,128)}, f32[64,16,128]{2,1,0:T(8,128)S(1)}, u32[]{:S(2)}) copy-start(f32[64,16,128]{2,1,0:T(8,128)S(1)} %collective-permute-done.3) | copy-start | bytes 1572868
  101.5 3.0 %copy-start.9 = (f32[64,16,128]{2,1,0:T(8,128)}, f32[64,16,128]{2,1,0:T(8,128)S(1)}, u32[]{:S(2)}) copy-start(f32[64,16,128]{2,1,0:T(8,128)S(1)} %collective-permute-done.2) | copy-start | bytes 1572868
  101.7 2.7 %collective-permute-start.5 = (f32[4,32,16,128]{3,2,1,0:T(8,128)S(1)}, f32[4,32,16,128]{3,2,1,0:T(8,128)S(1)}, u32[]{:S(2)}, u32[]{:S(2)}) collective-permute-start(f32[4,32,16,128]{3,2,1,0:T(8,128)S(1)} %pad_maximum_fusion), channel_id=1, source_target_pairs={{0,1},{1,0},{2,3},{3,2},{4,5},{5,4},{6,7},{7,6},{8,9},{9,8},{10,11... | collective-permute-start | bytes 3145736 | tf_op jit(solution)/shard_map/ppermute | solution.py:390
  104.4 1.0 copy-start.10
  110.8 5.5 %copy-start.12 = (f32[32,16,128]{2,1,0:T(8,128)S(1)}, f32[32,16,128]{2,1,0:T(8,128)}, u32[]{:S(2)}) copy-start(f32[32,16,128]{2,1,0:T(8,128)} %get-tuple-element.33) | copy-start | bytes 786436
  110.8 8.0 %copy-start.11 = (f32[32,16,128]{2,1,0:T(8,128)S(1)}, f32[32,16,128]{2,1,0:T(8,128)}, u32[]{:S(2)}) copy-start(f32[32,16,128]{2,1,0:T(8,128)} %get-tuple-element.34) | copy-start | bytes 786436
  110.8 3.0 %collective-permute-start.6 = (f32[4,32,16,128]{3,2,1,0:T(8,128)}, f32[4,32,16,128]{3,2,1,0:T(8,128)S(1)}, u32[]{:S(2)}, u32[]{:S(2)}) collective-permute-start(f32[4,32,16,128]{3,2,1,0:T(8,128)} %get-tuple-element.31), channel_id=1, source_target_pairs={{0,1},{1,0},{2,3},{3,2},{4,5},{5,4},{6,7},{7,6},{8,9},{9,8},{10,11... | collective-permute-start | bytes 3145736 | tf_op jit(solution)/shard_map/ppermute | solution.py:390
  114.8 26.6 %collective-permute-start.7 = (f32[64,16,128]{2,1,0:T(8,128)S(1)}, f32[64,16,128]{2,1,0:T(8,128)S(1)}, u32[]{:S(2)}, u32[]{:S(2)}) collective-permute-start(f32[64,16,128]{2,1,0:T(8,128)S(1)} %pad_maximum_fusion.2), channel_id=1, source_target_pairs={{0,2},{1,3},{2,0},{3,1},{4,6},{5,7},{6,4},{7,5},{8,10},{9,11},{10,... | collective-permute-start | bytes 1572872 | tf_op jit(solution)/shard_map/ppermute | solution.py:390
  116.3 32.6 %collective-permute-start.8 = (f32[64,16,128]{2,1,0:T(8,128)S(1)}, f32[64,16,128]{2,1,0:T(8,128)S(1)}, u32[]{:S(2)}, u32[]{:S(2)}) collective-permute-start(f32[64,16,128]{2,1,0:T(8,128)S(1)} %pad_maximum_fusion.3), channel_id=1, source_target_pairs={{0,4},{1,5},{2,6},{3,7},{4,0},{5,1},{6,2},{7,3},{8,12},{9,13},{10,... | collective-permute-start | bytes 1572872 | tf_op jit(solution)/shard_map/ppermute | solution.py:390
  118.8 30.1 %collective-permute-start.9 = (f32[64,16,128]{2,1,0:T(8,128)S(1)}, f32[64,16,128]{2,1,0:T(8,128)S(1)}, u32[]{:S(2)}, u32[]{:S(2)}) collective-permute-start(f32[64,16,128]{2,1,0:T(8,128)S(1)} %pad_maximum_fusion.4), channel_id=1, source_target_pairs={{0,6},{1,7},{2,4},{3,5},{4,2},{5,3},{6,0},{7,1},{8,14},{9,15},{10,... | collective-permute-start | bytes 1572872 | tf_op jit(solution)/shard_map/ppermute | solution.py:390
  126.5 22.4 %copy-start.2 = (f32[16,128]{1,0:T(8,128)S(1)}, f32[16,128]{1,0:T(8,128)}, u32[]{:S(2)}) copy-start(f32[16,128]{1,0:T(8,128)} %broadcast_in_dim.2.factor_ref) | copy-start | bytes 24580
  126.5 22.4 %copy-start.4 = (s32[2]{0:T(128)S(1)}, s32[2]{0:T(128)}, u32[]{:S(2)}) copy-start(s32[2]{0:T(128)} %sizes.7) | copy-start | bytes 28
  126.5 22.4 %copy-start.5 = (s32[2]{0:T(128)S(1)}, s32[2]{0:T(128)}, u32[]{:S(2)}) copy-start(s32[2]{0:T(128)} %pad_add_fusion.where_ref.where) | copy-start | bytes 28
  148.9 2.9 %copy-start.1 = (f32[128,128]{1,0:T(8,128)S(1)}, f32[128,128]{1,0:T(8,128)}, u32[]{:S(2)}) copy-start(f32[128,128]{1,0:T(8,128)} %param.16) | copy-start | bytes 196612

commit v4 on v3

--- a/solution.py
+++ b/solution.py
@@ -416,10 +416,13 @@
     sent_a = leading(flat, joined)
     got_a = exchange(sent_a)
     source = after(flat, sent_a)
-    sent = [part(source, d) for d in range(chips)]
-    ours = [sent[0]] + [swap(sent[d], 2 * d) for d in range(1, chips)]
+    order = tuple(reversed(range(chips)))
+    sent = {d: part(source, d) for d in order}
+    ours = {d: swap(sent[d], 2 * d) if d else sent[d] for d in order}
+    ours = [ours[d] for d in range(chips)]
+
     live_mask = (lax.broadcasted_iota(jnp.int32, (blocks, basis), 1) < basis_sizes[:, None]).astype(F32)
-    source = after(packet, *sent)
+    source = after(packet, *sent.values())
     upper = source[:1] * live_mask[:1, :, None, None]
     lower = source[1:] * live_mask[1:, :, None, None]
     from_ahead = from_behind(upper, "ka", -1)

time: 153 us -> 152 us (level)
  starting transfers between devices: 33.7 us -> 26.4 us
  waiting for transfers between devices: 20.5 us -> 27.2 us
    all_to_all x2, starting transfers between devices: 19.7 us -> 11.6 us  [exchange(): return lax.all_to_all(x, 'row', split_axis=0, concat_axis=0, tiled=True)]
    all_to_all x2, waiting for transfers between devices: 8.44 us -> 15.1 us  [exchange(): return lax.all_to_all(x, 'row', split_axis=0, concat_axis=0, tiled=True)]
  transfers between devices with their start and end apart: 12 -> 12, of which waited for: 5 -> 5; matrix products, arithmetic and copies ran while one was open for 11% -> 11% of each run, Pallas kernels for 48% -> 49%
where the time goes in v4:
time: 152 us; the launch traced here: 151 us
  Pallas kernels  79.8 us (52%)
  waiting for transfers between devices  27.2 us (18%)
  starting transfers between devices  26.4 us (17%)
  other arithmetic  10.9 us (7%)
  local copies, waits for them, and re-layouts  6.51 us (4%)
    pallas_call x2, Pallas kernels, local_terms(): pl.pallas_call(functools.partial(local_kernel, block), grid=(1,), in_spec...  47.8 us
    all_to_all x2, waiting for transfers between devices, exchange(): return lax.all_to_all(x, 'row', split_axis=0, concat_axis=0, tiled=True)  15.1 us
    pallas_call x1, Pallas kernels, middle_terms(): pl.pallas_call(middle_kernel, grid=(MIDDLE_PARTS,), in_specs=[smem, smem,...  14.9 us
    ppermute x8, waiting for transfers between devices, swap(): return lax.ppermute(x, 'row', [(i, i ^ by) for i in range(peers)])  12.1 us
    all_to_all x2, starting transfers between devices, exchange(): return lax.all_to_all(x, 'row', split_axis=0, concat_axis=0, tiled=True)  11.6 us
    ppermute x8, starting transfers between devices, swap(): return lax.ppermute(x, 'row', [(i, i ^ by) for i in range(peers)])  8.53 us
    ppermute x2, starting transfers between devices, from_behind(): return lax.ppermute(x, axis, pairs)  6.23 us
    pallas_call x1, Pallas kernels, radial_apply(): pl.pallas_call(radial_kernel, grid=(columns // 16,), in_specs=[pl.BlockSp...  5.55 us
  transfers between devices with their start and end apart: 12, of which 5 were waited for; matrix products, arithmetic and copies ran while one was open for 11% of the time, Pallas kernels for 49%

profile of v4, /device:TPU:1, one launch (start us, length us, event | category | flops | bytes accessed | tf_op | source)
XLA Modules:
  0.0 151.0 jit_solution(12695886621931591534)
XLA Ops:
  0.0 0.0 copy-start
  0.0 3.3 %leading.1 = f32[512,16,128]{2,1,0:T(8,128)} custom-call(f32[768,16,128]{2,1,0:T(8,128)} %bitcast.35), custom_call_target="tpu_custom_call" | custom-call | flops 1 | bytes 1 | tf_op jit(solution)/shard_map/leading/pallas_call | solution.py:57
  3.3 5.9 %all-to-all-start = ((f32[512,16,128]{2,1,0:T(8,128)}), f32[512,16,128]{2,1,0:T(8,128)}, u32[]{:S(2)}, u32[]{:S(2)}) async-start(f32[512,16,128]{2,1,0:T(8,128)} %leading.1), calls=%async_computation | async-start | bytes 8388608 | tf_op jit(solution)/shard_map/all_to_all | solution.py:23
  9.2 2.5 %constant_dynamic-slice_fusion.5 = (f32[64,16,128]{2,1,0:T(8,128)S(1)}, f32[64,16,128]{2,1,0:T(8,128)}, f32[64,16,128]{2,1,0:T(8,128)S(1)}, f32[64,16,128]{2,1,0:T(8,128)S(1)}) fusion(f32[768,16,128]{2,1,0:T(8,128)} %bitcast.36, s32[]{:T(128)S(6)} %select_n.43, s32[]{:T(128)S(6)} %select_n.42, s32[]{:T(128)S(6)} %select_n.41, s32[]{:T(128)S(6)} %select_n.40), kind=kLoop, calls=%fused_computation.26 | loop fusion | bytes 4194320 | tf_op jit(solution)/shard_map/dynamic_slice | solution.py:414
  11.7 0.0 copy-done.3
  11.7 0.1 compare_convert_fusion
  11.8 0.0 copy-start.15
  11.8 5.3 %slice_multiply_fusion = (f32[1,384,16,128]{3,2,1,0:T(8,128)}, f32[1,384,16,128]{3,2,1,0:T(8,128)}) fusion(f32[2,384,16,128]{3,2,1,0:T(8,128)} %param.11, f32[384]{0:T(512)S(1)} %get-tuple-element.35, f32[384]{0:T(512)S(1)} %get-tuple-element.36), kind=kLoop, calls=%fused_computation | loop fusion | flops 1572864 | bytes 12585984 | tf_op jit(solution)/shard_map/mul | solution.py:427
  17.2 5.0 %collective-permute-start = (f32[1,384,16,128]{3,2,1,0:T(8,128)}, f32[1,384,16,128]{3,2,1,0:T(8,128)}, u32[]{:S(2)}, u32[]{:S(2)}) collective-permute-start(f32[1,384,16,128]{3,2,1,0:T(8,128)} %get-tuple-element.37), channel_id=1, source_target_pairs={{0,8},{8,16},{16,24},{24,32},{32,40},{40,48},{48,56},{56,64},{64,7... | collective-permute-start | bytes 9437192 | tf_op jit(solution)/shard_map/ppermute | solution.py:19
  22.1 1.3 collective-permute-start.1
  23.4 1.5 collective-permute-start.2
  24.9 2.4 %collective-permute-start.3 = (f32[64,16,128]{2,1,0:T(8,128)S(1)}, f32[64,16,128]{2,1,0:T(8,128)S(1)}, u32[]{:S(2)}, u32[]{:S(2)}) collective-permute-start(f32[64,16,128]{2,1,0:T(8,128)S(1)} %get-tuple-element.41), channel_id=1, source_target_pairs={{0,4},{1,5},{2,6},{3,7},{4,0},{5,1},{6,2},{7,3},{8,12},{9,13},{10,... | collective-permute-start | bytes 1572872 | tf_op jit(solution)/shard_map/ppermute | solution.py:390
  27.3 0.1 collective-permute-start.4
  27.4 0.0 copy-done.13
  27.4 0.1 copy.13
  27.5 0.0 copy-done
  27.5 0.6 constant_dynamic-slice_fusion.4.inertia_ref
  28.1 0.7 maximum_maximum_fusion.stretch_ref
  28.8 0.0 copy-done.15
  28.8 0.7 broadcast_in_dim.2.factor_ref
  29.4 23.9 %local_terms.2.below_ref = f32[1,6144,128]{2,1,0:T(8,128)} custom-call(s32[2]{0:T(128)} %sizes.7, f32[2,384]{1,0:T(2,128)} %centrifugal.3, f32[2,6144,128]{2,1,0:T(8,128)} %bitcast.37, f32[2,6144,128]{2,1,0:T(8,128)} %bitcast.41, f32[8192,128]{1,0:T(8,128)} %bitcast.44, f32[2,512,384]{2,1,0:T(8,128)} %legendre_ref.3, ...), custom_call_target="tpu_custom_call" | custom-call | flops 1 | bytes 1 | tf_op jit(solution)/shard_map/local_terms/pallas_call | solution.py:140
  53.4 0.0 copy-done.14
  53.4 0.7 maximum_maximum_fusion.1.matrix_ref
  54.1 4.1 %all-to-all-done = f32[512,16,128]{2,1,0:T(8,128)} async-done(((f32[512,16,128]{2,1,0:T(8,128)}), f32[512,16,128]{2,1,0:T(8,128)}, u32[]{:S(2)}, u32[]{:S(2)}) %all-to-all-start) | async-done | bytes 4194336 | tf_op jit(solution)/shard_map/all_to_all | solution.py:23
  58.2 5.5 %radial_apply.1 = f32[8,64,16,128]{3,2,1,0:T(8,128)} custom-call(bf16[256,256]{1,0:T(8,128)(2,1)} %maximum_maximum_fusion.1.matrix_ref, f32[8,64,16,128]{3,2,1,0:T(8,128)} %bitcast.7.x_ref), custom_call_target="tpu_custom_call" | custom-call | flops 1 | bytes 1 | tf_op jit(solution)/shard_map/radial_apply/pallas_call | solution.py:181
  63.7 5.8 %all-to-all-start.1 = ((f32[512,16,128]{2,1,0:T(8,128)}), f32[512,16,128]{2,1,0:T(8,128)}, u32[]{:S(2)}, u32[]{:S(2)}) async-start(f32[512,16,128]{2,1,0:T(8,128)} %bitcast.43), calls=%async_computation.1 | async-start | bytes 8388608 | tf_op jit(solution)/shard_map/all_to_all | solution.py:23
  69.5 23.8 %local_terms.3.above_ref = f32[1,6144,128]{2,1,0:T(8,128)} custom-call(s32[2]{0:T(128)} %sizes.7, f32[2,384]{1,0:T(2,128)} %centrifugal.3, f32[2,6144,128]{2,1,0:T(8,128)} %bitcast.38, f32[2,6144,128]{2,1,0:T(8,128)} %bitcast.42, f32[8192,128]{1,0:T(8,128)} %bitcast.45, f32[2,512,384]{2,1,0:T(8,128)} %legendre_ref.3, ...), custom_call_target="tpu_custom_call" | custom-call | flops 1 | bytes 1 | tf_op jit(solution)/shard_map/local_terms/pallas_call | solution.py:140
  93.3 0.0 collective-permute-done.2
  93.3 0.0 collective-permute-done.3
  93.3 0.0 copy-start.8
  93.3 0.0 collective-permute-done.4
  93.4 0.0 copy-start.9
  93.4 0.0 copy-done.6
  93.5 0.1 pad_maximum_fusion
  93.6 0.2 collective-permute-start.5
  93.8 0.6 pad_add_fusion.where_ref.where
  94.4 0.0 collective-permute-done
  94.4 0.0 collective-permute-done.1
  94.4 1.9 %collective-permute-done.5.refs_4_ = f32[4,32,16,128]{3,2,1,0:T(8,128)S(1)} collective-permute-done((f32[4,32,16,128]{3,2,1,0:T(8,128)S(1)}, f32[4,32,16,128]{3,2,1,0:T(8,128)S(1)}, u32[]{:S(2)}, u32[]{:S(2)}) %collective-permute-start.5) | collective-permute-done | bytes 1048608 | tf_op jit(solution)/shard_map/ppermute | solution.py:390
  96.3 0.0 copy-done.7
  96.3 0.0 copy-done.8
  96.3 0.0 copy-done.9
  96.3 1.0 copy-done.10
  97.3 5.4 %radial_apart.1 = (f32[32,16,128]{2,1,0:T(8,128)}, f32[32,16,128]{2,1,0:T(8,128)}, f32[32,16,128]{2,1,0:T(8,128)}, f32[32,16,128]{2,1,0:T(8,128)}, f32[4,32,16,128]{3,2,1,0:T(8,128)}) custom-call(s32[2]{0:T(128)} %pad_add_fusion.where_ref.where, bf16[256,256]{1,0:T(8,128)(2,1)} %maximum_maximum_fusion.1.matrix_ref, f32[2,32,16,128]{3,2,1,0:T(8,128)} %bitcast.47, ...), custom_call_target="tpu_custom_call" | custom-call | flops 1 | bytes 1 | tf_op jit(solution)/shard_map/radial_apart/pallas_call | solution.py:234
  102.7 0.2 collective-permute-start.6
  102.9 2.7 %collective-permute-done.6 = f32[4,32,16,128]{3,2,1,0:T(8,128)S(1)} collective-permute-done((f32[4,32,16,128]{3,2,1,0:T(8,128)}, f32[4,32,16,128]{3,2,1,0:T(8,128)S(1)}, u32[]{:S(2)}, u32[]{:S(2)}) %collective-permute-start.6) | collective-permute-done | bytes 1048608 | tf_op jit(solution)/shard_map/ppermute | solution.py:390
  105.6 0.1 slice_bitcast_fusion
  105.7 1.0 pad_maximum_fusion.2
  106.7 1.5 collective-permute-start.7
  108.2 2.5 %collective-permute-start.8 = (f32[64,16,128]{2,1,0:T(8,128)S(1)}, f32[64,16,128]{2,1,0:T(8,128)S(1)}, u32[]{:S(2)}, u32[]{:S(2)}) collective-permute-start(f32[64,16,128]{2,1,0:T(8,128)S(1)} %pad_maximum_fusion.3), channel_id=1, source_target_pairs={{0,4},{1,5},{2,6},{3,7},{4,0},{5,1},{6,2},{7,3},{8,12},{9,13},{10,... | collective-permute-start | bytes 1572872 | tf_op jit(solution)/shard_map/ppermute | solution.py:390
  110.8 0.1 collective-permute-start.9
  110.9 0.7 constant_dynamic-slice_fusion.10
  111.6 0.7 constant_dynamic-slice_fusion.9
  112.3 0.6 pad_maximum_fusion.5.coriolis
  112.9 1.8 %pad_maximum_fusion.1 = f32[64,16,128]{2,1,0:T(8,128)} fusion(f32[32,16,128]{2,1,0:T(8,128)S(1)} %get-tuple-element.46, f32[32,16,128]{2,1,0:T(8,128)} %get-tuple-element.30), kind=kLoop, calls=%fused_computation.3 | loop fusion | flops 131072 | bytes 1048576 | tf_op jit(solution)/shard_map/concatenate | solution.py:464
  114.7 11.0 %all-to-all-done.1 = f32[512,16,128]{2,1,0:T(8,128)} async-done(((f32[512,16,128]{2,1,0:T(8,128)}), f32[512,16,128]{2,1,0:T(8,128)}, u32[]{:S(2)}, u32[]{:S(2)}) %all-to-all-start.1) | async-done | bytes 4194336 | tf_op jit(solution)/shard_map/all_to_all | solution.py:23
  125.7 14.9 %middle_terms.1 = f32[2,6144,128]{2,1,0:T(8,128)} custom-call(s32[2]{0:T(128)} %sizes.7, f32[3,384]{1,0:T(4,128)} %pad_maximum_fusion.5.coriolis, s32[2]{0:T(128)} %pad_add_fusion.where_ref.where, f32[1,6144,128]{2,1,0:T(8,128)} %local_terms.2.below_ref, f32[1,6144,128]{2,1,0:T(8,128)} %local_terms.3.above_ref, f32[2,6144,128]{2,1,0:T(8,128)} %bitcast.39, ...), custom_call_target="tpu_custom_call" | custom-call | flops 1 | bytes 1 | tf_op jit(solution)/shard_map/middle_terms/pallas_call | solution.py:315
  140.5 0.0 collective-permute-done.7
  140.5 7.5 %collective-permute-done.8 = f32[64,16,128]{2,1,0:T(8,128)S(1)} collective-permute-done((f32[64,16,128]{2,1,0:T(8,128)S(1)}, f32[64,16,128]{2,1,0:T(8,128)S(1)}, u32[]{:S(2)}, u32[]{:S(2)}) %collective-permute-start.8) | collective-permute-done | bytes 524320 | tf_op jit(solution)/shard_map/ppermute | solution.py:390
  148.0 0.0 collective-permute-done.9
  148.0 0.0 copy-done.2
  148.1 0.0 copy-start.1
  148.1 2.9 %add_apart.1 = f32[12288,128]{1,0:T(8,128)} custom-call(s32[2]{0:T(128)S(1)} %copy-done.5, s32[2]{0:T(128)S(1)} %copy-done.4, f32[12288,128]{1,0:T(8,128)} %bitcast.40, f32[16,128]{1,0:T(8,128)S(1)} %copy-done.2, f32[1024,128]{1,0:T(8,128)S(1)} %bitcast.32, f32[1024,128]{1,0:T(8,128)S(1)} %bitcast.33, ...), custom_call_target="tpu_custom_call", output_to_operand_aliasing={{}: (2, {})} | custom-call | flops 1 | bytes 1 | tf_op jit(solution)/shard_map/add_apart/pallas_call | solution.py:371
  151.0 0.0 copy-done.1
  (22 shorter events, 0.2 us)
Async XLA Ops:
  0.0 27.5 %copy-start = (f32[128,128]{1,0:T(8,128)S(1)}, f32[128,128]{1,0:T(8,128)}, u32[]{:S(2)}) copy-start(f32[128,128]{1,0:T(8,128)} %param.16) | copy-start | bytes 196612
  3.3 54.8 %all-to-all-start = ((f32[512,16,128]{2,1,0:T(8,128)}), f32[512,16,128]{2,1,0:T(8,128)}, u32[]{:S(2)}, u32[]{:S(2)}) async-start(f32[512,16,128]{2,1,0:T(8,128)} %leading.1), calls=%async_computation | async-start | bytes 8388608 | tf_op jit(solution)/shard_map/all_to_all | solution.py:23
  9.2 2.5 %copy-start.3 = (s32[2]{0:T(128)S(1)}, s32[2]{0:T(128)}, u32[]{:S(2)}) copy-start(s32[2]{0:T(128)} %sizes.7) | copy-start | bytes 28
  11.7 81.6 %copy-start.6 = (f32[64,16,128]{2,1,0:T(8,128)}, f32[64,16,128]{2,1,0:T(8,128)S(1)}, u32[]{:S(2)}) copy-start(f32[64,16,128]{2,1,0:T(8,128)S(1)} %get-tuple-element.26) | copy-start | bytes 1572868
  11.8 15.6 %copy-start.13 = (f32[128,128]{1,0:T(8,128)S(1)}, f32[128,128]{1,0:T(8,128)}, u32[]{:S(2)}) copy-start(f32[128,128]{1,0:T(8,128)} %param.19) | copy-start | bytes 196612
  11.8 16.9 %copy-start.15 = (f32[16]{0:T(128)S(1)}, f32[16]{0:T(128)}, u32[]{:S(2)}) copy-start(f32[16]{0:T(128)} %param.17) | copy-start | bytes 196
  17.2 77.2 %collective-permute-start = (f32[1,384,16,128]{3,2,1,0:T(8,128)}, f32[1,384,16,128]{3,2,1,0:T(8,128)}, u32[]{:S(2)}, u32[]{:S(2)}) collective-permute-start(f32[1,384,16,128]{3,2,1,0:T(8,128)} %get-tuple-element.37), channel_id=1, source_target_pairs={{0,8},{8,16},{16,24},{24,32},{32,40},{40,48},{48,56},{56,64},{64,7... | collective-permute-start | bytes 9437192 | tf_op jit(solution)/shard_map/ppermute | solution.py:19
  22.1 72.3 %collective-permute-start.1 = (f32[1,384,16,128]{3,2,1,0:T(8,128)}, f32[1,384,16,128]{3,2,1,0:T(8,128)}, u32[]{:S(2)}, u32[]{:S(2)}) collective-permute-start(f32[1,384,16,128]{3,2,1,0:T(8,128)} %get-tuple-element.38), channel_id=1, source_target_pairs={{8,0},{16,8},{24,16},{32,24},{40,32},{48,40},{56,48},{64,56},{72,6... | collective-permute-start | bytes 9437192 | tf_op jit(solution)/shard_map/ppermute | solution.py:19
  23.4 69.9 %collective-permute-start.2 = (f32[64,16,128]{2,1,0:T(8,128)}, f32[64,16,128]{2,1,0:T(8,128)S(1)}, u32[]{:S(2)}, u32[]{:S(2)}) collective-permute-start(f32[64,16,128]{2,1,0:T(8,128)} %get-tuple-element.40), channel_id=1, source_target_pairs={{0,2},{1,3},{2,0},{3,1},{4,6},{5,7},{6,4},{7,5},{8,10},{9,11},{10,... | collective-permute-start | bytes 1572872 | tf_op jit(solution)/shard_map/ppermute | solution.py:390
  24.9 68.4 %collective-permute-start.3 = (f32[64,16,128]{2,1,0:T(8,128)S(1)}, f32[64,16,128]{2,1,0:T(8,128)S(1)}, u32[]{:S(2)}, u32[]{:S(2)}) collective-permute-start(f32[64,16,128]{2,1,0:T(8,128)S(1)} %get-tuple-element.41), channel_id=1, source_target_pairs={{0,4},{1,5},{2,6},{3,7},{4,0},{5,1},{6,2},{7,3},{8,12},{9,13},{10,... | collective-permute-start | bytes 1572872 | tf_op jit(solution)/shard_map/ppermute | solution.py:390
  27.3 66.0 %collective-permute-start.4 = (f32[64,16,128]{2,1,0:T(8,128)S(1)}, f32[64,16,128]{2,1,0:T(8,128)S(1)}, u32[]{:S(2)}, u32[]{:S(2)}) collective-permute-start(f32[64,16,128]{2,1,0:T(8,128)S(1)} %get-tuple-element.42), channel_id=1, source_target_pairs={{0,6},{1,7},{2,4},{3,5},{4,2},{5,3},{6,0},{7,1},{8,14},{9,15},{10,... | collective-permute-start | bytes 1572872 | tf_op jit(solution)/shard_map/ppermute | solution.py:390
  29.4 23.9 %copy-start.14 = (f32[128,128]{1,0:T(8,128)S(1)}, f32[128,128]{1,0:T(8,128)}, u32[]{:S(2)}) copy-start(f32[128,128]{1,0:T(8,128)} %param.18) | copy-start | bytes 196612
  63.7 62.0 %all-to-all-start.1 = ((f32[512,16,128]{2,1,0:T(8,128)}), f32[512,16,128]{2,1,0:T(8,128)}, u32[]{:S(2)}, u32[]{:S(2)}) async-start(f32[512,16,128]{2,1,0:T(8,128)} %bitcast.43), calls=%async_computation.1 | async-start | bytes 8388608 | tf_op jit(solution)/shard_map/all_to_all | solution.py:23
  93.3 3.0 %copy-start.7 = (f32[64,16,128]{2,1,0:T(8,128)}, f32[64,16,128]{2,1,0:T(8,128)S(1)}, u32[]{:S(2)}) copy-start(f32[64,16,128]{2,1,0:T(8,128)S(1)} %collective-permute-done.2) | copy-start | bytes 1572868
  93.3 3.0 %copy-start.8 = (f32[64,16,128]{2,1,0:T(8,128)}, f32[64,16,128]{2,1,0:T(8,128)S(1)}, u32[]{:S(2)}) copy-start(f32[64,16,128]{2,1,0:T(8,128)S(1)} %collective-permute-done.3) | copy-start | bytes 1572868
  93.4 3.0 %copy-start.9 = (f32[64,16,128]{2,1,0:T(8,128)}, f32[64,16,128]{2,1,0:T(8,128)S(1)}, u32[]{:S(2)}) copy-start(f32[64,16,128]{2,1,0:T(8,128)S(1)} %collective-permute-done.4) | copy-start | bytes 1572868
  93.6 2.7 %collective-permute-start.5 = (f32[4,32,16,128]{3,2,1,0:T(8,128)S(1)}, f32[4,32,16,128]{3,2,1,0:T(8,128)S(1)}, u32[]{:S(2)}, u32[]{:S(2)}) collective-permute-start(f32[4,32,16,128]{3,2,1,0:T(8,128)S(1)} %pad_maximum_fusion), channel_id=1, source_target_pairs={{0,1},{1,0},{2,3},{3,2},{4,5},{5,4},{6,7},{7,6},{8,9},{9,8},{10,11... | collective-permute-start | bytes 3145736 | tf_op jit(solution)/shard_map/ppermute | solution.py:390
  96.3 1.0 copy-start.10
  102.7 5.5 %copy-start.12 = (f32[32,16,128]{2,1,0:T(8,128)S(1)}, f32[32,16,128]{2,1,0:T(8,128)}, u32[]{:S(2)}) copy-start(f32[32,16,128]{2,1,0:T(8,128)} %get-tuple-element.33) | copy-start | bytes 786436
  102.7 8.0 %copy-start.11 = (f32[32,16,128]{2,1,0:T(8,128)S(1)}, f32[32,16,128]{2,1,0:T(8,128)}, u32[]{:S(2)}) copy-start(f32[32,16,128]{2,1,0:T(8,128)} %get-tuple-element.34) | copy-start | bytes 786436
  102.7 3.0 %collective-permute-start.6 = (f32[4,32,16,128]{3,2,1,0:T(8,128)}, f32[4,32,16,128]{3,2,1,0:T(8,128)S(1)}, u32[]{:S(2)}, u32[]{:S(2)}) collective-permute-start(f32[4,32,16,128]{3,2,1,0:T(8,128)} %get-tuple-element.31), channel_id=1, source_target_pairs={{0,1},{1,0},{2,3},{3,2},{4,5},{5,4},{6,7},{7,6},{8,9},{9,8},{10,11... | collective-permute-start | bytes 3145736 | tf_op jit(solution)/shard_map/ppermute | solution.py:390
  106.7 33.8 %collective-permute-start.7 = (f32[64,16,128]{2,1,0:T(8,128)S(1)}, f32[64,16,128]{2,1,0:T(8,128)S(1)}, u32[]{:S(2)}, u32[]{:S(2)}) collective-permute-start(f32[64,16,128]{2,1,0:T(8,128)S(1)} %pad_maximum_fusion.2), channel_id=1, source_target_pairs={{0,2},{1,3},{2,0},{3,1},{4,6},{5,7},{6,4},{7,5},{8,10},{9,11},{10,... | collective-permute-start | bytes 1572872 | tf_op jit(solution)/shard_map/ppermute | solution.py:390
  108.2 39.8 %collective-permute-start.8 = (f32[64,16,128]{2,1,0:T(8,128)S(1)}, f32[64,16,128]{2,1,0:T(8,128)S(1)}, u32[]{:S(2)}, u32[]{:S(2)}) collective-permute-start(f32[64,16,128]{2,1,0:T(8,128)S(1)} %pad_maximum_fusion.3), channel_id=1, source_target_pairs={{0,4},{1,5},{2,6},{3,7},{4,0},{5,1},{6,2},{7,3},{8,12},{9,13},{10,... | collective-permute-start | bytes 1572872 | tf_op jit(solution)/shard_map/ppermute | solution.py:390
  110.8 37.3 %collective-permute-start.9 = (f32[64,16,128]{2,1,0:T(8,128)S(1)}, f32[64,16,128]{2,1,0:T(8,128)S(1)}, u32[]{:S(2)}, u32[]{:S(2)}) collective-permute-start(f32[64,16,128]{2,1,0:T(8,128)S(1)} %pad_maximum_fusion.4), channel_id=1, source_target_pairs={{0,6},{1,7},{2,4},{3,5},{4,2},{5,3},{6,0},{7,1},{8,14},{9,15},{10,... | collective-permute-start | bytes 1572872 | tf_op jit(solution)/shard_map/ppermute | solution.py:390
  125.7 22.4 %copy-start.2 = (f32[16,128]{1,0:T(8,128)S(1)}, f32[16,128]{1,0:T(8,128)}, u32[]{:S(2)}) copy-start(f32[16,128]{1,0:T(8,128)} %broadcast_in_dim.2.factor_ref) | copy-start | bytes 24580
  125.7 22.4 %copy-start.4 = (s32[2]{0:T(128)S(1)}, s32[2]{0:T(128)}, u32[]{:S(2)}) copy-start(s32[2]{0:T(128)} %sizes.7) | copy-start | bytes 28
  125.7 22.4 %copy-start.5 = (s32[2]{0:T(128)S(1)}, s32[2]{0:T(128)}, u32[]{:S(2)}) copy-start(s32[2]{0:T(128)} %pad_add_fusion.where_ref.where) | copy-start | bytes 28
  148.1 2.9 %copy-start.1 = (f32[128,128]{1,0:T(8,128)S(1)}, f32[128,128]{1,0:T(8,128)}, u32[]{:S(2)}) copy-start(f32[128,128]{1,0:T(8,128)} %param.16) | copy-start | bytes 196612

commit v5 on v4

--- a/solution.py
+++ b/solution.py
@@ -335,21 +335,24 @@
     half = columns // 2
     double = 2.0 * factor_ref[...]
     places = [lead + (where[0] // 2 ^ (i + 1)) for i in range(len(backs))]
-    windows = [out_ref.at[pl.ds(pl.multiple_of(p * rows, rows), rows), :] for p in places]
-    reads = [
-        pltpu.make_async_copy(w, held.at[i], sems.at[i]) for i, w in enumerate(windows)
-    ]
-    writes = [
-        pltpu.make_async_copy(held.at[i], w, end_sems.at[i]) for i, w in enumerate(windows)
-    ]
+    reads, writes = [], []
+    part = rows // 2
+    for i, p in enumerate(places):
+        for core in range(2):
+            start = pl.multiple_of((2 * p + core) * part, part)
+            window = out_ref.at[pl.ds(start, part), :]
+            kept = held.at[i, pl.ds(core * part, part), :]
+            n = 2 * i + core
+            reads.append(pltpu.make_async_copy(window, kept, sems.at[n]))
+            writes.append(pltpu.make_async_copy(kept, window, end_sems.at[n]))
     for read in reads:
         read.start()
     for i in range(len(backs)):
-        reads[i].wait()
         begin = places[i] * columns
         live = jnp.where(begin < basis, sizes[0], sizes[1] + basis) - begin
         for core in range(2):
             shift = (where[1] ^ core) - core
+            reads[2 * i + core].wait()
 
             @pl.loop(0, half // 8)
             def _(c):
@@ -358,7 +361,8 @@
                     at = pl.ds(pl.multiple_of(j * radial, radial), radial)
                     of = pl.ds(pl.multiple_of((j + shift * half) * radial, radial), radial)
                     held[i, at, :] += jnp.where(j < live, double * backs[i][of, :], 0.0)
-        writes[i].start()
+
+            writes[2 * i + core].start()
     for write in writes:
         write.wait()
 
@@ -376,8 +380,8 @@
         input_output_aliases={2: 0},
         scratch_shapes=[
             pltpu.VMEM((count, rows, width), F32),
-            pltpu.SemaphoreType.DMA((count,)),
-            pltpu.SemaphoreType.DMA((count,)),
+            pltpu.SemaphoreType.DMA((2 * count,)),
+            pltpu.SemaphoreType.DMA((2 * count,)),
         ],
         compiler_params=pltpu.CompilerParams(vmem_limit_bytes=16 * MIB),
         cost_estimate=BRIEF,
@@ -462,6 +466,7 @@
     *made_b, passed = radial_apart(where, after(matrix, above, from_ahead, from_below), ours, theirs)
     passed = swap(passed, 1)
     joint = [jnp.concatenate([made_b[d], passed[d]], 0) for d in range(chips)]
+    joint = [j if d in (0, 2) else after(j, joint[2]) for d, j in enumerate(joint)]
     back_b = [joint[0]] + [swap(joint[d], 2 * d) for d in range(1, chips)]
 
     upper = from_ahead.reshape(rows, width)

time: 152 us -> 152 us (level)
  no operation moved by 1% of the time
where the time goes in v5:
time: 152 us; the launch traced here: 151 us
  Pallas kernels  79.7 us (52%)
  waiting for transfers between devices  27.3 us (18%)
  starting transfers between devices  26.2 us (17%)
  other arithmetic  10.9 us (7%)
  local copies, waits for them, and re-layouts  6.52 us (4%)
    pallas_call x2, Pallas kernels, local_terms(): pl.pallas_call(functools.partial(local_kernel, block), grid=(1,), in_spec...  47.8 us
    all_to_all x2, waiting for transfers between devices, exchange(): return lax.all_to_all(x, 'row', split_axis=0, concat_axis=0, tiled=True)  15.3 us
    pallas_call x1, Pallas kernels, middle_terms(): pl.pallas_call(middle_kernel, grid=(MIDDLE_PARTS,), in_specs=[smem, smem,...  14.9 us
    ppermute x8, waiting for transfers between devices, swap(): return lax.ppermute(x, 'row', [(i, i ^ by) for i in range(peers)])  12.1 us
    all_to_all x2, starting transfers between devices, exchange(): return lax.all_to_all(x, 'row', split_axis=0, concat_axis=0, tiled=True)  11.6 us
    ppermute x8, starting transfers between devices, swap(): return lax.ppermute(x, 'row', [(i, i ^ by) for i in range(peers)])  8.33 us
    ppermute x2, starting transfers between devices, from_behind(): return lax.ppermute(x, axis, pairs)  6.23 us
    pallas_call x1, Pallas kernels, radial_apply(): pl.pallas_call(radial_kernel, grid=(columns // 16,), in_specs=[pl.BlockSp...  5.55 us
  transfers between devices with their start and end apart: 12, of which 5 were waited for; matrix products, arithmetic and copies ran while one was open for 11% of the time, Pallas kernels for 49%

profile of v5, /device:TPU:1, one launch (start us, length us, event | category | flops | bytes accessed | tf_op | source)
XLA Modules:
  0.0 150.9 jit_solution(15702537869636640644)
XLA Ops:
  0.0 0.0 copy-start
  0.0 3.3 %leading.1 = f32[512,16,128]{2,1,0:T(8,128)} custom-call(f32[768,16,128]{2,1,0:T(8,128)} %bitcast.35), custom_call_target="tpu_custom_call" | custom-call | flops 1 | bytes 1 | tf_op jit(solution)/shard_map/leading/pallas_call | solution.py:57
  3.3 5.9 %all-to-all-start = ((f32[512,16,128]{2,1,0:T(8,128)}), f32[512,16,128]{2,1,0:T(8,128)}, u32[]{:S(2)}, u32[]{:S(2)}) async-start(f32[512,16,128]{2,1,0:T(8,128)} %leading.1), calls=%async_computation | async-start | bytes 8388608 | tf_op jit(solution)/shard_map/all_to_all | solution.py:23
  9.2 2.5 %constant_dynamic-slice_fusion.5 = (f32[64,16,128]{2,1,0:T(8,128)S(1)}, f32[64,16,128]{2,1,0:T(8,128)}, f32[64,16,128]{2,1,0:T(8,128)S(1)}, f32[64,16,128]{2,1,0:T(8,128)S(1)}) fusion(f32[768,16,128]{2,1,0:T(8,128)} %bitcast.36, s32[]{:T(128)S(6)} %select_n.43, s32[]{:T(128)S(6)} %select_n.42, s32[]{:T(128)S(6)} %select_n.41, s32[]{:T(128)S(6)} %select_n.40), kind=kLoop, calls=%fused_computation.26 | loop fusion | bytes 4194320 | tf_op jit(solution)/shard_map/dynamic_slice | solution.py:418
  11.7 0.0 copy-done.3
  11.7 0.1 compare_convert_fusion
  11.8 0.0 copy-start.15
  11.8 5.3 %slice_multiply_fusion = (f32[1,384,16,128]{3,2,1,0:T(8,128)}, f32[1,384,16,128]{3,2,1,0:T(8,128)}) fusion(f32[2,384,16,128]{3,2,1,0:T(8,128)} %param.11, f32[384]{0:T(512)S(1)} %get-tuple-element.39, f32[384]{0:T(512)S(1)} %get-tuple-element.40), kind=kLoop, calls=%fused_computation | loop fusion | flops 1572864 | bytes 12585984 | tf_op jit(solution)/shard_map/mul | solution.py:431
  17.2 5.0 %collective-permute-start = (f32[1,384,16,128]{3,2,1,0:T(8,128)}, f32[1,384,16,128]{3,2,1,0:T(8,128)}, u32[]{:S(2)}, u32[]{:S(2)}) collective-permute-start(f32[1,384,16,128]{3,2,1,0:T(8,128)} %get-tuple-element.41), channel_id=1, source_target_pairs={{0,8},{8,16},{16,24},{24,32},{32,40},{40,48},{48,56},{56,64},{64,7... | collective-permute-start | bytes 9437192 | tf_op jit(solution)/shard_map/ppermute | solution.py:19
  22.1 1.3 collective-permute-start.1
  23.4 1.5 collective-permute-start.2
  24.9 2.4 %collective-permute-start.3 = (f32[64,16,128]{2,1,0:T(8,128)S(1)}, f32[64,16,128]{2,1,0:T(8,128)S(1)}, u32[]{:S(2)}, u32[]{:S(2)}) collective-permute-start(f32[64,16,128]{2,1,0:T(8,128)S(1)} %get-tuple-element.45), channel_id=1, source_target_pairs={{0,4},{1,5},{2,6},{3,7},{4,0},{5,1},{6,2},{7,3},{8,12},{9,13},{10,... | collective-permute-start | bytes 1572872 | tf_op jit(solution)/shard_map/ppermute | solution.py:394
  27.3 0.1 collective-permute-start.4
  27.4 0.0 copy-done.13
  27.4 0.1 copy.13
  27.5 0.0 copy-done
  27.5 0.6 constant_dynamic-slice_fusion.4.inertia_ref
  28.1 0.7 maximum_maximum_fusion.stretch_ref
  28.8 0.0 copy-done.15
  28.8 0.7 broadcast_in_dim.2.factor_ref
  29.4 23.9 %local_terms.2.below_ref = f32[1,6144,128]{2,1,0:T(8,128)} custom-call(s32[2]{0:T(128)} %sizes.7, f32[2,384]{1,0:T(2,128)} %centrifugal.3, f32[2,6144,128]{2,1,0:T(8,128)} %bitcast.37, f32[2,6144,128]{2,1,0:T(8,128)} %bitcast.41, f32[8192,128]{1,0:T(8,128)} %bitcast.44, f32[2,512,384]{2,1,0:T(8,128)} %legendre_ref.3, ...), custom_call_target="tpu_custom_call" | custom-call | flops 1 | bytes 1 | tf_op jit(solution)/shard_map/local_terms/pallas_call | solution.py:140
  53.4 0.0 copy-done.14
  53.4 0.7 maximum_maximum_fusion.1.matrix_ref
  54.1 4.1 %all-to-all-done = f32[512,16,128]{2,1,0:T(8,128)} async-done(((f32[512,16,128]{2,1,0:T(8,128)}), f32[512,16,128]{2,1,0:T(8,128)}, u32[]{:S(2)}, u32[]{:S(2)}) %all-to-all-start) | async-done | bytes 4194336 | tf_op jit(solution)/shard_map/all_to_all | solution.py:23
  58.2 5.5 %radial_apply.1 = f32[8,64,16,128]{3,2,1,0:T(8,128)} custom-call(bf16[256,256]{1,0:T(8,128)(2,1)} %maximum_maximum_fusion.1.matrix_ref, f32[8,64,16,128]{3,2,1,0:T(8,128)} %bitcast.7.x_ref), custom_call_target="tpu_custom_call" | custom-call | flops 1 | bytes 1 | tf_op jit(solution)/shard_map/radial_apply/pallas_call | solution.py:181
  63.7 5.8 %all-to-all-start.1 = ((f32[512,16,128]{2,1,0:T(8,128)}), f32[512,16,128]{2,1,0:T(8,128)}, u32[]{:S(2)}, u32[]{:S(2)}) async-start(f32[512,16,128]{2,1,0:T(8,128)} %bitcast.43), calls=%async_computation.1 | async-start | bytes 8388608 | tf_op jit(solution)/shard_map/all_to_all | solution.py:23
  69.5 23.8 %local_terms.3.above_ref = f32[1,6144,128]{2,1,0:T(8,128)} custom-call(s32[2]{0:T(128)} %sizes.7, f32[2,384]{1,0:T(2,128)} %centrifugal.3, f32[2,6144,128]{2,1,0:T(8,128)} %bitcast.38, f32[2,6144,128]{2,1,0:T(8,128)} %bitcast.42, f32[8192,128]{1,0:T(8,128)} %bitcast.45, f32[2,512,384]{2,1,0:T(8,128)} %legendre_ref.3, ...), custom_call_target="tpu_custom_call" | custom-call | flops 1 | bytes 1 | tf_op jit(solution)/shard_map/local_terms/pallas_call | solution.py:140
  93.3 0.0 collective-permute-done.2
  93.3 0.0 collective-permute-done.3
  93.3 0.0 copy-start.8
  93.3 0.0 collective-permute-done.4
  93.4 0.0 copy-start.9
  93.4 0.0 copy-done.6
  93.5 0.1 pad_maximum_fusion
  93.6 0.2 collective-permute-start.5
  93.8 0.6 pad_add_fusion.where_ref.where
  94.4 0.0 collective-permute-done
  94.4 0.0 collective-permute-done.1
  94.4 1.9 %collective-permute-done.5.refs_4_ = f32[4,32,16,128]{3,2,1,0:T(8,128)S(1)} collective-permute-done((f32[4,32,16,128]{3,2,1,0:T(8,128)S(1)}, f32[4,32,16,128]{3,2,1,0:T(8,128)S(1)}, u32[]{:S(2)}, u32[]{:S(2)}) %collective-permute-start.5) | collective-permute-done | bytes 1048608 | tf_op jit(solution)/shard_map/ppermute | solution.py:394
  96.3 0.0 copy-done.7
  96.3 0.0 copy-done.8
  96.3 0.0 copy-done.9
  96.3 0.0 copy-start.10
  96.3 1.0 copy-done.10
  97.3 5.4 %radial_apart.1 = (f32[32,16,128]{2,1,0:T(8,128)}, f32[32,16,128]{2,1,0:T(8,128)}, f32[32,16,128]{2,1,0:T(8,128)}, f32[32,16,128]{2,1,0:T(8,128)}, f32[4,32,16,128]{3,2,1,0:T(8,128)}) custom-call(s32[2]{0:T(128)} %pad_add_fusion.where_ref.where, bf16[256,256]{1,0:T(8,128)(2,1)} %maximum_maximum_fusion.1.matrix_ref, f32[2,32,16,128]{3,2,1,0:T(8,128)} %bitcast.47, ...), custom_call_target="tpu_custom_call" | custom-call | flops 1 | bytes 1 | tf_op jit(solution)/shard_map/radial_apart/pallas_call | solution.py:234
  102.7 0.2 collective-permute-start.6
  102.9 2.7 %collective-permute-done.6 = f32[4,32,16,128]{3,2,1,0:T(8,128)S(1)} collective-permute-done((f32[4,32,16,128]{3,2,1,0:T(8,128)}, f32[4,32,16,128]{3,2,1,0:T(8,128)S(1)}, u32[]{:S(2)}, u32[]{:S(2)}) %collective-permute-start.6) | collective-permute-done | bytes 1048608 | tf_op jit(solution)/shard_map/ppermute | solution.py:394
  105.6 0.1 slice_bitcast_fusion
  105.7 1.0 pad_maximum_fusion.4
  106.8 1.5 collective-permute-start.7
  108.3 1.8 %collective-permute-start.9 = (f32[64,16,128]{2,1,0:T(8,128)S(1)}, f32[64,16,128]{2,1,0:T(8,128)S(1)}, u32[]{:S(2)}, u32[]{:S(2)}) collective-permute-start(f32[64,16,128]{2,1,0:T(8,128)S(1)} %pad_maximum_fusion.4), channel_id=1, source_target_pairs={{0,6},{1,7},{2,4},{3,5},{4,2},{5,3},{6,0},{7,1},{8,14},{9,15},{10,... | collective-permute-start | bytes 1572872 | tf_op jit(solution)/shard_map/ppermute | solution.py:394
  110.1 0.6 collective-permute-start.8
  110.7 0.7 constant_dynamic-slice_fusion.10
  111.4 0.7 constant_dynamic-slice_fusion.9
  112.1 0.6 pad_maximum_fusion.5.coriolis
  112.7 1.8 %pad_maximum_fusion.1 = f32[64,16,128]{2,1,0:T(8,128)} fusion(f32[32,16,128]{2,1,0:T(8,128)S(1)} %get-tuple-element.50, f32[32,16,128]{2,1,0:T(8,128)} %get-tuple-element.32), kind=kLoop, calls=%fused_computation.3 | loop fusion | flops 131072 | bytes 1048576 | tf_op jit(solution)/shard_map/concatenate | solution.py:468
  114.5 11.2 %all-to-all-done.1 = f32[512,16,128]{2,1,0:T(8,128)} async-done(((f32[512,16,128]{2,1,0:T(8,128)}), f32[512,16,128]{2,1,0:T(8,128)}, u32[]{:S(2)}, u32[]{:S(2)}) %all-to-all-start.1) | async-done | bytes 4194336 | tf_op jit(solution)/shard_map/all_to_all | solution.py:23
  125.7 14.9 %middle_terms.1 = f32[2,6144,128]{2,1,0:T(8,128)} custom-call(s32[2]{0:T(128)} %sizes.7, f32[3,384]{1,0:T(4,128)} %pad_maximum_fusion.5.coriolis, s32[2]{0:T(128)} %pad_add_fusion.where_ref.where, f32[1,6144,128]{2,1,0:T(8,128)} %local_terms.2.below_ref, f32[1,6144,128]{2,1,0:T(8,128)} %local_terms.3.above_ref, f32[2,6144,128]{2,1,0:T(8,128)} %bitcast.39, ...), custom_call_target="tpu_custom_call" | custom-call | flops 1 | bytes 1 | tf_op jit(solution)/shard_map/middle_terms/pallas_call | solution.py:315
  140.5 0.0 collective-permute-done.7
  140.5 0.0 collective-permute-done.9
  140.5 7.5 %collective-permute-done.8 = f32[64,16,128]{2,1,0:T(8,128)S(1)} collective-permute-done((f32[64,16,128]{2,1,0:T(8,128)S(1)}, f32[64,16,128]{2,1,0:T(8,128)S(1)}, u32[]{:S(2)}, u32[]{:S(2)}) %collective-permute-start.8) | collective-permute-done | bytes 524320 | tf_op jit(solution)/shard_map/ppermute | solution.py:394
  148.0 0.0 copy-done.4
  148.0 0.0 copy-start.1
  148.1 2.8 %add_apart.1 = f32[12288,128]{1,0:T(8,128)} custom-call(s32[2]{0:T(128)S(1)} %copy-done.5, s32[2]{0:T(128)S(1)} %copy-done.4, f32[12288,128]{1,0:T(8,128)} %bitcast.40, f32[16,128]{1,0:T(8,128)S(1)} %copy-done.2, f32[1024,128]{1,0:T(8,128)S(1)} %bitcast.32, f32[1024,128]{1,0:T(8,128)S(1)} %bitcast.34, ...), custom_call_target="tpu_custom_call", output_to_operand_aliasing={{}: (2, {})} | custom-call | flops 1 | bytes 1 | tf_op jit(solution)/shard_map/add_apart/pallas_call | solution.py:375
  (22 shorter events, 0.2 us)
Async XLA Ops:
  0.0 27.5 %copy-start = (f32[128,128]{1,0:T(8,128)S(1)}, f32[128,128]{1,0:T(8,128)}, u32[]{:S(2)}) copy-start(f32[128,128]{1,0:T(8,128)} %param.16) | copy-start | bytes 196612
  3.3 54.8 %all-to-all-start = ((f32[512,16,128]{2,1,0:T(8,128)}), f32[512,16,128]{2,1,0:T(8,128)}, u32[]{:S(2)}, u32[]{:S(2)}) async-start(f32[512,16,128]{2,1,0:T(8,128)} %leading.1), calls=%async_computation | async-start | bytes 8388608 | tf_op jit(solution)/shard_map/all_to_all | solution.py:23
  9.2 2.5 %copy-start.3 = (s32[2]{0:T(128)S(1)}, s32[2]{0:T(128)}, u32[]{:S(2)}) copy-start(s32[2]{0:T(128)} %sizes.7) | copy-start | bytes 28
  11.7 81.6 %copy-start.6 = (f32[64,16,128]{2,1,0:T(8,128)}, f32[64,16,128]{2,1,0:T(8,128)S(1)}, u32[]{:S(2)}) copy-start(f32[64,16,128]{2,1,0:T(8,128)S(1)} %get-tuple-element.28) | copy-start | bytes 1572868
  11.8 15.6 %copy-start.13 = (f32[128,128]{1,0:T(8,128)S(1)}, f32[128,128]{1,0:T(8,128)}, u32[]{:S(2)}) copy-start(f32[128,128]{1,0:T(8,128)} %param.19) | copy-start | bytes 196612
  11.8 16.9 %copy-start.15 = (f32[16]{0:T(128)S(1)}, f32[16]{0:T(128)}, u32[]{:S(2)}) copy-start(f32[16]{0:T(128)} %param.17) | copy-start | bytes 196
  17.2 77.2 %collective-permute-start = (f32[1,384,16,128]{3,2,1,0:T(8,128)}, f32[1,384,16,128]{3,2,1,0:T(8,128)}, u32[]{:S(2)}, u32[]{:S(2)}) collective-permute-start(f32[1,384,16,128]{3,2,1,0:T(8,128)} %get-tuple-element.41), channel_id=1, source_target_pairs={{0,8},{8,16},{16,24},{24,32},{32,40},{40,48},{48,56},{56,64},{64,7... | collective-permute-start | bytes 9437192 | tf_op jit(solution)/shard_map/ppermute | solution.py:19
  22.1 72.3 %collective-permute-start.1 = (f32[1,384,16,128]{3,2,1,0:T(8,128)}, f32[1,384,16,128]{3,2,1,0:T(8,128)}, u32[]{:S(2)}, u32[]{:S(2)}) collective-permute-start(f32[1,384,16,128]{3,2,1,0:T(8,128)} %get-tuple-element.42), channel_id=1, source_target_pairs={{8,0},{16,8},{24,16},{32,24},{40,32},{48,40},{56,48},{64,56},{72,6... | collective-permute-start | bytes 9437192 | tf_op jit(solution)/shard_map/ppermute | solution.py:19
  23.4 69.9 %collective-permute-start.2 = (f32[64,16,128]{2,1,0:T(8,128)}, f32[64,16,128]{2,1,0:T(8,128)S(1)}, u32[]{:S(2)}, u32[]{:S(2)}) collective-permute-start(f32[64,16,128]{2,1,0:T(8,128)} %get-tuple-element.44), channel_id=1, source_target_pairs={{0,2},{1,3},{2,0},{3,1},{4,6},{5,7},{6,4},{7,5},{8,10},{9,11},{10,... | collective-permute-start | bytes 1572872 | tf_op jit(solution)/shard_map/ppermute | solution.py:394
  24.9 68.4 %collective-permute-start.3 = (f32[64,16,128]{2,1,0:T(8,128)S(1)}, f32[64,16,128]{2,1,0:T(8,128)S(1)}, u32[]{:S(2)}, u32[]{:S(2)}) collective-permute-start(f32[64,16,128]{2,1,0:T(8,128)S(1)} %get-tuple-element.45), channel_id=1, source_target_pairs={{0,4},{1,5},{2,6},{3,7},{4,0},{5,1},{6,2},{7,3},{8,12},{9,13},{10,... | collective-permute-start | bytes 1572872 | tf_op jit(solution)/shard_map/ppermute | solution.py:394
  27.3 66.0 %collective-permute-start.4 = (f32[64,16,128]{2,1,0:T(8,128)S(1)}, f32[64,16,128]{2,1,0:T(8,128)S(1)}, u32[]{:S(2)}, u32[]{:S(2)}) collective-permute-start(f32[64,16,128]{2,1,0:T(8,128)S(1)} %get-tuple-element.46), channel_id=1, source_target_pairs={{0,6},{1,7},{2,4},{3,5},{4,2},{5,3},{6,0},{7,1},{8,14},{9,15},{10,... | collective-permute-start | bytes 1572872 | tf_op jit(solution)/shard_map/ppermute | solution.py:394
  29.4 23.9 %copy-start.14 = (f32[128,128]{1,0:T(8,128)S(1)}, f32[128,128]{1,0:T(8,128)}, u32[]{:S(2)}) copy-start(f32[128,128]{1,0:T(8,128)} %param.18) | copy-start | bytes 196612
  63.7 62.0 %all-to-all-start.1 = ((f32[512,16,128]{2,1,0:T(8,128)}), f32[512,16,128]{2,1,0:T(8,128)}, u32[]{:S(2)}, u32[]{:S(2)}) async-start(f32[512,16,128]{2,1,0:T(8,128)} %bitcast.43), calls=%async_computation.1 | async-start | bytes 8388608 | tf_op jit(solution)/shard_map/all_to_all | solution.py:23
  93.3 3.0 %copy-start.7 = (f32[64,16,128]{2,1,0:T(8,128)}, f32[64,16,128]{2,1,0:T(8,128)S(1)}, u32[]{:S(2)}) copy-start(f32[64,16,128]{2,1,0:T(8,128)S(1)} %collective-permute-done.2) | copy-start | bytes 1572868
  93.3 3.0 %copy-start.8 = (f32[64,16,128]{2,1,0:T(8,128)}, f32[64,16,128]{2,1,0:T(8,128)S(1)}, u32[]{:S(2)}) copy-start(f32[64,16,128]{2,1,0:T(8,128)S(1)} %collective-permute-done.3) | copy-start | bytes 1572868
  93.4 3.0 %copy-start.9 = (f32[64,16,128]{2,1,0:T(8,128)}, f32[64,16,128]{2,1,0:T(8,128)S(1)}, u32[]{:S(2)}) copy-start(f32[64,16,128]{2,1,0:T(8,128)S(1)} %collective-permute-done.4) | copy-start | bytes 1572868
  93.6 2.7 %collective-permute-start.5 = (f32[4,32,16,128]{3,2,1,0:T(8,128)S(1)}, f32[4,32,16,128]{3,2,1,0:T(8,128)S(1)}, u32[]{:S(2)}, u32[]{:S(2)}) collective-permute-start(f32[4,32,16,128]{3,2,1,0:T(8,128)S(1)} %pad_maximum_fusion), channel_id=1, source_target_pairs={{0,1},{1,0},{2,3},{3,2},{4,5},{5,4},{6,7},{7,6},{8,9},{9,8},{10,11... | collective-permute-start | bytes 3145736 | tf_op jit(solution)/shard_map/ppermute | solution.py:394
  96.3 1.0 copy-start.10
  102.7 4.0 %copy-start.12 = (f32[32,16,128]{2,1,0:T(8,128)S(1)}, f32[32,16,128]{2,1,0:T(8,128)}, u32[]{:S(2)}) copy-start(f32[32,16,128]{2,1,0:T(8,128)} %get-tuple-element.35) | copy-start | bytes 786436
  102.7 4.1 %copy-start.11 = (f32[32,16,128]{2,1,0:T(8,128)S(1)}, f32[32,16,128]{2,1,0:T(8,128)}, u32[]{:S(2)}) copy-start(f32[32,16,128]{2,1,0:T(8,128)} %get-tuple-element.34) | copy-start | bytes 786436
  102.7 3.0 %collective-permute-start.6 = (f32[4,32,16,128]{3,2,1,0:T(8,128)}, f32[4,32,16,128]{3,2,1,0:T(8,128)S(1)}, u32[]{:S(2)}, u32[]{:S(2)}) collective-permute-start(f32[4,32,16,128]{3,2,1,0:T(8,128)} %get-tuple-element.33), channel_id=1, source_target_pairs={{0,1},{1,0},{2,3},{3,2},{4,5},{5,4},{6,7},{7,6},{8,9},{9,8},{10,11... | collective-permute-start | bytes 3145736 | tf_op jit(solution)/shard_map/ppermute | solution.py:394
  106.8 33.7 %collective-permute-start.7 = (f32[64,16,128]{2,1,0:T(8,128)S(1)}, f32[64,16,128]{2,1,0:T(8,128)S(1)}, u32[]{:S(2)}, u32[]{:S(2)}) collective-permute-start(f32[64,16,128]{2,1,0:T(8,128)S(1)} %pad_maximum_fusion.2), channel_id=1, source_target_pairs={{0,2},{1,3},{2,0},{3,1},{4,6},{5,7},{6,4},{7,5},{8,10},{9,11},{10,... | collective-permute-start | bytes 1572872 | tf_op jit(solution)/shard_map/ppermute | solution.py:394
  108.3 32.2 %collective-permute-start.9 = (f32[64,16,128]{2,1,0:T(8,128)S(1)}, f32[64,16,128]{2,1,0:T(8,128)S(1)}, u32[]{:S(2)}, u32[]{:S(2)}) collective-permute-start(f32[64,16,128]{2,1,0:T(8,128)S(1)} %pad_maximum_fusion.4), channel_id=1, source_target_pairs={{0,6},{1,7},{2,4},{3,5},{4,2},{5,3},{6,0},{7,1},{8,14},{9,15},{10,... | collective-permute-start | bytes 1572872 | tf_op jit(solution)/shard_map/ppermute | solution.py:394
  110.1 37.9 %collective-permute-start.8 = (f32[64,16,128]{2,1,0:T(8,128)S(1)}, f32[64,16,128]{2,1,0:T(8,128)S(1)}, u32[]{:S(2)}, u32[]{:S(2)}) collective-permute-start(f32[64,16,128]{2,1,0:T(8,128)S(1)} %pad_maximum_fusion.3), channel_id=1, source_target_pairs={{0,4},{1,5},{2,6},{3,7},{4,0},{5,1},{6,2},{7,3},{8,12},{9,13},{10,... | collective-permute-start | bytes 1572872 | tf_op jit(solution)/shard_map/ppermute | solution.py:394
  125.7 22.4 %copy-start.2 = (f32[16,128]{1,0:T(8,128)S(1)}, f32[16,128]{1,0:T(8,128)}, u32[]{:S(2)}) copy-start(f32[16,128]{1,0:T(8,128)} %broadcast_in_dim.2.factor_ref) | copy-start | bytes 24580
  125.7 22.4 %copy-start.4 = (s32[2]{0:T(128)S(1)}, s32[2]{0:T(128)}, u32[]{:S(2)}) copy-start(s32[2]{0:T(128)} %sizes.7) | copy-start | bytes 28
  125.7 22.4 %copy-start.5 = (s32[2]{0:T(128)S(1)}, s32[2]{0:T(128)}, u32[]{:S(2)}) copy-start(s32[2]{0:T(128)} %pad_add_fusion.where_ref.where) | copy-start | bytes 28
  148.0 2.8 %copy-start.1 = (f32[128,128]{1,0:T(8,128)S(1)}, f32[128,128]{1,0:T(8,128)}, u32[]{:S(2)}) copy-start(f32[128,128]{1,0:T(8,128)} %param.16) | copy-start | bytes 196612
